TPU v7x, 32 devices: a whole 2x2x4 slice. The times are simulated.
32 devices in a mesh: lat: 4 (over x, core), lon: 8 (over z, y).
Axes of the slice: x: 2, y: 2, z: 4, core: 2. Of those that a mesh axis runs over, the one named last changes fastest.
Arguments:
- spectra: bfloat16 [98304, 616], P(('lat', 'lon')), may hold values from -6 to 6
- block_target: int32 [768], P(('lat', 'lon')), may hold values from 0 to 7, as said below
- block_patch: int32 [768], P(('lat', 'lon')), may hold values from 0 to 11
- block_kernel: int32 [768], P(('lat', 'lon')), may hold values from 0 to 15
- encoder_weight: bfloat16 [616, 512], replicated, may hold values from -0.25 to 0.25
- kernels: bfloat16 [16, 128, 128], replicated, may hold values from 0.049804688 to 1
- gain: float32 [512], replicated, may hold values from 0.1 to 1.9
- conv_weight: bfloat16 [3, 3, 512, 512], replicated, may hold values from -0.09375 to 0.09375
- cotangent: bfloat16 [96, 512, 512], P('lat', 'lon'), may hold values from -6 to 6
Outputs:
- conv_out: bfloat16 [96, 512, 512], P('lat', 'lon')
- conv_grad: float32 [3, 3, 512, 512], replicated
- encoder_grad: float32 [616, 512], replicated
- gain_grad: float32 [512], replicated
Inputs may be any that keep to these rules, and one draw needn't show every extreme that they name: `block_target`: within one device's 24 blocks no tile is named more than 3 times; in every latitude band one tile is named exactly 3 times by every device of the band.
All inputs are finite; a program needn't handle non-finite values.
Results may differ from a plain program's by a relative error of at most 0.0059.
Values may be sent and summed in bfloat16 or wider, within the bound.
No kernel may reach another device: no remote copies, remote signals or barrier semaphores. Data moves between devices by JAX's collectives and lax.ppermute only.
A program may use at most 192 MiB of HBM per device.

v0:
```python
import math

import jax
import jax.numpy as jnp
from jax import lax
from jax.experimental import pallas as pl
from jax.experimental.pallas import tpu as pltpu
from jax.sharding import PartitionSpec as P


PH = 8
PW = 16
MOST = 3
EPS = 1e-06
LANES = 128
AXES = ("lat", "lon")
VMEM_LIMIT = 56 * 1024 * 1024


def bits_of(count):
    assert count & (count - 1) == 0
    return [1 << i for i in range(count.bit_length() - 1)]


def parity(value, mask):
    out = jnp.zeros((), jnp.int32)
    while mask:
        low = mask & -mask
        out = out ^ ((value & low) != 0).astype(jnp.int32)
        mask ^= low
    return out


def exchange(value, lats, lons, move):
    pairs = []
    for a in range(lats):
        for b in range(lons):
            c, d = move(a, b)
            pairs.append((a * lons + b, c * lons + d))
    return lax.ppermute(value, AXES, pairs)


def stage_plan(lats, lons):
    lat_bits, lon_bits = bits_of(lats), bits_of(lons)
    first = lat_bits[:1]
    lat_rest = lat_bits[1:]
    low, high = lon_bits[:1], lon_bits[1:]
    plan = [(((m, 0), (m, 0)), ((m, 0), (m, 0))) for m in first]
    ab = [(m, 0) for m in lat_rest] + [(0, m) for m in low]
    ba = [(0, m) for m in low] + [(m, 0) for m in lat_rest]
    plan += [((p, q), (p, q)) for p, q in zip(ab, ba)]
    if len(high) == 2:
        one, two = high
        plan += [(((0, one),) * 2, ((0, one | two),) * 2), (((0, one | two),) * 2, ((0, two),) * 2)]
    else:
        plan += [(((0, m),) * 2, ((0, m),) * 2) for m in high]
    return plan


def kept_half(masks, lat, lon):
    even = parity(lat, masks[0][0]) ^ parity(lon, masks[0][1])
    odd = parity(lat, masks[1][0]) ^ parity(lon, masks[1][1])
    return jnp.where((lat & 1) == 0, even, odd)


def step(value, steps, lats, lons):
    return exchange(value, lats, lons, lambda a, b: (a ^ steps[a & 1][0], b ^ steps[a & 1][1]))


def pick(value, half):
    pair = value.reshape(2, value.shape[0] // 2, value.shape[1])
    return lax.dynamic_index_in_dim(pair, half, 0, keepdims=False)


def split_sum(keep, came, half):
    away = pick(keep, 1 - half) + pick(came, 1 - half).astype(jnp.float32)
    stay = pick(keep, half) + pick(came, half).astype(jnp.float32)
    return away.astype(jnp.bfloat16), stay


def padded_2(shard, sides, width, wrap):
    for axis, dim in sides:
        size, length = (lax.axis_size(axis), shard.shape[dim])
        up = [(i, (i + 1) % size) for i in range(size if wrap else size - 1)]
        down = [(j, i) for i, j in up]
        last = lax.slice_in_dim(shard, length - width, length, axis=dim)
        leading = lax.slice_in_dim(shard, 0, width, axis=dim)
        before = lax.ppermute(last, axis, up)
        after = lax.ppermute(leading, axis, down)
        shard = jnp.concatenate([before, shard, after], axis=dim)
    return shard


def widen(field):
    beside_all = padded_2(field, (("lon", 1),), 1, True)
    return padded_2(beside_all, (("lat", 0),), 1, False)


def to_patches(tile):
    rows, cols, width = tile.shape
    shaped = tile.reshape(rows // PH, PH, cols // PW, PW, width)
    return shaped.transpose(0, 2, 1, 3, 4).reshape(-1, width)


def whole(shape):
    zeros = (0,) * len(shape)
    return pl.BlockSpec(shape, lambda *_: zeros)


def call(body, scalars, ins, outs, grid=(1,), in_specs=None, out_specs=None, scratch=(), alias=None):
    return pl.pallas_call(
        body,
        out_shape=outs,
        grid_spec=pltpu.PrefetchScalarGridSpec(
            num_scalar_prefetch=1,
            grid=grid,
            in_specs=in_specs or [whole(a.shape) for a in ins],
            out_specs=out_specs or [whole(o.shape) for o in outs],
            scratch_shapes=list(scratch),
        ),
        input_output_aliases=alias or {},
        compiler_params=pltpu.CompilerParams(vmem_limit_bytes=VMEM_LIMIT),
    )(scalars, *ins)


def shape_of(shape, dtype):
    return jax.ShapeDtypeStruct(shape, dtype)


def nt(left, right):
    return lax.dot_general(left, right, (((1,), (1,)), ((), ())), preferred_element_type=jnp.float32)


def lanes(at, size):
    return pl.ds(pl.multiple_of(at * size, size), size)


def pack(spectra_t, source, places, rows):
    channels = spectra_t.shape[0]

    def body(src, full, *refs):
        outs, sems = refs[:-1], refs[-1]
        copies = []
        for n, k in enumerate(places):
            for j in range(MOST):
                copies.append(
                    pltpu.make_async_copy(
                        full.at[:, lanes(src[k * MOST + j], rows)],
                        outs[n].at[:, j * rows : (j + 1) * rows],
                        sems.at[n * MOST + j],
                    )
                )
        for c in copies:
            c.start()
        for c in copies:
            c.wait()

    outs = [shape_of((channels, MOST * rows), spectra_t.dtype)] * len(places)
    return call(
        body,
        source,
        [spectra_t],
        outs,
        in_specs=[pl.BlockSpec(memory_space=pl.ANY)],
        scratch=[pltpu.SemaphoreType.DMA((len(places) * MOST,))],
    )


def spread_blocks(meta, first, arrived, weight_t, kernels, gain_col, before, patches, last):
    count = len(arrived)
    kernel_count, rows, cells = kernels.shape
    width = weight_t.shape[0]

    def body(meta_ref, *refs):
        xs = refs[:count]
        w, kern, g = refs[count : count + 3]
        spread, slope, *rest = refs[count + 3 + (before is not None) :]
        if before is None:
            spread[...] = jnp.zeros_like(spread)
        else:
            spread[...] = refs[count + 3][...]
        for k in range(count):
            pre = jnp.dot(w[...], xs[k][...], preferred_element_type=jnp.float32)
            s = jax.nn.sigmoid(pre)
            slope[k] = (s * (1.0 + pre * (1.0 - s))).astype(jnp.bfloat16)
            enc = (pre * s).astype(jnp.bfloat16)
            for j in range(MOST):
                code = meta_ref[(first + k) * MOST + j]

                @pl.when(code >= 0)
                def _():
                    spread[code // kernel_count] += jnp.dot(
                        enc[:, j * rows : (j + 1) * rows],
                        kern[code % kernel_count],
                        preferred_element_type=jnp.float32,
                    )

        if last:
            for q in range(patches):
                cell = spread[q]
                r = lax.rsqrt(jnp.mean(cell * cell, axis=0, keepdims=True) + EPS)
                rest[0][:, q * cells : (q + 1) * cells] = (cell * r * g[...]).astype(jnp.bfloat16)

    outs = [
        shape_of((patches, width, cells), jnp.float32),
        shape_of((count, width, MOST * rows), jnp.bfloat16),
    ]
    if last:
        outs.append(shape_of((width, patches * cells), jnp.bfloat16))
    ins = [*arrived, weight_t, kernels, gain_col] + ([] if before is None else [before])
    return call(body, meta, ins, outs)


def backward(meta, arrived, kernels_t, gain_col, spread, slopes, d_normed_t):
    count = len(arrived)
    groups = len(slopes)
    place_of = [(n, k) for n, one in enumerate(slopes) for k in range(one.shape[0])]
    kernel_count, cells, rows = kernels_t.shape
    patches, width, _ = spread.shape
    channels = arrived[0].shape[0]

    def body(meta_ref, *refs):
        xs = refs[:count]
        slos = refs[count : count + groups]
        kern, g, spr, dn, out, dsp, dpre = refs[count + groups :]
        total = jnp.zeros((width, 1), jnp.float32)
        for q in range(patches):
            cell = spr[q]
            d = dn[:, q * cells : (q + 1) * cells]
            r = lax.rsqrt(jnp.mean(cell * cell, axis=0, keepdims=True) + EPS)
            unit = cell * r
            total = total + jnp.sum(d * unit, axis=1, keepdims=True)
            dg = d * g[...]
            inner = jnp.mean(dg * unit, axis=0, keepdims=True)
            dsp[q] = ((dg - unit * inner) * r).astype(jnp.bfloat16)
        out[...] = jnp.zeros_like(out)
        out[:, channels : channels + 1] = total
        for k in range(count):
            for j in range(MOST):
                code = meta_ref[k * MOST + j]
                span = slice(j * rows, (j + 1) * rows)

                @pl.when(code >= 0)
                def _():
                    drow = jnp.dot(
                        dsp[code // kernel_count],
                        kern[code % kernel_count],
                        preferred_element_type=jnp.float32,
                    ).astype(jnp.bfloat16)
                    dpre[:, span] = (
                        drow.astype(jnp.float32) * slos[place_of[k][0]][place_of[k][1], :, span].astype(jnp.float32)
                    ).astype(jnp.bfloat16)

                @pl.when(code < 0)
                def _():
                    dpre[:, span] = jnp.zeros((width, rows), jnp.bfloat16)

            out[:, :channels] += nt(dpre[...], xs[k][...])

    ins = [*arrived, *slopes, kernels_t, gain_col, spread, d_normed_t]
    outs = [shape_of((width, (channels // LANES + 1) * LANES), jnp.float32)]
    scratch = [
        pltpu.VMEM((patches, width, cells), jnp.bfloat16),
        pltpu.VMEM((width, MOST * rows), jnp.bfloat16),
    ]
    return call(body, meta, ins, outs, scratch=scratch)[0]


def place(half, part, taps, lane, scale, into=None):
    rows = part.shape[0]
    steps = 8
    unit = rows // steps

    def body(half_ref, piece, *refs):
        for t in range(taps):
            refs[-1][t] = piece[:, t * lane : (t + 1) * lane].astype(jnp.float32) * scale

    specs = [pl.BlockSpec((unit, part.shape[1]), lambda i, h: (i, 0))]
    ins = [part]
    if into is not None:
        ins.append(into)
        specs.append(pl.BlockSpec(memory_space=pl.ANY))
    return call(
        body,
        half.reshape(1),
        ins,
        [shape_of((taps, 2 * rows, lane), jnp.float32)],
        grid=(steps,),
        in_specs=specs,
        out_specs=[pl.BlockSpec((taps, unit, lane), lambda i, h: (0, h[0] * steps + i, 0))],
        alias=None if into is None else {2: 0},
    )[0]


def shards(
    spectra,
    block_target,
    block_patch,
    block_kernel,
    encoder_weight,
    kernels,
    gain,
    conv_weight,
    cotangent,
):
    lons = lax.axis_size("lon")
    lats = lax.axis_size("lat")
    lon = lax.axis_index("lon")
    blocks = block_target.shape[0]
    kernel_count, block_rows, _ = kernels.shape
    channels = spectra.shape[1]
    width = encoder_weight.shape[1]
    tile_rows, tile_cols = (cotangent.shape[0], cotangent.shape[1])
    loss_scale = 1.0 / math.sqrt(tile_rows * lats * tile_cols * lons)
    cells = tile_rows * tile_cols

    cot_beside = padded_2(cotangent, (("lon", 1),), 1, True)
    order = lon ^ jnp.arange(lons, dtype=jnp.int32)
    hit = (block_target[:, None] == order[None, :]).astype(jnp.int32)
    rank = jnp.cumsum(hit, axis=0) - hit
    chosen = hit[:, :, None] * (rank[:, :, None] == jnp.arange(MOST)[None, None, :]).astype(jnp.int32)
    number = jnp.arange(blocks, dtype=jnp.int32)
    source = jnp.sum(chosen * number[:, None, None], axis=0).reshape(-1)
    code = block_patch * kernel_count + block_kernel + 1
    codes = jnp.sum(chosen * code[:, None, None], axis=0) - 1
    spectra_t = spectra.T
    far, near = range(lons // 2, lons), range(lons // 2)
    packed = dict(zip(far, pack(spectra_t, source, far, block_rows)))
    packed |= zip(near, pack(spectra_t, source, near, block_rows))
    cot_padded = padded_2(cot_beside, (("lat", 0),), 1, False)

    by_tile = jnp.sum(
        jnp.where((order[None, :] == jnp.arange(lons)[:, None])[:, :, None], codes[None], 0), axis=1
    )
    came = lax.all_to_all(by_tile, "lon", 0, 0, tiled=True)
    meta = jnp.sum(
        jnp.where((order[:, None] == jnp.arange(lons)[None, :])[:, :, None], came[None], 0), axis=1
    ).reshape(-1)

    arrived = [packed[0]] + [None] * (lons - 1)
    for k in [*far, *near[1:]]:
        arrived[k] = exchange(packed[k], lats, lons, lambda a, b, k=k: (a, b ^ k))

    windows = jnp.concatenate(
        [
            to_patches(cot_padded[2 - a : 2 - a + tile_rows, 2 - b : 2 - b + tile_cols])
            for a in range(3)
            for b in range(3)
        ],
        axis=1,
    )
    taps = 9
    weight_all = conv_weight.reshape(taps, width, width).transpose(1, 0, 2).reshape(width, -1)
    d_normed_t = nt(weight_all, windows)

    meta, d_normed_t, windows = lax.optimization_barrier((meta, d_normed_t, windows))
    patches = tile_rows // PH * (tile_cols // PW)
    gain_col = gain.reshape(width, 1)
    weight_t = encoder_weight.T
    cuts = [0, lons // 2, lons - 1, lons]
    spread, slopes = None, []
    for low, high in zip(cuts, cuts[1:]):
        last = high == lons
        spread, slope, *rest = spread_blocks(
            meta, low, arrived[low:high], weight_t, kernels, gain_col, spread, patches, last
        )
        slopes.append(slope)
    normed_t = rest[0]

    plan = stage_plan(lats, lons)
    lat = lax.axis_index("lat")
    halves = [kept_half(masks, lat, lon) for _, masks in plan]
    core = halves[0]
    away = jnp.dot(
        pick(normed_t, 1 - core), windows, preferred_element_type=jnp.float32
    ).astype(jnp.bfloat16)
    keep = jnp.dot(pick(normed_t, core), windows, preferred_element_type=jnp.float32)
    came = step(away, plan[0][0], lats, lons)

    small = backward(
        meta, arrived, kernels.transpose(0, 2, 1), gain_col, spread, slopes, d_normed_t
    )
    small_keep = pick(small, core)
    small_came = step(pick(small, 1 - core).astype(jnp.bfloat16), plan[0][0], lats, lons)

    apart = len(plan) - 2
    for n in range(1, apart):
        away, keep = split_sum(keep, came, halves[n])
        came = step(away, plan[n][0], lats, lons)
        away, small_keep = split_sum(small_keep, small_came, halves[n])
        small_came = step(away, plan[n][0], lats, lons)
    wide = taps * width
    keep = jnp.concatenate([keep, small_keep], axis=1)
    came = jnp.concatenate([came, small_came], axis=1)
    for n in range(apart, len(plan)):
        away, keep = split_sum(keep, came, halves[n])
        came = step(away, plan[n][0], lats, lons)
    normed = normed_t.reshape(width, tile_rows // PH, tile_cols // PW, PH, PW)
    normed = normed.transpose(1, 3, 2, 4, 0).reshape(tile_rows, tile_cols, width)
    padded = widen(normed)
    result_sum = jnp.zeros((cells, width), jnp.float32)
    for a in range(3):
        for b in range(3):
            window = padded[a : a + tile_rows, b : b + tile_cols].reshape(-1, width)
            result_sum = result_sum + jnp.dot(
                window, conv_weight[a, b], preferred_element_type=jnp.float32
            )
    conv_out = result_sum.reshape(tile_rows, tile_cols, width).astype(jnp.bfloat16)
    part = (keep + came.astype(jnp.float32)).astype(jnp.bfloat16)
    for n in range(len(plan) - 1, 0, -1):
        if n == 1:
            part, conv_out = lax.optimization_barrier((part, conv_out))
        other = step(part, plan[n][0], lats, lons)
        part = jnp.where(
            halves[n] == 0, jnp.concatenate([part, other]), jnp.concatenate([other, part])
        )
    others = step(part, plan[0][0], lats, lons)
    conv_total = place(core, part, taps, width, loss_scale)
    conv_total = place(1 - core, others, taps, width, loss_scale, conv_total)
    mine, theirs = part[:, wide:], others[:, wide:]
    small = jnp.where(
        core == 0, jnp.concatenate([mine, theirs]), jnp.concatenate([theirs, mine])
    ).astype(jnp.float32) * loss_scale
    gain_total = small[:, channels]
    encoder_total = small[:, :channels].T

    return (conv_out, conv_total.reshape(3, 3, width, width), encoder_total, gain_total)


def solution(mesh):
    placed = (
        P(("lat", "lon"), None),
        P(("lat", "lon")),
        P(("lat", "lon")),
        P(("lat", "lon")),
        P(),
        P(),
        P(),
        P(),
        P("lat", "lon", None),
    )

    return jax.shard_map(
        shards,
        mesh=mesh,
        in_specs=placed,
        out_specs=(P("lat", "lon", None), P(), P(), P()),
        check_vma=False,
    )
```

profile of v0, /device:TPU:0, one launch (start us, length us, event | category | flops | bytes accessed | tf_op | source)
XLA Modules:
  0.0 305.2 jit_solution(15368154423828142777)
XLA Ops:
  4.1 7.3 %all-to-all-start = ((s32[8,1,3]{2,1,0:T(1,128)}), s32[8,1,3]{2,1,0:T(1,128)S(1)}, u32[]{:S(2)}, u32[]{:S(2)}) async-start(s32[8,1,3]{2,1,0:T(1,128)} %copy.76), calls=%async_computation | async-start | bytes 8192 | tf_op jit(solution)/shard_map/all_to_all | solution.py:335
  13.1 4.7 %collective-permute-start.1 = (bf16[24,1,512]{2,1,0:T(2,128)(2,1)}, bf16[24,1,512]{2,1,0:T(2,128)(2,1)}, u32[]{:S(2)}, u32[]{:S(2)}) collective-permute-start(bf16[24,1,512]{2,1,0:T(2,128)(2,1)} %get-tuple-element.95), channel_id=1, source_target_pairs={{1,0},{2,1},{3,2},{4,3},{5,4},{6,5},{7,6},{0,7},{9,8},{10,9},{11,1... | collective-permute-start | bytes 73736 | tf_op jit(solution)/shard_map/ppermute | solution.py:89
  30.7 6.6 %copy.88 = bf16[3,3,512,512]{2,3,1,0:T(8,128)(2,1)} copy(bf16[3,3,512,512]{3,2,1,0:T(8,128)(2,1)} %param.16) | data formatting | bytes 9437184 | tf_op args[7]
  75.4 12.3 %convolution_bitcast_fusion.refs_14_ = f32[512,1536]{1,0:T(8,128)} fusion(bf16[1536,4608]{1,0:T(8,128)(2,1)} %constant_dynamic-update-slice_fusion, bf16[512,4608]{0,1:T(8,128)(2,1)S(1)} %bitcast.190), kind=kOutput, calls=%fused_computation.11 | convolution fusion | flops 7247757312 | bytes 22020096 | tf_op jit(solution)/shard_map/dot_general | solution.py:131
  88.5 9.7 %shard_map.122 = (f32[12,512,128]{2,1,0:T(8,128)}, bf16[4,512,384]{2,1,0:T(8,128)(2,1)}) custom-call(s32[24]{0:T(128)} %reshape.348.meta_ref, bf16[616,384]{1,0:T(8,128)(2,1)} %get-tuple-element.29.refs_0_, bf16[616,384]{1,0:T(8,128)(2,1)} %copy-done.7, bf16[616,384]{1,0:T(8,128)(2,1)} %copy-done.8, bf16[616,384]{1,0:T(8,128)(2,1)} %copy-done.9, ...), custom_call_target="tpu_custom_call" | custom-call | tf_op jit(solution)/shard_map/pallas_call | solution.py:111
  98.3 5.0 %collective-permute-done.5.refs_0_.refs_4_ = bf16[616,384]{1,0:T(8,128)(2,1)S(1)} collective-permute-done((bf16[616,384]{1,0:T(8,128)(2,1)}, bf16[616,384]{1,0:T(8,128)(2,1)S(1)}, u32[]{:S(2)}, u32[]{:S(2)}) %collective-permute-start.5) | collective-permute-done | bytes 473120 | tf_op jit(solution)/shard_map/ppermute | solution.py:40
  103.3 9.4 %collective-permute-done.6.refs_1_.refs_5_ = bf16[616,384]{1,0:T(8,128)(2,1)S(1)} collective-permute-done((bf16[616,384]{1,0:T(8,128)(2,1)}, bf16[616,384]{1,0:T(8,128)(2,1)S(1)}, u32[]{:S(2)}, u32[]{:S(2)}) %collective-permute-start.6) | collective-permute-done | bytes 473120 | tf_op jit(solution)/shard_map/ppermute | solution.py:40
  113.6 9.2 %shard_map.123 = (f32[12,512,128]{2,1,0:T(8,128)}, bf16[3,512,384]{2,1,0:T(8,128)(2,1)}) custom-call(s32[24]{0:T(128)} %reshape.348.meta_ref, bf16[616,384]{1,0:T(8,128)(2,1)} %copy-done.10, bf16[616,384]{1,0:T(8,128)(2,1)} %copy-done.11, bf16[616,384]{1,0:T(8,128)(2,1)} %copy-done.12, bf16[512,616]{1,0:T(8,128)(2,1)} %bitcast.161, ...), custom_call_target="tpu_custom_call" | custom-call | tf_op jit(solution)/shard_map/pallas_call | solution.py:111
  123.6 6.9 %shard_map.124 = (f32[12,512,128]{2,1,0:T(8,128)}, bf16[1,512,384]{2,1,0:T(8,128)(2,1)}, bf16[512,1536]{1,0:T(8,128)(2,1)}) custom-call(s32[24]{0:T(128)} %reshape.348.meta_ref, bf16[616,384]{1,0:T(8,128)(2,1)} %copy-done.13, bf16[512,616]{1,0:T(8,128)(2,1)} %bitcast.162, bf16[16,128,128]{2,1,0:T(8,128)(2,1)} %refs_2_.1, ...), custom_call_target="tpu_custom_call" | custom-call | tf_op jit(solution)/shard_map/pallas_call | solution.py:111
  130.5 18.5 %shard_map.125 = f32[512,640]{1,0:T(8,128)} custom-call(s32[24]{0:T(128)} %reshape.348.meta_ref, bf16[616,384]{1,0:T(8,128)(2,1)} %get-tuple-element.29.refs_0_, bf16[616,384]{1,0:T(8,128)(2,1)} %copy-done.7, bf16[616,384]{1,0:T(8,128)(2,1)} %copy-done.8, bf16[616,384]{1,0:T(8,128)(2,1)} %copy-done.9, bf16[616,384]{1,0:T(8,128)(2,1)} %copy-done.10, ...), custom_call_target="tpu_custom_call" | custom-call | tf_op jit(solution)/shard_map/pallas_call | solution.py:111
  154.5 9.2 %convolution_convert_fusion = bf16[256,4608]{1,0:T(8,128)(2,1)S(1)} fusion(bf16[1536,4608]{1,0:T(8,128)(2,1)} %constant_dynamic-update-slice_fusion, bf16[2,256,1536]{2,1,0:T(8,128)(2,1)S(1)} %bitcast.194, s32[]{:T(128)S(6)} %select_n.128), kind=kOutput, calls=%fused_computation.2 | convolution fusion | flops 3625058304 | bytes 17301508 | tf_op jit(solution)/shard_map/dot_general | solution.py:374
  168.1 7.1 %fusion = f32[2,128,4608]{2,1,0:T(8,128)S(1)} fusion(bf16[2,128,1536]{2,1,0:T(8,128)(2,1)S(1)} %bitcast.205, bf16[1536,4608]{1,0:T(8,128)(2,1)} %constant_dynamic-update-slice_fusion), kind=kOutput, calls=%fused_computation | convolution fusion | flops 3623878656 | bytes 19660800 | tf_op jit(solution)/shard_map/dot_general | solution.py:377
  180.2 5.1 %collective-permute-start.12 = (bf16[128,4608]{1,0:T(8,128)(2,1)S(1)}, bf16[128,4608]{1,0:T(8,128)(2,1)S(1)}, u32[]{:S(2)}, u32[]{:S(2)}) collective-permute-start(bf16[128,4608]{1,0:T(8,128)(2,1)S(1)} %get-tuple-element.62), channel_id=1, source_target_pairs={{0,16},{1,17},{2,18},{3,19},{4,20},{5,21},{6,22},{7,23},{8,9},{9,8... | collective-permute-start | bytes 3538952 | tf_op jit(solution)/shard_map/ppermute | solution.py:40
  190.0 9.5 %collective-permute-done.12 = bf16[128,4608]{1,0:T(8,128)(2,1)S(1)} collective-permute-done((bf16[128,4608]{1,0:T(8,128)(2,1)S(1)}, bf16[128,4608]{1,0:T(8,128)(2,1)S(1)}, u32[]{:S(2)}, u32[]{:S(2)}) %collective-permute-start.12) | collective-permute-done | bytes 1179680 | tf_op jit(solution)/shard_map/ppermute | solution.py:40
  199.8 8.6 %collective-permute-start.15 = (bf16[64,4608]{1,0:T(8,128)(2,1)S(1)}, bf16[64,4608]{1,0:T(8,128)(2,1)S(1)}, u32[]{:S(2)}, u32[]{:S(2)}) collective-permute-start(bf16[64,4608]{1,0:T(8,128)(2,1)S(1)} %get-tuple-element.64), channel_id=1, source_target_pairs={{0,1},{1,0},{2,3},{3,2},{4,5},{5,4},{6,7},{7,6},{8,24},{9,25},{10,... | collective-permute-start | bytes 1769480 | tf_op jit(solution)/shard_map/ppermute | solution.py:40
  211.4 5.7 %collective-permute-done.16 = bf16[64,640]{1,0:T(8,128)(2,1)S(1)} collective-permute-done((bf16[64,640]{1,0:T(8,128)(2,1)S(1)}, bf16[64,640]{1,0:T(8,128)(2,1)S(1)}, u32[]{:S(2)}, u32[]{:S(2)}) %collective-permute-start.16) | collective-permute-done | bytes 81952 | tf_op jit(solution)/shard_map/ppermute | solution.py:40
  221.8 5.9 %collective-permute-done.17 = bf16[32,5248]{1,0:T(8,128)(2,1)S(1)} collective-permute-done((bf16[32,5248]{1,0:T(8,128)(2,1)S(1)}, bf16[32,5248]{1,0:T(8,128)(2,1)S(1)}, u32[]{:S(2)}, u32[]{:S(2)}) %collective-permute-start.17) | collective-permute-done | bytes 335904 | tf_op jit(solution)/shard_map/ppermute | solution.py:40
  238.6 3.9 %collective-permute-done.19 = bf16[16,5248]{1,0:T(8,128)(2,1)S(1)} collective-permute-done((bf16[16,5248]{1,0:T(8,128)(2,1)S(1)}, bf16[16,5248]{1,0:T(8,128)(2,1)S(1)}, u32[]{:S(2)}, u32[]{:S(2)}) %collective-permute-start.19) | collective-permute-done | bytes 167968 | tf_op jit(solution)/shard_map/ppermute | solution.py:40
  246.0 4.0 %collective-permute-done.20 = bf16[32,5248]{1,0:T(8,128)(2,1)S(1)} collective-permute-done((bf16[32,5248]{1,0:T(8,128)(2,1)S(1)}, bf16[32,5248]{1,0:T(8,128)(2,1)S(1)}, u32[]{:S(2)}, u32[]{:S(2)}) %collective-permute-start.20) | collective-permute-done | bytes 335904 | tf_op jit(solution)/shard_map/ppermute | solution.py:40
  255.0 8.1 %collective-permute-done.21 = bf16[64,5248]{1,0:T(8,128)(2,1)S(1)} collective-permute-done((bf16[64,5248]{1,0:T(8,128)(2,1)S(1)}, bf16[64,5248]{1,0:T(8,128)(2,1)S(1)}, u32[]{:S(2)}, u32[]{:S(2)}) %collective-permute-start.21) | collective-permute-done | bytes 671776 | tf_op jit(solution)/shard_map/ppermute | solution.py:40
  263.3 5.0 %collective-permute-start.26 = (bf16[128,5248]{1,0:T(8,128)(2,1)S(1)}, bf16[128,5248]{1,0:T(8,128)(2,1)}, u32[]{:S(2)}, u32[]{:S(2)}) collective-permute-start(bf16[128,5248]{1,0:T(8,128)(2,1)S(1)} %maximum_select_fusion.1), channel_id=1, source_target_pairs={{0,16},{1,17},{2,18},{3,19},{4,20},{5,21},{6,22},{7,23},{8,9},{9,8... | collective-permute-start | bytes 4030472 | tf_op jit(solution)/shard_map/ppermute | solution.py:40
  268.2 16.0 %collective-permute-done.26 = bf16[128,5248]{1,0:T(8,128)(2,1)} collective-permute-done((bf16[128,5248]{1,0:T(8,128)(2,1)S(1)}, bf16[128,5248]{1,0:T(8,128)(2,1)}, u32[]{:S(2)}, u32[]{:S(2)}) %collective-permute-start.26) | collective-permute-done | bytes 1343520 | tf_op jit(solution)/shard_map/ppermute | solution.py:40
  288.9 6.3 %shard_map.126.refs_0_ = f32[9,512,512]{2,1,0:T(8,128)} custom-call(s32[1]{0:T(128)} %bitcast.86.half_ref, bf16[256,5248]{1,0:T(8,128)(2,1)} %copy-done.1), custom_call_target="tpu_custom_call" | custom-call | tf_op jit(solution)/shard_map/pallas_call | solution.py:111
  298.7 6.3 %shard_map.127 = f32[9,512,512]{2,1,0:T(8,128)} custom-call(s32[1]{0:T(128)} %bitcast.85.half_ref, bf16[256,5248]{1,0:T(8,128)(2,1)} %collective-permute-done.27.piece, f32[9,512,512]{2,1,0:T(8,128)} %shard_map.126.refs_0_), custom_call_target="tpu_custom_call", output_to_operand_aliasing={{}: (2, {})} | custom-call | tf_op jit(solution)/shard_map/pallas_call | solution.py:111
  (172 shorter events, 113.3 us)
Async XLA Ops:
  4.1 37.4 %all-to-all-start = ((s32[8,1,3]{2,1,0:T(1,128)}), s32[8,1,3]{2,1,0:T(1,128)S(1)}, u32[]{:S(2)}, u32[]{:S(2)}) async-start(s32[8,1,3]{2,1,0:T(1,128)} %copy.76), calls=%async_computation | async-start | bytes 8192 | tf_op jit(solution)/shard_map/all_to_all | solution.py:335
  13.1 29.3 %collective-permute-start.1 = (bf16[24,1,512]{2,1,0:T(2,128)(2,1)}, bf16[24,1,512]{2,1,0:T(2,128)(2,1)}, u32[]{:S(2)}, u32[]{:S(2)}) collective-permute-start(bf16[24,1,512]{2,1,0:T(2,128)(2,1)} %get-tuple-element.95), channel_id=1, source_target_pairs={{1,0},{2,1},{3,2},{4,3},{5,4},{6,5},{7,6},{0,7},{9,8},{10,9},{11,1... | collective-permute-start | bytes 73736 | tf_op jit(solution)/shard_map/ppermute | solution.py:89
  17.8 24.6 %collective-permute-start = (bf16[24,1,512]{2,1,0:T(2,128)(2,1)}, bf16[24,1,512]{2,1,0:T(2,128)(2,1)}, u32[]{:S(2)}, u32[]{:S(2)}) collective-permute-start(bf16[24,1,512]{2,1,0:T(2,128)(2,1)} %get-tuple-element.94), channel_id=1, source_target_pairs={{0,1},{1,2},{2,3},{3,4},{4,5},{5,6},{6,7},{7,0},{8,9},{9,10},{10,1... | collective-permute-start | bytes 73736 | tf_op jit(solution)/shard_map/ppermute | solution.py:88
  22.1 49.2 %collective-permute-start.8 = (bf16[616,384]{1,0:T(8,128)(2,1)}, bf16[616,384]{1,0:T(8,128)(2,1)S(1)}, u32[]{:S(2)}, u32[]{:S(2)}) collective-permute-start(bf16[616,384]{1,0:T(8,128)(2,1)} %get-tuple-element.30), channel_id=1, source_target_pairs={{0,1},{1,0},{2,3},{3,2},{4,5},{5,4},{6,7},{7,6},{8,9},{9,8},{10,11... | collective-permute-start | bytes 1419272 | tf_op jit(solution)/shard_map/ppermute | solution.py:40
  22.4 52.5 %collective-permute-start.9 = (bf16[616,384]{1,0:T(8,128)(2,1)}, bf16[616,384]{1,0:T(8,128)(2,1)S(1)}, u32[]{:S(2)}, u32[]{:S(2)}) collective-permute-start(bf16[616,384]{1,0:T(8,128)(2,1)} %get-tuple-element.31), channel_id=1, source_target_pairs={{0,2},{1,3},{2,0},{3,1},{4,6},{5,7},{6,4},{7,5},{8,10},{9,11},{10,... | collective-permute-start | bytes 1419272 | tf_op jit(solution)/shard_map/ppermute | solution.py:40
  23.9 63.9 %collective-permute-start.10 = (bf16[616,384]{1,0:T(8,128)(2,1)}, bf16[616,384]{1,0:T(8,128)(2,1)S(1)}, u32[]{:S(2)}, u32[]{:S(2)}) collective-permute-start(bf16[616,384]{1,0:T(8,128)(2,1)} %get-tuple-element.32), channel_id=1, source_target_pairs={{0,3},{1,2},{2,1},{3,0},{4,7},{5,6},{6,5},{7,4},{8,11},{9,10},{10,... | collective-permute-start | bytes 1419272 | tf_op jit(solution)/shard_map/ppermute | solution.py:40
  48.4 54.9 %collective-permute-start.5 = (bf16[616,384]{1,0:T(8,128)(2,1)}, bf16[616,384]{1,0:T(8,128)(2,1)S(1)}, u32[]{:S(2)}, u32[]{:S(2)}) collective-permute-start(bf16[616,384]{1,0:T(8,128)(2,1)} %get-tuple-element.26), channel_id=1, source_target_pairs={{0,4},{1,5},{2,6},{3,7},{4,0},{5,1},{6,2},{7,3},{8,12},{9,13},{10,... | collective-permute-start | bytes 1419272 | tf_op jit(solution)/shard_map/ppermute | solution.py:40
  50.9 61.8 %collective-permute-start.6 = (bf16[616,384]{1,0:T(8,128)(2,1)}, bf16[616,384]{1,0:T(8,128)(2,1)S(1)}, u32[]{:S(2)}, u32[]{:S(2)}) collective-permute-start(bf16[616,384]{1,0:T(8,128)(2,1)} %get-tuple-element.27), channel_id=1, source_target_pairs={{0,5},{1,4},{2,7},{3,6},{4,1},{5,0},{6,3},{7,2},{8,13},{9,12},{10,... | collective-permute-start | bytes 1419272 | tf_op jit(solution)/shard_map/ppermute | solution.py:40
  71.3 41.4 %collective-permute-start.7 = (bf16[616,384]{1,0:T(8,128)(2,1)S(1)}, bf16[616,384]{1,0:T(8,128)(2,1)S(1)}, u32[]{:S(2)}, u32[]{:S(2)}) collective-permute-start(bf16[616,384]{1,0:T(8,128)(2,1)S(1)} %copy-done.16), channel_id=1, source_target_pairs={{0,6},{1,7},{2,4},{3,5},{4,2},{5,3},{6,0},{7,1},{8,14},{9,15},{10,... | collective-permute-start | bytes 1419272 | tf_op jit(solution)/shard_map/ppermute | solution.py:40
  74.9 48.0 %collective-permute-start.4 = (bf16[616,384]{1,0:T(8,128)(2,1)S(1)}, bf16[616,384]{1,0:T(8,128)(2,1)S(1)}, u32[]{:S(2)}, u32[]{:S(2)}) collective-permute-start(bf16[616,384]{1,0:T(8,128)(2,1)S(1)} %copy-done.15), channel_id=1, source_target_pairs={{0,7},{1,6},{2,5},{3,4},{4,3},{5,2},{6,1},{7,0},{8,15},{9,14},{10,... | collective-permute-start | bytes 1419272 | tf_op jit(solution)/shard_map/ppermute | solution.py:40
  150.9 38.9 %collective-permute-start.13 = (bf16[256,640]{1,0:T(8,128)(2,1)}, bf16[256,640]{1,0:T(8,128)(2,1)S(1)}, u32[]{:S(2)}, u32[]{:S(2)}) collective-permute-start(bf16[256,640]{1,0:T(8,128)(2,1)} %fusion.37), channel_id=1, source_target_pairs={{0,8},{1,9},{2,10},{3,11},{4,12},{5,13},{6,14},{7,15},{8,0},{9,1},... | collective-permute-start | bytes 983048 | tf_op jit(solution)/shard_map/ppermute | solution.py:40
  163.8 15.8 %collective-permute-start.11 = (bf16[256,4608]{1,0:T(8,128)(2,1)S(1)}, bf16[256,4608]{1,0:T(8,128)(2,1)S(1)}, u32[]{:S(2)}, u32[]{:S(2)}) collective-permute-start(bf16[256,4608]{1,0:T(8,128)(2,1)S(1)} %convolution_convert_fusion), channel_id=1, source_target_pairs={{0,8},{1,9},{2,10},{3,11},{4,12},{5,13},{6,14},{7,15},{8,0},{9,1},... | collective-permute-start | bytes 7077896 | tf_op jit(solution)/shard_map/ppermute | solution.py:40
  164.1 11.2 %collective-permute-start.23 = (bf16[24,1,512]{2,1,0:T(2,128)(2,1)S(1)}, bf16[24,1,512]{2,1,0:T(2,128)(2,1)S(1)}, u32[]{:S(2)}, u32[]{:S(2)}) collective-permute-start(bf16[24,1,512]{2,1,0:T(2,128)(2,1)S(1)} %get-tuple-element.91), channel_id=1, source_target_pairs={{1,0},{2,1},{3,2},{4,3},{5,4},{6,5},{7,6},{0,7},{9,8},{10,9},{11,1... | collective-permute-start | bytes 73736 | tf_op jit(solution)/shard_map/ppermute | solution.py:89
  167.0 8.3 %collective-permute-start.22 = (bf16[24,1,512]{2,1,0:T(2,128)(2,1)S(1)}, bf16[24,1,512]{2,1,0:T(2,128)(2,1)S(1)}, u32[]{:S(2)}, u32[]{:S(2)}) collective-permute-start(bf16[24,1,512]{2,1,0:T(2,128)(2,1)S(1)} %get-tuple-element.90), channel_id=1, source_target_pairs={{0,1},{1,2},{2,3},{3,4},{4,5},{5,6},{6,7},{7,0},{8,9},{9,10},{10,1... | collective-permute-start | bytes 73736 | tf_op jit(solution)/shard_map/ppermute | solution.py:88
  175.4 10.0 %collective-permute-start.24 = (bf16[1,66,512]{2,1,0:T(8,128)(2,1)S(1)}, bf16[1,66,512]{2,1,0:T(8,128)(2,1)S(1)}, u32[]{:S(2)}, u32[]{:S(2)}) collective-permute-start(bf16[1,66,512]{2,1,0:T(8,128)(2,1)S(1)} %get-tuple-element.82), channel_id=1, source_target_pairs={{0,8},{8,16},{16,24},{1,9},{9,17},{17,25},{2,10},{10,18},{18,26},{... | collective-permute-start | bytes 202760 | tf_op jit(solution)/shard_map/ppermute | solution.py:88
  177.1 8.2 %collective-permute-start.25 = (bf16[1,66,512]{2,1,0:T(8,128)(2,1)S(1)}, bf16[1,66,512]{2,1,0:T(8,128)(2,1)S(1)}, u32[]{:S(2)}, u32[]{:S(2)}) collective-permute-start(bf16[1,66,512]{2,1,0:T(8,128)(2,1)S(1)} %get-tuple-element.83), channel_id=1, source_target_pairs={{8,0},{16,8},{24,16},{9,1},{17,9},{25,17},{10,2},{18,10},{26,18},{... | collective-permute-start | bytes 202760 | tf_op jit(solution)/shard_map/ppermute | solution.py:89
  180.2 19.3 %collective-permute-start.12 = (bf16[128,4608]{1,0:T(8,128)(2,1)S(1)}, bf16[128,4608]{1,0:T(8,128)(2,1)S(1)}, u32[]{:S(2)}, u32[]{:S(2)}) collective-permute-start(bf16[128,4608]{1,0:T(8,128)(2,1)S(1)} %get-tuple-element.62), channel_id=1, source_target_pairs={{0,16},{1,17},{2,18},{3,19},{4,20},{5,21},{6,22},{7,23},{8,9},{9,8... | collective-permute-start | bytes 3538952 | tf_op jit(solution)/shard_map/ppermute | solution.py:40
  189.8 19.5 %collective-permute-start.14 = (bf16[128,640]{1,0:T(8,128)(2,1)S(1)}, bf16[128,640]{1,0:T(8,128)(2,1)S(1)}, u32[]{:S(2)}, u32[]{:S(2)}) collective-permute-start(bf16[128,640]{1,0:T(8,128)(2,1)S(1)} %get-tuple-element.96), channel_id=1, source_target_pairs={{0,16},{1,17},{2,18},{3,19},{4,20},{5,21},{6,22},{7,23},{8,9},{9,8... | collective-permute-start | bytes 491528 | tf_op jit(solution)/shard_map/ppermute | solution.py:40
  199.8 17.3 %collective-permute-start.15 = (bf16[64,4608]{1,0:T(8,128)(2,1)S(1)}, bf16[64,4608]{1,0:T(8,128)(2,1)S(1)}, u32[]{:S(2)}, u32[]{:S(2)}) collective-permute-start(bf16[64,4608]{1,0:T(8,128)(2,1)S(1)} %get-tuple-element.64), channel_id=1, source_target_pairs={{0,1},{1,0},{2,3},{3,2},{4,5},{5,4},{6,7},{7,6},{8,24},{9,25},{10,... | collective-permute-start | bytes 1769480 | tf_op jit(solution)/shard_map/ppermute | solution.py:40
  209.4 7.7 %collective-permute-start.16 = (bf16[64,640]{1,0:T(8,128)(2,1)S(1)}, bf16[64,640]{1,0:T(8,128)(2,1)S(1)}, u32[]{:S(2)}, u32[]{:S(2)}) collective-permute-start(bf16[64,640]{1,0:T(8,128)(2,1)S(1)} %get-tuple-element.98), channel_id=1, source_target_pairs={{0,1},{1,0},{2,3},{3,2},{4,5},{5,4},{6,7},{7,6},{8,24},{9,25},{10,... | collective-permute-start | bytes 245768 | tf_op jit(solution)/shard_map/ppermute | solution.py:40
  217.3 10.4 %collective-permute-start.17 = (bf16[32,5248]{1,0:T(8,128)(2,1)S(1)}, bf16[32,5248]{1,0:T(8,128)(2,1)S(1)}, u32[]{:S(2)}, u32[]{:S(2)}) collective-permute-start(bf16[32,5248]{1,0:T(8,128)(2,1)S(1)} %get-tuple-element.66), channel_id=1, source_target_pairs={{0,2},{1,3},{2,0},{3,1},{4,6},{5,7},{6,4},{7,5},{8,10},{9,11},{10,... | collective-permute-start | bytes 1007624 | tf_op jit(solution)/shard_map/ppermute | solution.py:40
  250.1 12.9 %collective-permute-start.21 = (bf16[64,5248]{1,0:T(8,128)(2,1)S(1)}, bf16[64,5248]{1,0:T(8,128)(2,1)S(1)}, u32[]{:S(2)}, u32[]{:S(2)}) collective-permute-start(bf16[64,5248]{1,0:T(8,128)(2,1)S(1)} %maximum_select_fusion.2), channel_id=1, source_target_pairs={{0,1},{1,0},{2,3},{3,2},{4,5},{5,4},{6,7},{7,6},{8,24},{9,25},{10,... | collective-permute-start | bytes 2015240 | tf_op jit(solution)/shard_map/ppermute | solution.py:40
  263.3 21.0 %collective-permute-start.26 = (bf16[128,5248]{1,0:T(8,128)(2,1)S(1)}, bf16[128,5248]{1,0:T(8,128)(2,1)}, u32[]{:S(2)}, u32[]{:S(2)}) collective-permute-start(bf16[128,5248]{1,0:T(8,128)(2,1)S(1)} %maximum_select_fusion.1), channel_id=1, source_target_pairs={{0,16},{1,17},{2,18},{3,19},{4,20},{5,21},{6,22},{7,23},{8,9},{9,8... | collective-permute-start | bytes 4030472 | tf_op jit(solution)/shard_map/ppermute | solution.py:40
  287.4 7.8 %collective-permute-start.27 = (bf16[256,5248]{1,0:T(8,128)(2,1)S(1)}, bf16[256,5248]{1,0:T(8,128)(2,1)}, u32[]{:S(2)}, u32[]{:S(2)}) collective-permute-start(bf16[256,5248]{1,0:T(8,128)(2,1)S(1)} %maximum_select_fusion.piece), channel_id=1, source_target_pairs={{0,8},{1,9},{2,10},{3,11},{4,12},{5,13},{6,14},{7,15},{8,0},{9,1},... | collective-permute-start | bytes 8060936 | tf_op jit(solution)/shard_map/ppermute | solution.py:40
  (26 other events, 182.3 us)
where the time goes:
time: 310 us; the launch traced here: 305 us
  waiting for transfers between devices  71.4 us (23%)
  starting transfers between devices  68.1 us (22%)
  Pallas kernels  64.1 us (21%)
  local copies, waits for them, and re-layouts  44.4 us (14%)
  matrix products  39.1 us (13%)
  other arithmetic  16.6 us (5%)
    ppermute x20, waiting for transfers between devices, exchange(): return lax.ppermute(value, AXES, pairs)  71.4 us
    pallas_call x8, Pallas kernels, call(): pl.pallas_call(body, out_shape=outs, grid_spec=pltpu.PrefetchScalarGridSp...  64.1 us
    ppermute x20, starting transfers between devices, exchange(): return lax.ppermute(value, AXES, pairs)  47 us
    unnamed x54, local copies, waits for them, and re-layouts  26.4 us
    dot_general x1, matrix products, nt(): lax.dot_general(left, right, (((1,), (1,)), ((), ())), preferred_element_...  12.3 us
    ppermute x4, starting transfers between devices, padded_2(): after = lax.ppermute(leading, axis, down)  10.7 us
    dot_general x9, matrix products, shards(): jnp.dot(window, conv_weight[a, b], preferred_element_type=jnp.float32)  10.4 us
    dot_general x1, matrix products, shards(): jnp.dot(pick(normed_t, 1 - core), windows, preferred_element_type=jnp.flo...  9.25 us
  transfers between devices with their start and end apart: 29, of which 10 were waited for; matrix products, arithmetic and copies ran while one was open for 27% of the time, Pallas kernels for 11%

commit v1 on v0

--- a/solution.py
+++ b/solution.py
@@ -14,7 +14,7 @@
 EPS = 1e-06
 LANES = 128
 AXES = ("lat", "lon")
-VMEM_LIMIT = 56 * 1024 * 1024
+VMEM_LIMIT = 24 * 1024 * 1024
 
 
 def bits_of(count):
@@ -104,7 +104,7 @@
 
 def whole(shape):
     zeros = (0,) * len(shape)
-    return pl.BlockSpec(shape, lambda *_: zeros)
+    return pl.BlockSpec(shape, lambda *_: zeros, pipeline_mode=pl.Buffered(1))
 
 
 def call(body, scalars, ins, outs, grid=(1,), in_specs=None, out_specs=None, scratch=(), alias=None):
@@ -266,30 +266,50 @@
     return call(body, meta, ins, outs, scratch=scratch)[0]
 
 
-def place(half, part, taps, lane, scale, into=None):
+def place(quarter, part, taps, lane, channels, scale, into=None):
     rows = part.shape[0]
-    steps = 8
+    steps = 2
     unit = rows // steps
 
-    def body(half_ref, piece, *refs):
+    def body(at, piece, small, *refs):
+        conv, encoder, gain = refs[-3:]
         for t in range(taps):
-            refs[-1][t] = piece[:, t * lane : (t + 1) * lane].astype(jnp.float32) * scale
-
-    specs = [pl.BlockSpec((unit, part.shape[1]), lambda i, h: (i, 0))]
-    ins = [part]
+            conv[t] = piece[:, t * lane : (t + 1) * lane].astype(jnp.float32) * scale
+
+        @pl.when(pl.program_id(0) == 0)
+        def _():
+            turned = (small[...].astype(jnp.float32) * scale).T
+            encoder[...] = turned[:channels]
+            gain[...] = turned[channels : channels + 1]
+
+    wide = taps * lane
+    extra = part.shape[1] - wide
+    specs = [
+        pl.BlockSpec((unit, wide), lambda i, q: (i, 0)),
+        pl.BlockSpec((rows, extra), lambda i, q: (0, 0)),
+    ]
+    ins = [part, part[:, wide:]]
     if into is not None:
-        ins.append(into)
-        specs.append(pl.BlockSpec(memory_space=pl.ANY))
+        ins += list(into)
+        specs += [pl.BlockSpec(memory_space=pl.ANY)] * 3
     return call(
         body,
-        half.reshape(1),
+        quarter.reshape(1),
         ins,
-        [shape_of((taps, 2 * rows, lane), jnp.float32)],
+        [
+            shape_of((taps, 4 * rows, lane), jnp.float32),
+            shape_of((channels, 4 * rows), jnp.float32),
+            shape_of((1, 4 * rows), jnp.float32),
+        ],
         grid=(steps,),
         in_specs=specs,
-        out_specs=[pl.BlockSpec((taps, unit, lane), lambda i, h: (0, h[0] * steps + i, 0))],
-        alias=None if into is None else {2: 0},
-    )[0]
+        out_specs=[
+            pl.BlockSpec((taps, unit, lane), lambda i, q: (0, q[0] * steps + i, 0)),
+            pl.BlockSpec((channels, rows), lambda i, q: (0, q[0])),
+            pl.BlockSpec((1, rows), lambda i, q: (0, q[0])),
+        ],
+        alias=None if into is None else {3: 0, 4: 1, 5: 2},
+    )
 
 
 def shards(
@@ -377,19 +397,23 @@
     keep = jnp.dot(pick(normed_t, core), windows, preferred_element_type=jnp.float32)
     came = step(away, plan[0][0], lats, lons)
 
+    away, keep = split_sum(keep, came, halves[1])
+    away, spread = lax.optimization_barrier((away, spread))
+    came = step(away, plan[1][0], lats, lons)
     small = backward(
         meta, arrived, kernels.transpose(0, 2, 1), gain_col, spread, slopes, d_normed_t
     )
     small_keep = pick(small, core)
     small_came = step(pick(small, 1 - core).astype(jnp.bfloat16), plan[0][0], lats, lons)
 
+    away, small_keep = split_sum(small_keep, small_came, halves[1])
+    small_came = step(away, plan[1][0], lats, lons)
     apart = len(plan) - 2
-    for n in range(1, apart):
+    for n in range(2, apart):
         away, keep = split_sum(keep, came, halves[n])
         came = step(away, plan[n][0], lats, lons)
         away, small_keep = split_sum(small_keep, small_came, halves[n])
         small_came = step(away, plan[n][0], lats, lons)
-    wide = taps * width
     keep = jnp.concatenate([keep, small_keep], axis=1)
     came = jnp.concatenate([came, small_came], axis=1)
     for n in range(apart, len(plan)):
@@ -407,23 +431,26 @@
             )
     conv_out = result_sum.reshape(tile_rows, tile_cols, width).astype(jnp.bfloat16)
     part = (keep + came.astype(jnp.float32)).astype(jnp.bfloat16)
-    for n in range(len(plan) - 1, 0, -1):
-        if n == 1:
-            part, conv_out = lax.optimization_barrier((part, conv_out))
+    for n in range(len(plan) - 1, 1, -1):
         other = step(part, plan[n][0], lats, lons)
         part = jnp.where(
             halves[n] == 0, jnp.concatenate([part, other]), jnp.concatenate([other, part])
         )
-    others = step(part, plan[0][0], lats, lons)
-    conv_total = place(core, part, taps, width, loss_scale)
-    conv_total = place(1 - core, others, taps, width, loss_scale, conv_total)
-    mine, theirs = part[:, wide:], others[:, wide:]
-    small = jnp.where(
-        core == 0, jnp.concatenate([mine, theirs]), jnp.concatenate([theirs, mine])
-    ).astype(jnp.float32) * loss_scale
-    gain_total = small[:, channels]
-    encoder_total = small[:, :channels].T
-
+    part, conv_out = lax.optimization_barrier((part, conv_out))
+    own, beside = halves[1], kept_half(plan[1][1], lat ^ 1, lon)
+    other = step(part, plan[1][0], lats, lons)
+    beside_part = step(part, plan[0][0], lats, lons)
+    beside_other = step(other, plan[0][0], lats, lons)
+    totals = None
+    for quarter, value in (
+        (2 * core + own, part),
+        (2 * (1 - core) + beside, beside_part),
+        (2 * core + 1 - own, other),
+        (2 * (1 - core) + 1 - beside, beside_other),
+    ):
+        totals = place(quarter, value, taps, width, channels, loss_scale, totals)
+    conv_total, encoder_total, gain_total = totals
+    gain_total = gain_total[0]
     return (conv_out, conv_total.reshape(3, 3, width, width), encoder_total, gain_total)
 
 

time: 310 us -> 288 us (0.929)
  Pallas kernels: 64.1 us -> 40.2 us
  starting transfers between devices: 68.1 us -> 73.2 us
  waiting for transfers between devices: 71.4 us -> 66.7 us
    pallas_call x8 -> x10, Pallas kernels: 64.1 us -> 40.2 us  [call(): pl.pallas_call(body, out_shape=outs, grid_spec=pltpu.PrefetchScalarGridSp...]
    ppermute x20 -> x21, starting transfers between devices: 47 us -> 52.1 us  [exchange(): return lax.ppermute(value, AXES, pairs)]
    ppermute x20 -> x21, waiting for transfers between devices: 71.4 us -> 66.6 us  [exchange(): return lax.ppermute(value, AXES, pairs)]
    select_n x4 -> x3, other arithmetic: 3.5 us -> 0.39 us  [shards(): jnp.where(halves[n] == 0, jnp.concatenate([part, other]), jnp.concatenate...]
    unnamed x54 -> x97, local copies, waits for them, and re-layouts: 26.4 us -> 28 us
  transfers between devices with their start and end apart: 29 -> 30, of which waited for: 10 -> 11; matrix products, arithmetic and copies ran while one was open for 27% -> 27% of each run, Pallas kernels for 11% -> 12%
where the time goes in v1:
time: 288 us; the launch traced here: 284 us
  starting transfers between devices  73.2 us (25%)
  waiting for transfers between devices  66.7 us (23%)
  local copies, waits for them, and re-layouts  46.3 us (16%)
  Pallas kernels  40.2 us (14%)
  matrix products  39.9 us (14%)
  other arithmetic  16 us (6%)
    ppermute x21, waiting for transfers between devices, exchange(): return lax.ppermute(value, AXES, pairs)  66.6 us
    ppermute x21, starting transfers between devices, exchange(): return lax.ppermute(value, AXES, pairs)  52.1 us
    pallas_call x10, Pallas kernels, call(): pl.pallas_call(body, out_shape=outs, grid_spec=pltpu.PrefetchScalarGridSp...  40.2 us
    unnamed x97, local copies, waits for them, and re-layouts  28 us
    dot_general x1, matrix products, nt(): lax.dot_general(left, right, (((1,), (1,)), ((), ())), preferred_element_...  13.4 us
    concatenate x5, other arithmetic, padded_2(): shard = jnp.concatenate([before, shard, after], axis=dim)  10.6 us
    ppermute x4, starting transfers between devices, padded_2(): after = lax.ppermute(leading, axis, down)  10.4 us
    dot_general x9, matrix products, shards(): jnp.dot(window, conv_weight[a, b], preferred_element_type=jnp.float32)  10.2 us
  transfers between devices with their start and end apart: 30, of which 11 were waited for; matrix products, arithmetic and copies ran while one was open for 27% of the time, Pallas kernels for 12%

profile of v1, /device:TPU:0, one launch (start us, length us, event | category | flops | bytes accessed | tf_op | source)
XLA Modules:
  0.0 283.8 jit_solution(6981500216985095982)
XLA Ops:
  4.1 7.3 %all-to-all-start = ((s32[8,1,3]{2,1,0:T(1,128)}), s32[8,1,3]{2,1,0:T(1,128)S(1)}, u32[]{:S(2)}, u32[]{:S(2)}) async-start(s32[8,1,3]{2,1,0:T(1,128)} %copy.81), calls=%async_computation | async-start | bytes 8192 | tf_op jit(solution)/shard_map/all_to_all | solution.py:355
  13.1 4.7 %collective-permute-start.1 = (bf16[24,1,512]{2,1,0:T(2,128)(2,1)}, bf16[24,1,512]{2,1,0:T(2,128)(2,1)}, u32[]{:S(2)}, u32[]{:S(2)}) collective-permute-start(bf16[24,1,512]{2,1,0:T(2,128)(2,1)} %get-tuple-element.107), channel_id=1, source_target_pairs={{1,0},{2,1},{3,2},{4,3},{5,4},{6,5},{7,6},{0,7},{9,8},{10,9},{11,1... | collective-permute-start | bytes 73736 | tf_op jit(solution)/shard_map/ppermute | solution.py:89
  27.9 3.2 %copy.88 = bf16[3,4,8,16,512]{4,3,2,1,0:T(8,128)(2,1)} copy(bf16[3,4,8,16,512]{4,3,1,2,0:T(8,128)(2,1)} %bitcast.164) | data formatting | bytes 3145728 | tf_op jit(solution)/shard_map/transpose | solution.py:102
  31.2 6.7 %copy.93 = bf16[3,3,512,512]{2,3,1,0:T(8,128)(2,1)} copy(bf16[3,3,512,512]{3,2,1,0:T(8,128)(2,1)} %param.16) | data formatting | bytes 9437184 | tf_op args[7]
  68.8 4.1 %collective-permute-start.7 = (bf16[616,384]{1,0:T(8,128)(2,1)S(1)}, bf16[616,384]{1,0:T(8,128)(2,1)S(1)}, u32[]{:S(2)}, u32[]{:S(2)}) collective-permute-start(bf16[616,384]{1,0:T(8,128)(2,1)S(1)} %copy-done.28), channel_id=1, source_target_pairs={{0,6},{1,7},{2,4},{3,5},{4,2},{5,3},{6,0},{7,1},{8,14},{9,15},{10,... | collective-permute-start | bytes 1419272 | tf_op jit(solution)/shard_map/ppermute | solution.py:40
  72.9 13.4 %convolution_bitcast_fusion.refs_14_ = f32[512,1536]{1,0:T(8,128)} fusion(bf16[1536,4608]{1,0:T(8,128)(2,1)} %constant_dynamic-update-slice_fusion, bf16[512,4608]{0,1:T(8,128)(2,1)} %bitcast.194), kind=kOutput, calls=%fused_computation.11 | convolution fusion | flops 7247757312 | bytes 22020096 | tf_op jit(solution)/shard_map/dot_general | solution.py:131
  86.3 6.6 %shard_map.122 = (f32[12,512,128]{2,1,0:T(8,128)S(1)}, bf16[4,512,384]{2,1,0:T(8,128)(2,1)S(1)}) custom-call(s32[24]{0:T(128)S(1)} %reshape.354.meta_ref, bf16[616,384]{1,0:T(8,128)(2,1)S(1)} %get-tuple-element.43.refs_0_, bf16[616,384]{1,0:T(8,128)(2,1)S(1)} %collective-permute-done.8.refs_1_, bf16[616,384]{1,0:T(8,128)(2,1)S(1)} %collective-permute-done.9.refs_2_, ...), custom_call_target="tpu_custom_call" | custom-call | tf_op jit(solution)/shard_map/pallas_call | solution.py:111
  93.0 8.2 %collective-permute-done.5.refs_0_.refs_4_ = bf16[616,384]{1,0:T(8,128)(2,1)S(1)} collective-permute-done((bf16[616,384]{1,0:T(8,128)(2,1)S(1)}, bf16[616,384]{1,0:T(8,128)(2,1)S(1)}, u32[]{:S(2)}, u32[]{:S(2)}) %collective-permute-start.5) | collective-permute-done | bytes 473120 | tf_op jit(solution)/shard_map/ppermute | solution.py:40
  101.2 9.4 %collective-permute-done.6.refs_1_.refs_5_ = bf16[616,384]{1,0:T(8,128)(2,1)S(1)} collective-permute-done((bf16[616,384]{1,0:T(8,128)(2,1)S(1)}, bf16[616,384]{1,0:T(8,128)(2,1)S(1)}, u32[]{:S(2)}, u32[]{:S(2)}) %collective-permute-start.6) | collective-permute-done | bytes 473120 | tf_op jit(solution)/shard_map/ppermute | solution.py:40
  110.6 4.3 %shard_map.123 = (f32[12,512,128]{2,1,0:T(8,128)S(1)}, bf16[3,512,384]{2,1,0:T(8,128)(2,1)S(1)}) custom-call(s32[24]{0:T(128)S(1)} %reshape.354.meta_ref, bf16[616,384]{1,0:T(8,128)(2,1)S(1)} %collective-permute-done.5.refs_0_.refs_4_, bf16[616,384]{1,0:T(8,128)(2,1)S(1)} %collective-permute-done.6.refs_1_.refs_5_, ...), custom_call_target="tpu_custom_call" | custom-call | tf_op jit(solution)/shard_map/pallas_call | solution.py:111
  122.8 9.2 %convolution_convert_fusion = bf16[256,4608]{1,0:T(8,128)(2,1)S(1)} fusion(bf16[1536,4608]{1,0:T(8,128)(2,1)} %constant_dynamic-update-slice_fusion, bf16[2,256,1536]{2,1,0:T(8,128)(2,1)S(1)} %bitcast.155, s32[]{:T(128)S(6)} %select_n.115), kind=kOutput, calls=%fused_computation.2 | convolution fusion | flops 3625058304 | bytes 17301508 | tf_op jit(solution)/shard_map/dot_general | solution.py:394
  137.8 7.1 %fusion = f32[2,128,4608]{2,1,0:T(8,128)S(1)} fusion(bf16[2,128,1536]{2,1,0:T(8,128)(2,1)S(1)} %bitcast.204, bf16[1536,4608]{1,0:T(8,128)(2,1)} %constant_dynamic-update-slice_fusion), kind=kOutput, calls=%fused_computation | convolution fusion | flops 3623878656 | bytes 19660800 | tf_op jit(solution)/shard_map/dot_general | solution.py:397
  154.2 4.6 %collective-permute-start.12 = (bf16[128,4608]{1,0:T(8,128)(2,1)}, bf16[128,4608]{1,0:T(8,128)(2,1)S(1)}, u32[]{:S(2)}, u32[]{:S(2)}) collective-permute-start(bf16[128,4608]{1,0:T(8,128)(2,1)} %get-tuple-element.52), channel_id=1, source_target_pairs={{0,16},{1,17},{2,18},{3,19},{4,20},{5,21},{6,22},{7,23},{8,9},{9,8... | collective-permute-start | bytes 3538952 | tf_op jit(solution)/shard_map/ppermute | solution.py:40
  165.0 13.5 %shard_map.125 = f32[512,640]{1,0:T(8,128)S(1)} custom-call(s32[24]{0:T(128)S(1)} %reshape.354.meta_ref, bf16[616,384]{1,0:T(8,128)(2,1)S(1)} %copy-done.6, bf16[616,384]{1,0:T(8,128)(2,1)S(1)} %copy-done.8, bf16[616,384]{1,0:T(8,128)(2,1)S(1)} %copy-done.10, bf16[616,384]{1,0:T(8,128)(2,1)} %collective-permute-done.10.refs_3_, ...), custom_call_target="tpu_custom_call" | custom-call | tf_op jit(solution)/shard_map/pallas_call | solution.py:111
  178.6 11.6 %collective-permute-start.13 = (bf16[256,640]{1,0:T(8,128)(2,1)S(1)}, bf16[256,640]{1,0:T(8,128)(2,1)S(1)}, u32[]{:S(2)}, u32[]{:S(2)}) collective-permute-start(bf16[256,640]{1,0:T(8,128)(2,1)S(1)} %fusion.37), channel_id=1, source_target_pairs={{0,8},{1,9},{2,10},{3,11},{4,12},{5,13},{6,14},{7,15},{8,0},{9,1},... | collective-permute-start | bytes 983048 | tf_op jit(solution)/shard_map/ppermute | solution.py:40
  197.2 3.8 %collective-permute-start.16 = (bf16[64,640]{1,0:T(8,128)(2,1)S(1)}, bf16[64,640]{1,0:T(8,128)(2,1)S(1)}, u32[]{:S(2)}, u32[]{:S(2)}) collective-permute-start(bf16[64,640]{1,0:T(8,128)(2,1)S(1)} %get-tuple-element.110), channel_id=1, source_target_pairs={{0,1},{1,0},{2,3},{3,2},{4,5},{5,4},{6,7},{7,6},{8,24},{9,25},{10,... | collective-permute-start | bytes 245768 | tf_op jit(solution)/shard_map/ppermute | solution.py:40
  207.7 7.2 %collective-permute-done.17 = bf16[32,5248]{1,0:T(8,128)(2,1)S(1)} collective-permute-done((bf16[32,5248]{1,0:T(8,128)(2,1)S(1)}, bf16[32,5248]{1,0:T(8,128)(2,1)S(1)}, u32[]{:S(2)}, u32[]{:S(2)}) %collective-permute-start.17) | collective-permute-done | bytes 335904 | tf_op jit(solution)/shard_map/ppermute | solution.py:40
  215.0 3.6 %collective-permute-start.18 = (bf16[16,5248]{1,0:T(8,128)(2,1)S(1)}, bf16[16,5248]{1,0:T(8,128)(2,1)S(1)}, u32[]{:S(2)}, u32[]{:S(2)}) collective-permute-start(bf16[16,5248]{1,0:T(8,128)(2,1)S(1)} %fusion.38), channel_id=1, source_target_pairs={{0,6},{1,7},{2,4},{3,5},{4,2},{5,3},{6,0},{7,1},{8,14},{9,15},{10,... | collective-permute-start | bytes 503816 | tf_op jit(solution)/shard_map/ppermute | solution.py:40
  219.7 3.5 %collective-permute-done.18 = bf16[16,5248]{1,0:T(8,128)(2,1)S(1)} collective-permute-done((bf16[16,5248]{1,0:T(8,128)(2,1)S(1)}, bf16[16,5248]{1,0:T(8,128)(2,1)S(1)}, u32[]{:S(2)}, u32[]{:S(2)}) %collective-permute-start.18) | collective-permute-done | bytes 167968 | tf_op jit(solution)/shard_map/ppermute | solution.py:40
  223.3 3.6 %collective-permute-start.19 = (bf16[16,5248]{1,0:T(8,128)(2,1)S(1)}, bf16[16,5248]{1,0:T(8,128)(2,1)S(1)}, u32[]{:S(2)}, u32[]{:S(2)}) collective-permute-start(bf16[16,5248]{1,0:T(8,128)(2,1)S(1)} %fusion.36), channel_id=1, source_target_pairs={{0,6},{1,7},{2,4},{3,5},{4,2},{5,3},{6,0},{7,1},{8,14},{9,15},{10,... | collective-permute-start | bytes 503816 | tf_op jit(solution)/shard_map/ppermute | solution.py:40
  230.7 4.3 %collective-permute-start.20 = (bf16[32,5248]{1,0:T(8,128)(2,1)S(1)}, bf16[32,5248]{1,0:T(8,128)(2,1)S(1)}, u32[]{:S(2)}, u32[]{:S(2)}) collective-permute-start(bf16[32,5248]{1,0:T(8,128)(2,1)S(1)} %maximum_select_fusion.2), channel_id=1, source_target_pairs={{0,2},{1,3},{2,0},{3,1},{4,6},{5,7},{6,4},{7,5},{8,10},{9,11},{10,... | collective-permute-start | bytes 1007624 | tf_op jit(solution)/shard_map/ppermute | solution.py:40
  236.0 7.1 %collective-permute-done.20 = bf16[32,5248]{1,0:T(8,128)(2,1)S(1)} collective-permute-done((bf16[32,5248]{1,0:T(8,128)(2,1)S(1)}, bf16[32,5248]{1,0:T(8,128)(2,1)S(1)}, u32[]{:S(2)}, u32[]{:S(2)}) %collective-permute-start.20) | collective-permute-done | bytes 335904 | tf_op jit(solution)/shard_map/ppermute | solution.py:40
  247.4 6.6 %collective-permute-done.21 = bf16[64,5248]{1,0:T(8,128)(2,1)S(1)} collective-permute-done((bf16[64,5248]{1,0:T(8,128)(2,1)S(1)}, bf16[64,5248]{1,0:T(8,128)(2,1)S(1)}, u32[]{:S(2)}, u32[]{:S(2)}) %collective-permute-start.21) | collective-permute-done | bytes 671776 | tf_op jit(solution)/shard_map/ppermute | solution.py:40
  254.4 17.9 %collective-permute-done.26.piece = bf16[128,5248]{1,0:T(8,128)(2,1)S(1)} collective-permute-done((bf16[128,5248]{1,0:T(8,128)(2,1)S(1)}, bf16[128,5248]{1,0:T(8,128)(2,1)S(1)}, u32[]{:S(2)}, u32[]{:S(2)}) %collective-permute-start.26) | collective-permute-done | bytes 1343520 | tf_op jit(solution)/shard_map/ppermute | solution.py:40
  (216 shorter events, 110.8 us)
Async XLA Ops:
  4.1 35.1 %all-to-all-start = ((s32[8,1,3]{2,1,0:T(1,128)}), s32[8,1,3]{2,1,0:T(1,128)S(1)}, u32[]{:S(2)}, u32[]{:S(2)}) async-start(s32[8,1,3]{2,1,0:T(1,128)} %copy.81), calls=%async_computation | async-start | bytes 8192 | tf_op jit(solution)/shard_map/all_to_all | solution.py:355
  13.1 26.5 %collective-permute-start.1 = (bf16[24,1,512]{2,1,0:T(2,128)(2,1)}, bf16[24,1,512]{2,1,0:T(2,128)(2,1)}, u32[]{:S(2)}, u32[]{:S(2)}) collective-permute-start(bf16[24,1,512]{2,1,0:T(2,128)(2,1)} %get-tuple-element.107), channel_id=1, source_target_pairs={{1,0},{2,1},{3,2},{4,3},{5,4},{6,5},{7,6},{0,7},{9,8},{10,9},{11,1... | collective-permute-start | bytes 73736 | tf_op jit(solution)/shard_map/ppermute | solution.py:89
  17.8 21.8 %collective-permute-start = (bf16[24,1,512]{2,1,0:T(2,128)(2,1)}, bf16[24,1,512]{2,1,0:T(2,128)(2,1)}, u32[]{:S(2)}, u32[]{:S(2)}) collective-permute-start(bf16[24,1,512]{2,1,0:T(2,128)(2,1)} %get-tuple-element.106), channel_id=1, source_target_pairs={{0,1},{1,2},{2,3},{3,4},{4,5},{5,6},{6,7},{7,0},{8,9},{9,10},{10,1... | collective-permute-start | bytes 73736 | tf_op jit(solution)/shard_map/ppermute | solution.py:88
  22.4 46.4 %collective-permute-start.8 = (bf16[616,384]{1,0:T(8,128)(2,1)}, bf16[616,384]{1,0:T(8,128)(2,1)S(1)}, u32[]{:S(2)}, u32[]{:S(2)}) collective-permute-start(bf16[616,384]{1,0:T(8,128)(2,1)} %get-tuple-element.44), channel_id=1, source_target_pairs={{0,1},{1,0},{2,3},{3,2},{4,5},{5,4},{6,7},{7,6},{8,9},{9,8},{10,11... | collective-permute-start | bytes 1419272 | tf_op jit(solution)/shard_map/ppermute | solution.py:40
  22.7 50.2 %collective-permute-start.9 = (bf16[616,384]{1,0:T(8,128)(2,1)}, bf16[616,384]{1,0:T(8,128)(2,1)S(1)}, u32[]{:S(2)}, u32[]{:S(2)}) collective-permute-start(bf16[616,384]{1,0:T(8,128)(2,1)} %get-tuple-element.45), channel_id=1, source_target_pairs={{0,2},{1,3},{2,0},{3,1},{4,6},{5,7},{6,4},{7,5},{8,10},{9,11},{10,... | collective-permute-start | bytes 1419272 | tf_op jit(solution)/shard_map/ppermute | solution.py:40
  24.1 62.2 %collective-permute-start.10 = (bf16[616,384]{1,0:T(8,128)(2,1)}, bf16[616,384]{1,0:T(8,128)(2,1)}, u32[]{:S(2)}, u32[]{:S(2)}) collective-permute-start(bf16[616,384]{1,0:T(8,128)(2,1)} %get-tuple-element.46), channel_id=1, source_target_pairs={{0,3},{1,2},{2,1},{3,0},{4,7},{5,6},{6,5},{7,4},{8,11},{9,10},{10,... | collective-permute-start | bytes 1419272 | tf_op jit(solution)/shard_map/ppermute | solution.py:40
  46.5 54.6 %collective-permute-start.5 = (bf16[616,384]{1,0:T(8,128)(2,1)S(1)}, bf16[616,384]{1,0:T(8,128)(2,1)S(1)}, u32[]{:S(2)}, u32[]{:S(2)}) collective-permute-start(bf16[616,384]{1,0:T(8,128)(2,1)S(1)} %copy-done.32), channel_id=1, source_target_pairs={{0,4},{1,5},{2,6},{3,7},{4,0},{5,1},{6,2},{7,3},{8,12},{9,13},{10,... | collective-permute-start | bytes 1419272 | tf_op jit(solution)/shard_map/ppermute | solution.py:40
  48.9 61.7 %collective-permute-start.6 = (bf16[616,384]{1,0:T(8,128)(2,1)S(1)}, bf16[616,384]{1,0:T(8,128)(2,1)S(1)}, u32[]{:S(2)}, u32[]{:S(2)}) collective-permute-start(bf16[616,384]{1,0:T(8,128)(2,1)S(1)} %copy-done.30), channel_id=1, source_target_pairs={{0,5},{1,4},{2,7},{3,6},{4,1},{5,0},{6,3},{7,2},{8,13},{9,12},{10,... | collective-permute-start | bytes 1419272 | tf_op jit(solution)/shard_map/ppermute | solution.py:40
  68.8 41.8 %collective-permute-start.7 = (bf16[616,384]{1,0:T(8,128)(2,1)S(1)}, bf16[616,384]{1,0:T(8,128)(2,1)S(1)}, u32[]{:S(2)}, u32[]{:S(2)}) collective-permute-start(bf16[616,384]{1,0:T(8,128)(2,1)S(1)} %copy-done.28), channel_id=1, source_target_pairs={{0,6},{1,7},{2,4},{3,5},{4,2},{5,3},{6,0},{7,1},{8,14},{9,15},{10,... | collective-permute-start | bytes 1419272 | tf_op jit(solution)/shard_map/ppermute | solution.py:40
  72.9 43.1 %collective-permute-start.4 = (bf16[616,384]{1,0:T(8,128)(2,1)S(1)}, bf16[616,384]{1,0:T(8,128)(2,1)S(1)}, u32[]{:S(2)}, u32[]{:S(2)}) collective-permute-start(bf16[616,384]{1,0:T(8,128)(2,1)S(1)} %copy-done.26), channel_id=1, source_target_pairs={{0,7},{1,6},{2,5},{3,4},{4,3},{5,2},{6,1},{7,0},{8,15},{9,14},{10,... | collective-permute-start | bytes 1419272 | tf_op jit(solution)/shard_map/ppermute | solution.py:40
  132.0 20.5 %collective-permute-start.11 = (bf16[256,4608]{1,0:T(8,128)(2,1)S(1)}, bf16[256,4608]{1,0:T(8,128)(2,1)S(1)}, u32[]{:S(2)}, u32[]{:S(2)}) collective-permute-start(bf16[256,4608]{1,0:T(8,128)(2,1)S(1)} %convolution_convert_fusion), channel_id=1, source_target_pairs={{0,8},{1,9},{2,10},{3,11},{4,12},{5,13},{6,14},{7,15},{8,0},{9,1},... | collective-permute-start | bytes 7077896 | tf_op jit(solution)/shard_map/ppermute | solution.py:40
  135.3 10.7 %collective-permute-start.23 = (bf16[24,1,512]{2,1,0:T(2,128)(2,1)S(1)}, bf16[24,1,512]{2,1,0:T(2,128)(2,1)S(1)}, u32[]{:S(2)}, u32[]{:S(2)}) collective-permute-start(bf16[24,1,512]{2,1,0:T(2,128)(2,1)S(1)} %get-tuple-element.103), channel_id=1, source_target_pairs={{1,0},{2,1},{3,2},{4,3},{5,4},{6,5},{7,6},{0,7},{9,8},{10,9},{11,1... | collective-permute-start | bytes 73736 | tf_op jit(solution)/shard_map/ppermute | solution.py:89
  137.8 8.2 %collective-permute-start.22 = (bf16[24,1,512]{2,1,0:T(2,128)(2,1)S(1)}, bf16[24,1,512]{2,1,0:T(2,128)(2,1)S(1)}, u32[]{:S(2)}, u32[]{:S(2)}) collective-permute-start(bf16[24,1,512]{2,1,0:T(2,128)(2,1)S(1)} %get-tuple-element.102), channel_id=1, source_target_pairs={{0,1},{1,2},{2,3},{3,4},{4,5},{5,6},{6,7},{7,0},{8,9},{9,10},{10,1... | collective-permute-start | bytes 73736 | tf_op jit(solution)/shard_map/ppermute | solution.py:88
  146.1 12.8 %collective-permute-start.24 = (bf16[1,66,512]{2,1,0:T(8,128)(2,1)S(1)}, bf16[1,66,512]{2,1,0:T(8,128)(2,1)S(1)}, u32[]{:S(2)}, u32[]{:S(2)}) collective-permute-start(bf16[1,66,512]{2,1,0:T(8,128)(2,1)S(1)} %get-tuple-element.94), channel_id=1, source_target_pairs={{0,8},{8,16},{16,24},{1,9},{9,17},{17,25},{2,10},{10,18},{18,26},{... | collective-permute-start | bytes 202760 | tf_op jit(solution)/shard_map/ppermute | solution.py:88
  148.1 10.7 %collective-permute-start.25 = (bf16[1,66,512]{2,1,0:T(8,128)(2,1)S(1)}, bf16[1,66,512]{2,1,0:T(8,128)(2,1)S(1)}, u32[]{:S(2)}, u32[]{:S(2)}) collective-permute-start(bf16[1,66,512]{2,1,0:T(8,128)(2,1)S(1)} %get-tuple-element.95), channel_id=1, source_target_pairs={{8,0},{16,8},{24,16},{9,1},{17,9},{25,17},{10,2},{18,10},{26,18},{... | collective-permute-start | bytes 202760 | tf_op jit(solution)/shard_map/ppermute | solution.py:89
  154.2 38.0 %collective-permute-start.12 = (bf16[128,4608]{1,0:T(8,128)(2,1)}, bf16[128,4608]{1,0:T(8,128)(2,1)S(1)}, u32[]{:S(2)}, u32[]{:S(2)}) collective-permute-start(bf16[128,4608]{1,0:T(8,128)(2,1)} %get-tuple-element.52), channel_id=1, source_target_pairs={{0,16},{1,17},{2,18},{3,19},{4,20},{5,21},{6,22},{7,23},{8,9},{9,8... | collective-permute-start | bytes 3538952 | tf_op jit(solution)/shard_map/ppermute | solution.py:40
  178.6 12.8 %collective-permute-start.13 = (bf16[256,640]{1,0:T(8,128)(2,1)S(1)}, bf16[256,640]{1,0:T(8,128)(2,1)S(1)}, u32[]{:S(2)}, u32[]{:S(2)}) collective-permute-start(bf16[256,640]{1,0:T(8,128)(2,1)S(1)} %fusion.37), channel_id=1, source_target_pairs={{0,8},{1,9},{2,10},{3,11},{4,12},{5,13},{6,14},{7,15},{8,0},{9,1},... | collective-permute-start | bytes 983048 | tf_op jit(solution)/shard_map/ppermute | solution.py:40
  192.3 11.4 %collective-permute-start.15 = (bf16[64,4608]{1,0:T(8,128)(2,1)S(1)}, bf16[64,4608]{1,0:T(8,128)(2,1)S(1)}, u32[]{:S(2)}, u32[]{:S(2)}) collective-permute-start(bf16[64,4608]{1,0:T(8,128)(2,1)S(1)} %get-tuple-element.76), channel_id=1, source_target_pairs={{0,1},{1,0},{2,3},{3,2},{4,5},{5,4},{6,7},{7,6},{8,24},{9,25},{10,... | collective-permute-start | bytes 1769480 | tf_op jit(solution)/shard_map/ppermute | solution.py:40
  204.0 11.0 %collective-permute-start.17 = (bf16[32,5248]{1,0:T(8,128)(2,1)S(1)}, bf16[32,5248]{1,0:T(8,128)(2,1)S(1)}, u32[]{:S(2)}, u32[]{:S(2)}) collective-permute-start(bf16[32,5248]{1,0:T(8,128)(2,1)S(1)} %get-tuple-element.78), channel_id=1, source_target_pairs={{0,2},{1,3},{2,0},{3,1},{4,6},{5,7},{6,4},{7,5},{8,10},{9,11},{10,... | collective-permute-start | bytes 1007624 | tf_op jit(solution)/shard_map/ppermute | solution.py:40
  215.0 8.2 %collective-permute-start.18 = (bf16[16,5248]{1,0:T(8,128)(2,1)S(1)}, bf16[16,5248]{1,0:T(8,128)(2,1)S(1)}, u32[]{:S(2)}, u32[]{:S(2)}) collective-permute-start(bf16[16,5248]{1,0:T(8,128)(2,1)S(1)} %fusion.38), channel_id=1, source_target_pairs={{0,6},{1,7},{2,4},{3,5},{4,2},{5,3},{6,0},{7,1},{8,14},{9,15},{10,... | collective-permute-start | bytes 503816 | tf_op jit(solution)/shard_map/ppermute | solution.py:40
  230.7 12.4 %collective-permute-start.20 = (bf16[32,5248]{1,0:T(8,128)(2,1)S(1)}, bf16[32,5248]{1,0:T(8,128)(2,1)S(1)}, u32[]{:S(2)}, u32[]{:S(2)}) collective-permute-start(bf16[32,5248]{1,0:T(8,128)(2,1)S(1)} %maximum_select_fusion.2), channel_id=1, source_target_pairs={{0,2},{1,3},{2,0},{3,1},{4,6},{5,7},{6,4},{7,5},{8,10},{9,11},{10,... | collective-permute-start | bytes 1007624 | tf_op jit(solution)/shard_map/ppermute | solution.py:40
  243.2 10.8 %collective-permute-start.21 = (bf16[64,5248]{1,0:T(8,128)(2,1)S(1)}, bf16[64,5248]{1,0:T(8,128)(2,1)S(1)}, u32[]{:S(2)}, u32[]{:S(2)}) collective-permute-start(bf16[64,5248]{1,0:T(8,128)(2,1)S(1)} %maximum_select_fusion.1), channel_id=1, source_target_pairs={{0,1},{1,0},{2,3},{3,2},{4,5},{5,4},{6,7},{7,6},{8,24},{9,25},{10,... | collective-permute-start | bytes 2015240 | tf_op jit(solution)/shard_map/ppermute | solution.py:40
  254.2 18.0 %collective-permute-start.26 = (bf16[128,5248]{1,0:T(8,128)(2,1)S(1)}, bf16[128,5248]{1,0:T(8,128)(2,1)S(1)}, u32[]{:S(2)}, u32[]{:S(2)}) collective-permute-start(bf16[128,5248]{1,0:T(8,128)(2,1)S(1)} %maximum_select_fusion.piece), channel_id=1, source_target_pairs={{0,16},{1,17},{2,18},{3,19},{4,20},{5,21},{6,22},{7,23},{8,9},{9,8... | collective-permute-start | bytes 4030472 | tf_op jit(solution)/shard_map/ppermute | solution.py:40
  254.3 19.9 %collective-permute-start.28 = (bf16[128,5248]{1,0:T(8,128)(2,1)S(1)}, bf16[128,5248]{1,0:T(8,128)(2,1)}, u32[]{:S(2)}, u32[]{:S(2)}) collective-permute-start(bf16[128,5248]{1,0:T(8,128)(2,1)S(1)} %maximum_select_fusion.piece), channel_id=1, source_target_pairs={{0,8},{1,9},{2,10},{3,11},{4,12},{5,13},{6,14},{7,15},{8,0},{9,1},... | collective-permute-start | bytes 4030472 | tf_op jit(solution)/shard_map/ppermute | solution.py:40
  (49 other events, 316.4 us)

commit v2 on v1

--- a/solution.py
+++ b/solution.py
@@ -278,17 +278,12 @@
 
         @pl.when(pl.program_id(0) == 0)
         def _():
-            turned = (small[...].astype(jnp.float32) * scale).T
+            turned = (small[:, taps * lane :].astype(jnp.float32) * scale).T
             encoder[...] = turned[:channels]
             gain[...] = turned[channels : channels + 1]
 
-    wide = taps * lane
-    extra = part.shape[1] - wide
-    specs = [
-        pl.BlockSpec((unit, wide), lambda i, q: (i, 0)),
-        pl.BlockSpec((rows, extra), lambda i, q: (0, 0)),
-    ]
-    ins = [part, part[:, wide:]]
+    specs = [pl.BlockSpec((unit, part.shape[1]), lambda i, q: (i, 0)), whole(part.shape)]
+    ins = [part, part]
     if into is not None:
         ins += list(into)
         specs += [pl.BlockSpec(memory_space=pl.ANY)] * 3

time: 288 us -> 287 us (level)
  no operation moved by 1% of the time
where the time goes in v2:
time: 287 us; the launch traced here: 283 us
  starting transfers between devices  73.2 us (26%)
  waiting for transfers between devices  66.7 us (23%)
  local copies, waits for them, and re-layouts  44.4 us (15%)
  Pallas kernels  41.1 us (14%)
  matrix products  39.9 us (14%)
  other arithmetic  16 us (6%)
    ppermute x21, waiting for transfers between devices, exchange(): return lax.ppermute(value, AXES, pairs)  66.6 us
    ppermute x21, starting transfers between devices, exchange(): return lax.ppermute(value, AXES, pairs)  52.1 us
    pallas_call x10, Pallas kernels, call(): pl.pallas_call(body, out_shape=outs, grid_spec=pltpu.PrefetchScalarGridSp...  41.1 us
    unnamed x97, local copies, waits for them, and re-layouts  28 us
    dot_general x1, matrix products, nt(): lax.dot_general(left, right, (((1,), (1,)), ((), ())), preferred_element_...  13.4 us
    concatenate x5, other arithmetic, padded_2(): shard = jnp.concatenate([before, shard, after], axis=dim)  10.6 us
    ppermute x4, starting transfers between devices, padded_2(): after = lax.ppermute(leading, axis, down)  10.4 us
    dot_general x9, matrix products, shards(): jnp.dot(window, conv_weight[a, b], preferred_element_type=jnp.float32)  10.2 us
  transfers between devices with their start and end apart: 30, of which 11 were waited for; matrix products, arithmetic and copies ran while one was open for 27% of the time, Pallas kernels for 12%

profile of v2, /device:TPU:0, one launch (start us, length us, event | category | flops | bytes accessed | tf_op | source)
XLA Modules:
  0.0 282.8 jit_solution(10981608408332592033)
XLA Ops:
  4.1 7.3 %all-to-all-start = ((s32[8,1,3]{2,1,0:T(1,128)}), s32[8,1,3]{2,1,0:T(1,128)S(1)}, u32[]{:S(2)}, u32[]{:S(2)}) async-start(s32[8,1,3]{2,1,0:T(1,128)} %copy.81), calls=%async_computation | async-start | bytes 8192 | tf_op jit(solution)/shard_map/all_to_all | solution.py:350
  13.1 4.7 %collective-permute-start.1 = (bf16[24,1,512]{2,1,0:T(2,128)(2,1)}, bf16[24,1,512]{2,1,0:T(2,128)(2,1)}, u32[]{:S(2)}, u32[]{:S(2)}) collective-permute-start(bf16[24,1,512]{2,1,0:T(2,128)(2,1)} %get-tuple-element.107), channel_id=1, source_target_pairs={{1,0},{2,1},{3,2},{4,3},{5,4},{6,5},{7,6},{0,7},{9,8},{10,9},{11,1... | collective-permute-start | bytes 73736 | tf_op jit(solution)/shard_map/ppermute | solution.py:89
  31.2 6.7 %copy.93 = bf16[3,3,512,512]{2,3,1,0:T(8,128)(2,1)} copy(bf16[3,3,512,512]{3,2,1,0:T(8,128)(2,1)} %param.16) | data formatting | bytes 9437184 | tf_op args[7]
  68.8 4.1 %collective-permute-start.7 = (bf16[616,384]{1,0:T(8,128)(2,1)S(1)}, bf16[616,384]{1,0:T(8,128)(2,1)S(1)}, u32[]{:S(2)}, u32[]{:S(2)}) collective-permute-start(bf16[616,384]{1,0:T(8,128)(2,1)S(1)} %copy-done.28), channel_id=1, source_target_pairs={{0,6},{1,7},{2,4},{3,5},{4,2},{5,3},{6,0},{7,1},{8,14},{9,15},{10,... | collective-permute-start | bytes 1419272 | tf_op jit(solution)/shard_map/ppermute | solution.py:40
  72.9 13.4 %convolution_bitcast_fusion.refs_14_ = f32[512,1536]{1,0:T(8,128)} fusion(bf16[1536,4608]{1,0:T(8,128)(2,1)} %constant_dynamic-update-slice_fusion, bf16[512,4608]{0,1:T(8,128)(2,1)} %bitcast.194), kind=kOutput, calls=%fused_computation.11 | convolution fusion | flops 7247757312 | bytes 22020096 | tf_op jit(solution)/shard_map/dot_general | solution.py:131
  86.3 6.6 %shard_map.122 = (f32[12,512,128]{2,1,0:T(8,128)S(1)}, bf16[4,512,384]{2,1,0:T(8,128)(2,1)S(1)}) custom-call(s32[24]{0:T(128)S(1)} %reshape.354.meta_ref, bf16[616,384]{1,0:T(8,128)(2,1)S(1)} %get-tuple-element.43.refs_0_, bf16[616,384]{1,0:T(8,128)(2,1)S(1)} %collective-permute-done.8.refs_1_, bf16[616,384]{1,0:T(8,128)(2,1)S(1)} %collective-permute-done.9.refs_2_, ...), custom_call_target="tpu_custom_call" | custom-call | tf_op jit(solution)/shard_map/pallas_call | solution.py:111
  93.0 8.2 %collective-permute-done.5.refs_0_.refs_4_ = bf16[616,384]{1,0:T(8,128)(2,1)S(1)} collective-permute-done((bf16[616,384]{1,0:T(8,128)(2,1)S(1)}, bf16[616,384]{1,0:T(8,128)(2,1)S(1)}, u32[]{:S(2)}, u32[]{:S(2)}) %collective-permute-start.5) | collective-permute-done | bytes 473120 | tf_op jit(solution)/shard_map/ppermute | solution.py:40
  101.2 9.4 %collective-permute-done.6.refs_1_.refs_5_ = bf16[616,384]{1,0:T(8,128)(2,1)S(1)} collective-permute-done((bf16[616,384]{1,0:T(8,128)(2,1)S(1)}, bf16[616,384]{1,0:T(8,128)(2,1)S(1)}, u32[]{:S(2)}, u32[]{:S(2)}) %collective-permute-start.6) | collective-permute-done | bytes 473120 | tf_op jit(solution)/shard_map/ppermute | solution.py:40
  110.6 4.3 %shard_map.123 = (f32[12,512,128]{2,1,0:T(8,128)S(1)}, bf16[3,512,384]{2,1,0:T(8,128)(2,1)S(1)}) custom-call(s32[24]{0:T(128)S(1)} %reshape.354.meta_ref, bf16[616,384]{1,0:T(8,128)(2,1)S(1)} %collective-permute-done.5.refs_0_.refs_4_, bf16[616,384]{1,0:T(8,128)(2,1)S(1)} %collective-permute-done.6.refs_1_.refs_5_, ...), custom_call_target="tpu_custom_call" | custom-call | tf_op jit(solution)/shard_map/pallas_call | solution.py:111
  122.8 9.2 %convolution_convert_fusion = bf16[256,4608]{1,0:T(8,128)(2,1)S(1)} fusion(bf16[1536,4608]{1,0:T(8,128)(2,1)} %constant_dynamic-update-slice_fusion, bf16[2,256,1536]{2,1,0:T(8,128)(2,1)S(1)} %bitcast.155, s32[]{:T(128)S(6)} %select_n.115), kind=kOutput, calls=%fused_computation.2 | convolution fusion | flops 3625058304 | bytes 17301508 | tf_op jit(solution)/shard_map/dot_general | solution.py:389
  137.8 7.1 %fusion = f32[2,128,4608]{2,1,0:T(8,128)S(1)} fusion(bf16[2,128,1536]{2,1,0:T(8,128)(2,1)S(1)} %bitcast.204, bf16[1536,4608]{1,0:T(8,128)(2,1)} %constant_dynamic-update-slice_fusion), kind=kOutput, calls=%fused_computation | convolution fusion | flops 3623878656 | bytes 19660800 | tf_op jit(solution)/shard_map/dot_general | solution.py:392
  154.2 4.6 %collective-permute-start.12 = (bf16[128,4608]{1,0:T(8,128)(2,1)}, bf16[128,4608]{1,0:T(8,128)(2,1)S(1)}, u32[]{:S(2)}, u32[]{:S(2)}) collective-permute-start(bf16[128,4608]{1,0:T(8,128)(2,1)} %get-tuple-element.52), channel_id=1, source_target_pairs={{0,16},{1,17},{2,18},{3,19},{4,20},{5,21},{6,22},{7,23},{8,9},{9,8... | collective-permute-start | bytes 3538952 | tf_op jit(solution)/shard_map/ppermute | solution.py:40
  165.0 13.5 %shard_map.125 = f32[512,640]{1,0:T(8,128)S(1)} custom-call(s32[24]{0:T(128)S(1)} %reshape.354.meta_ref, bf16[616,384]{1,0:T(8,128)(2,1)S(1)} %copy-done.6, bf16[616,384]{1,0:T(8,128)(2,1)S(1)} %copy-done.8, bf16[616,384]{1,0:T(8,128)(2,1)S(1)} %copy-done.10, bf16[616,384]{1,0:T(8,128)(2,1)} %collective-permute-done.10.refs_3_, ...), custom_call_target="tpu_custom_call" | custom-call | tf_op jit(solution)/shard_map/pallas_call | solution.py:111
  178.6 11.6 %collective-permute-start.13 = (bf16[256,640]{1,0:T(8,128)(2,1)S(1)}, bf16[256,640]{1,0:T(8,128)(2,1)S(1)}, u32[]{:S(2)}, u32[]{:S(2)}) collective-permute-start(bf16[256,640]{1,0:T(8,128)(2,1)S(1)} %fusion.37), channel_id=1, source_target_pairs={{0,8},{1,9},{2,10},{3,11},{4,12},{5,13},{6,14},{7,15},{8,0},{9,1},... | collective-permute-start | bytes 983048 | tf_op jit(solution)/shard_map/ppermute | solution.py:40
  197.2 3.8 %collective-permute-start.16 = (bf16[64,640]{1,0:T(8,128)(2,1)S(1)}, bf16[64,640]{1,0:T(8,128)(2,1)S(1)}, u32[]{:S(2)}, u32[]{:S(2)}) collective-permute-start(bf16[64,640]{1,0:T(8,128)(2,1)S(1)} %get-tuple-element.110), channel_id=1, source_target_pairs={{0,1},{1,0},{2,3},{3,2},{4,5},{5,4},{6,7},{7,6},{8,24},{9,25},{10,... | collective-permute-start | bytes 245768 | tf_op jit(solution)/shard_map/ppermute | solution.py:40
  207.7 7.2 %collective-permute-done.17 = bf16[32,5248]{1,0:T(8,128)(2,1)S(1)} collective-permute-done((bf16[32,5248]{1,0:T(8,128)(2,1)S(1)}, bf16[32,5248]{1,0:T(8,128)(2,1)S(1)}, u32[]{:S(2)}, u32[]{:S(2)}) %collective-permute-start.17) | collective-permute-done | bytes 335904 | tf_op jit(solution)/shard_map/ppermute | solution.py:40
  215.0 3.6 %collective-permute-start.18 = (bf16[16,5248]{1,0:T(8,128)(2,1)S(1)}, bf16[16,5248]{1,0:T(8,128)(2,1)S(1)}, u32[]{:S(2)}, u32[]{:S(2)}) collective-permute-start(bf16[16,5248]{1,0:T(8,128)(2,1)S(1)} %fusion.38), channel_id=1, source_target_pairs={{0,6},{1,7},{2,4},{3,5},{4,2},{5,3},{6,0},{7,1},{8,14},{9,15},{10,... | collective-permute-start | bytes 503816 | tf_op jit(solution)/shard_map/ppermute | solution.py:40
  219.7 3.5 %collective-permute-done.18 = bf16[16,5248]{1,0:T(8,128)(2,1)S(1)} collective-permute-done((bf16[16,5248]{1,0:T(8,128)(2,1)S(1)}, bf16[16,5248]{1,0:T(8,128)(2,1)S(1)}, u32[]{:S(2)}, u32[]{:S(2)}) %collective-permute-start.18) | collective-permute-done | bytes 167968 | tf_op jit(solution)/shard_map/ppermute | solution.py:40
  223.3 3.6 %collective-permute-start.19 = (bf16[16,5248]{1,0:T(8,128)(2,1)S(1)}, bf16[16,5248]{1,0:T(8,128)(2,1)S(1)}, u32[]{:S(2)}, u32[]{:S(2)}) collective-permute-start(bf16[16,5248]{1,0:T(8,128)(2,1)S(1)} %fusion.36), channel_id=1, source_target_pairs={{0,6},{1,7},{2,4},{3,5},{4,2},{5,3},{6,0},{7,1},{8,14},{9,15},{10,... | collective-permute-start | bytes 503816 | tf_op jit(solution)/shard_map/ppermute | solution.py:40
  230.7 4.3 %collective-permute-start.20 = (bf16[32,5248]{1,0:T(8,128)(2,1)S(1)}, bf16[32,5248]{1,0:T(8,128)(2,1)S(1)}, u32[]{:S(2)}, u32[]{:S(2)}) collective-permute-start(bf16[32,5248]{1,0:T(8,128)(2,1)S(1)} %maximum_select_fusion.2), channel_id=1, source_target_pairs={{0,2},{1,3},{2,0},{3,1},{4,6},{5,7},{6,4},{7,5},{8,10},{9,11},{10,... | collective-permute-start | bytes 1007624 | tf_op jit(solution)/shard_map/ppermute | solution.py:40
  236.0 7.1 %collective-permute-done.20 = bf16[32,5248]{1,0:T(8,128)(2,1)S(1)} collective-permute-done((bf16[32,5248]{1,0:T(8,128)(2,1)S(1)}, bf16[32,5248]{1,0:T(8,128)(2,1)S(1)}, u32[]{:S(2)}, u32[]{:S(2)}) %collective-permute-start.20) | collective-permute-done | bytes 335904 | tf_op jit(solution)/shard_map/ppermute | solution.py:40
  247.4 6.6 %collective-permute-done.21 = bf16[64,5248]{1,0:T(8,128)(2,1)S(1)} collective-permute-done((bf16[64,5248]{1,0:T(8,128)(2,1)S(1)}, bf16[64,5248]{1,0:T(8,128)(2,1)S(1)}, u32[]{:S(2)}, u32[]{:S(2)}) %collective-permute-start.21) | collective-permute-done | bytes 671776 | tf_op jit(solution)/shard_map/ppermute | solution.py:40
  254.4 17.9 %collective-permute-done.26.piece.small = bf16[128,5248]{1,0:T(8,128)(2,1)S(1)} collective-permute-done((bf16[128,5248]{1,0:T(8,128)(2,1)S(1)}, bf16[128,5248]{1,0:T(8,128)(2,1)S(1)}, u32[]{:S(2)}, u32[]{:S(2)}) %collective-permute-start.26) | collective-permute-done | bytes 1343520 | tf_op jit(solution)/shard_map/ppermute | solution.py:40
  279.1 3.5 %shard_map.129 = (f32[9,512,512]{2,1,0:T(8,128)}, f32[616,512]{1,0:T(8,128)}, f32[1,512]{1,0:T(1,128)}) custom-call(s32[1]{0:T(128)} %bitcast.85.at, bf16[128,5248]{1,0:T(8,128)(2,1)} %collective-permute-done.27.piece.small, bf16[128,5248]{1,0:T(8,128)(2,1)} %collective-permute-done.27.piece.small, ...), custom_call_target="tpu_custom_call", output_to_operand_aliasing={{0}: (3, {}), {1}: (4, {}), {2}: (5, {})} | custom-call | tf_op jit(solution)/shard_map/pallas_call | solution.py:111
  (212 shorter events, 109.6 us)
Async XLA Ops:
  4.1 35.1 %all-to-all-start = ((s32[8,1,3]{2,1,0:T(1,128)}), s32[8,1,3]{2,1,0:T(1,128)S(1)}, u32[]{:S(2)}, u32[]{:S(2)}) async-start(s32[8,1,3]{2,1,0:T(1,128)} %copy.81), calls=%async_computation | async-start | bytes 8192 | tf_op jit(solution)/shard_map/all_to_all | solution.py:350
  13.1 26.5 %collective-permute-start.1 = (bf16[24,1,512]{2,1,0:T(2,128)(2,1)}, bf16[24,1,512]{2,1,0:T(2,128)(2,1)}, u32[]{:S(2)}, u32[]{:S(2)}) collective-permute-start(bf16[24,1,512]{2,1,0:T(2,128)(2,1)} %get-tuple-element.107), channel_id=1, source_target_pairs={{1,0},{2,1},{3,2},{4,3},{5,4},{6,5},{7,6},{0,7},{9,8},{10,9},{11,1... | collective-permute-start | bytes 73736 | tf_op jit(solution)/shard_map/ppermute | solution.py:89
  17.8 21.8 %collective-permute-start = (bf16[24,1,512]{2,1,0:T(2,128)(2,1)}, bf16[24,1,512]{2,1,0:T(2,128)(2,1)}, u32[]{:S(2)}, u32[]{:S(2)}) collective-permute-start(bf16[24,1,512]{2,1,0:T(2,128)(2,1)} %get-tuple-element.106), channel_id=1, source_target_pairs={{0,1},{1,2},{2,3},{3,4},{4,5},{5,6},{6,7},{7,0},{8,9},{9,10},{10,1... | collective-permute-start | bytes 73736 | tf_op jit(solution)/shard_map/ppermute | solution.py:88
  22.4 46.4 %collective-permute-start.8 = (bf16[616,384]{1,0:T(8,128)(2,1)}, bf16[616,384]{1,0:T(8,128)(2,1)S(1)}, u32[]{:S(2)}, u32[]{:S(2)}) collective-permute-start(bf16[616,384]{1,0:T(8,128)(2,1)} %get-tuple-element.44), channel_id=1, source_target_pairs={{0,1},{1,0},{2,3},{3,2},{4,5},{5,4},{6,7},{7,6},{8,9},{9,8},{10,11... | collective-permute-start | bytes 1419272 | tf_op jit(solution)/shard_map/ppermute | solution.py:40
  22.7 50.2 %collective-permute-start.9 = (bf16[616,384]{1,0:T(8,128)(2,1)}, bf16[616,384]{1,0:T(8,128)(2,1)S(1)}, u32[]{:S(2)}, u32[]{:S(2)}) collective-permute-start(bf16[616,384]{1,0:T(8,128)(2,1)} %get-tuple-element.45), channel_id=1, source_target_pairs={{0,2},{1,3},{2,0},{3,1},{4,6},{5,7},{6,4},{7,5},{8,10},{9,11},{10,... | collective-permute-start | bytes 1419272 | tf_op jit(solution)/shard_map/ppermute | solution.py:40
  24.1 62.2 %collective-permute-start.10 = (bf16[616,384]{1,0:T(8,128)(2,1)}, bf16[616,384]{1,0:T(8,128)(2,1)}, u32[]{:S(2)}, u32[]{:S(2)}) collective-permute-start(bf16[616,384]{1,0:T(8,128)(2,1)} %get-tuple-element.46), channel_id=1, source_target_pairs={{0,3},{1,2},{2,1},{3,0},{4,7},{5,6},{6,5},{7,4},{8,11},{9,10},{10,... | collective-permute-start | bytes 1419272 | tf_op jit(solution)/shard_map/ppermute | solution.py:40
  46.5 54.6 %collective-permute-start.5 = (bf16[616,384]{1,0:T(8,128)(2,1)S(1)}, bf16[616,384]{1,0:T(8,128)(2,1)S(1)}, u32[]{:S(2)}, u32[]{:S(2)}) collective-permute-start(bf16[616,384]{1,0:T(8,128)(2,1)S(1)} %copy-done.32), channel_id=1, source_target_pairs={{0,4},{1,5},{2,6},{3,7},{4,0},{5,1},{6,2},{7,3},{8,12},{9,13},{10,... | collective-permute-start | bytes 1419272 | tf_op jit(solution)/shard_map/ppermute | solution.py:40
  48.9 61.7 %collective-permute-start.6 = (bf16[616,384]{1,0:T(8,128)(2,1)S(1)}, bf16[616,384]{1,0:T(8,128)(2,1)S(1)}, u32[]{:S(2)}, u32[]{:S(2)}) collective-permute-start(bf16[616,384]{1,0:T(8,128)(2,1)S(1)} %copy-done.30), channel_id=1, source_target_pairs={{0,5},{1,4},{2,7},{3,6},{4,1},{5,0},{6,3},{7,2},{8,13},{9,12},{10,... | collective-permute-start | bytes 1419272 | tf_op jit(solution)/shard_map/ppermute | solution.py:40
  68.8 41.8 %collective-permute-start.7 = (bf16[616,384]{1,0:T(8,128)(2,1)S(1)}, bf16[616,384]{1,0:T(8,128)(2,1)S(1)}, u32[]{:S(2)}, u32[]{:S(2)}) collective-permute-start(bf16[616,384]{1,0:T(8,128)(2,1)S(1)} %copy-done.28), channel_id=1, source_target_pairs={{0,6},{1,7},{2,4},{3,5},{4,2},{5,3},{6,0},{7,1},{8,14},{9,15},{10,... | collective-permute-start | bytes 1419272 | tf_op jit(solution)/shard_map/ppermute | solution.py:40
  72.9 43.1 %collective-permute-start.4 = (bf16[616,384]{1,0:T(8,128)(2,1)S(1)}, bf16[616,384]{1,0:T(8,128)(2,1)S(1)}, u32[]{:S(2)}, u32[]{:S(2)}) collective-permute-start(bf16[616,384]{1,0:T(8,128)(2,1)S(1)} %copy-done.26), channel_id=1, source_target_pairs={{0,7},{1,6},{2,5},{3,4},{4,3},{5,2},{6,1},{7,0},{8,15},{9,14},{10,... | collective-permute-start | bytes 1419272 | tf_op jit(solution)/shard_map/ppermute | solution.py:40
  132.0 20.5 %collective-permute-start.11 = (bf16[256,4608]{1,0:T(8,128)(2,1)S(1)}, bf16[256,4608]{1,0:T(8,128)(2,1)S(1)}, u32[]{:S(2)}, u32[]{:S(2)}) collective-permute-start(bf16[256,4608]{1,0:T(8,128)(2,1)S(1)} %convolution_convert_fusion), channel_id=1, source_target_pairs={{0,8},{1,9},{2,10},{3,11},{4,12},{5,13},{6,14},{7,15},{8,0},{9,1},... | collective-permute-start | bytes 7077896 | tf_op jit(solution)/shard_map/ppermute | solution.py:40
  135.3 10.7 %collective-permute-start.23 = (bf16[24,1,512]{2,1,0:T(2,128)(2,1)S(1)}, bf16[24,1,512]{2,1,0:T(2,128)(2,1)S(1)}, u32[]{:S(2)}, u32[]{:S(2)}) collective-permute-start(bf16[24,1,512]{2,1,0:T(2,128)(2,1)S(1)} %get-tuple-element.103), channel_id=1, source_target_pairs={{1,0},{2,1},{3,2},{4,3},{5,4},{6,5},{7,6},{0,7},{9,8},{10,9},{11,1... | collective-permute-start | bytes 73736 | tf_op jit(solution)/shard_map/ppermute | solution.py:89
  137.8 8.2 %collective-permute-start.22 = (bf16[24,1,512]{2,1,0:T(2,128)(2,1)S(1)}, bf16[24,1,512]{2,1,0:T(2,128)(2,1)S(1)}, u32[]{:S(2)}, u32[]{:S(2)}) collective-permute-start(bf16[24,1,512]{2,1,0:T(2,128)(2,1)S(1)} %get-tuple-element.102), channel_id=1, source_target_pairs={{0,1},{1,2},{2,3},{3,4},{4,5},{5,6},{6,7},{7,0},{8,9},{9,10},{10,1... | collective-permute-start | bytes 73736 | tf_op jit(solution)/shard_map/ppermute | solution.py:88
  146.1 12.8 %collective-permute-start.24 = (bf16[1,66,512]{2,1,0:T(8,128)(2,1)S(1)}, bf16[1,66,512]{2,1,0:T(8,128)(2,1)S(1)}, u32[]{:S(2)}, u32[]{:S(2)}) collective-permute-start(bf16[1,66,512]{2,1,0:T(8,128)(2,1)S(1)} %get-tuple-element.94), channel_id=1, source_target_pairs={{0,8},{8,16},{16,24},{1,9},{9,17},{17,25},{2,10},{10,18},{18,26},{... | collective-permute-start | bytes 202760 | tf_op jit(solution)/shard_map/ppermute | solution.py:88
  148.1 10.7 %collective-permute-start.25 = (bf16[1,66,512]{2,1,0:T(8,128)(2,1)S(1)}, bf16[1,66,512]{2,1,0:T(8,128)(2,1)S(1)}, u32[]{:S(2)}, u32[]{:S(2)}) collective-permute-start(bf16[1,66,512]{2,1,0:T(8,128)(2,1)S(1)} %get-tuple-element.95), channel_id=1, source_target_pairs={{8,0},{16,8},{24,16},{9,1},{17,9},{25,17},{10,2},{18,10},{26,18},{... | collective-permute-start | bytes 202760 | tf_op jit(solution)/shard_map/ppermute | solution.py:89
  154.2 38.0 %collective-permute-start.12 = (bf16[128,4608]{1,0:T(8,128)(2,1)}, bf16[128,4608]{1,0:T(8,128)(2,1)S(1)}, u32[]{:S(2)}, u32[]{:S(2)}) collective-permute-start(bf16[128,4608]{1,0:T(8,128)(2,1)} %get-tuple-element.52), channel_id=1, source_target_pairs={{0,16},{1,17},{2,18},{3,19},{4,20},{5,21},{6,22},{7,23},{8,9},{9,8... | collective-permute-start | bytes 3538952 | tf_op jit(solution)/shard_map/ppermute | solution.py:40
  178.6 12.8 %collective-permute-start.13 = (bf16[256,640]{1,0:T(8,128)(2,1)S(1)}, bf16[256,640]{1,0:T(8,128)(2,1)S(1)}, u32[]{:S(2)}, u32[]{:S(2)}) collective-permute-start(bf16[256,640]{1,0:T(8,128)(2,1)S(1)} %fusion.37), channel_id=1, source_target_pairs={{0,8},{1,9},{2,10},{3,11},{4,12},{5,13},{6,14},{7,15},{8,0},{9,1},... | collective-permute-start | bytes 983048 | tf_op jit(solution)/shard_map/ppermute | solution.py:40
  192.3 11.4 %collective-permute-start.15 = (bf16[64,4608]{1,0:T(8,128)(2,1)S(1)}, bf16[64,4608]{1,0:T(8,128)(2,1)S(1)}, u32[]{:S(2)}, u32[]{:S(2)}) collective-permute-start(bf16[64,4608]{1,0:T(8,128)(2,1)S(1)} %get-tuple-element.76), channel_id=1, source_target_pairs={{0,1},{1,0},{2,3},{3,2},{4,5},{5,4},{6,7},{7,6},{8,24},{9,25},{10,... | collective-permute-start | bytes 1769480 | tf_op jit(solution)/shard_map/ppermute | solution.py:40
  204.0 11.0 %collective-permute-start.17 = (bf16[32,5248]{1,0:T(8,128)(2,1)S(1)}, bf16[32,5248]{1,0:T(8,128)(2,1)S(1)}, u32[]{:S(2)}, u32[]{:S(2)}) collective-permute-start(bf16[32,5248]{1,0:T(8,128)(2,1)S(1)} %get-tuple-element.78), channel_id=1, source_target_pairs={{0,2},{1,3},{2,0},{3,1},{4,6},{5,7},{6,4},{7,5},{8,10},{9,11},{10,... | collective-permute-start | bytes 1007624 | tf_op jit(solution)/shard_map/ppermute | solution.py:40
  215.0 8.2 %collective-permute-start.18 = (bf16[16,5248]{1,0:T(8,128)(2,1)S(1)}, bf16[16,5248]{1,0:T(8,128)(2,1)S(1)}, u32[]{:S(2)}, u32[]{:S(2)}) collective-permute-start(bf16[16,5248]{1,0:T(8,128)(2,1)S(1)} %fusion.38), channel_id=1, source_target_pairs={{0,6},{1,7},{2,4},{3,5},{4,2},{5,3},{6,0},{7,1},{8,14},{9,15},{10,... | collective-permute-start | bytes 503816 | tf_op jit(solution)/shard_map/ppermute | solution.py:40
  230.7 12.4 %collective-permute-start.20 = (bf16[32,5248]{1,0:T(8,128)(2,1)S(1)}, bf16[32,5248]{1,0:T(8,128)(2,1)S(1)}, u32[]{:S(2)}, u32[]{:S(2)}) collective-permute-start(bf16[32,5248]{1,0:T(8,128)(2,1)S(1)} %maximum_select_fusion.2), channel_id=1, source_target_pairs={{0,2},{1,3},{2,0},{3,1},{4,6},{5,7},{6,4},{7,5},{8,10},{9,11},{10,... | collective-permute-start | bytes 1007624 | tf_op jit(solution)/shard_map/ppermute | solution.py:40
  243.2 10.8 %collective-permute-start.21 = (bf16[64,5248]{1,0:T(8,128)(2,1)S(1)}, bf16[64,5248]{1,0:T(8,128)(2,1)S(1)}, u32[]{:S(2)}, u32[]{:S(2)}) collective-permute-start(bf16[64,5248]{1,0:T(8,128)(2,1)S(1)} %maximum_select_fusion.1), channel_id=1, source_target_pairs={{0,1},{1,0},{2,3},{3,2},{4,5},{5,4},{6,7},{7,6},{8,24},{9,25},{10,... | collective-permute-start | bytes 2015240 | tf_op jit(solution)/shard_map/ppermute | solution.py:40
  254.2 18.0 %collective-permute-start.26 = (bf16[128,5248]{1,0:T(8,128)(2,1)S(1)}, bf16[128,5248]{1,0:T(8,128)(2,1)S(1)}, u32[]{:S(2)}, u32[]{:S(2)}) collective-permute-start(bf16[128,5248]{1,0:T(8,128)(2,1)S(1)} %maximum_select_fusion.piece.small), channel_id=1, source_target_pairs={{0,16},{1,17},{2,18},{3,19},{4,20},{5,21},{6,22},{7,23},{8,9},{9,8... | collective-permute-start | bytes 4030472 | tf_op jit(solution)/shard_map/ppermute | solution.py:40
  254.3 19.7 %collective-permute-start.28 = (bf16[128,5248]{1,0:T(8,128)(2,1)S(1)}, bf16[128,5248]{1,0:T(8,128)(2,1)}, u32[]{:S(2)}, u32[]{:S(2)}) collective-permute-start(bf16[128,5248]{1,0:T(8,128)(2,1)S(1)} %maximum_select_fusion.piece.small), channel_id=1, source_target_pairs={{0,8},{1,9},{2,10},{3,11},{4,12},{5,13},{6,14},{7,15},{8,0},{9,1},... | collective-permute-start | bytes 4030472 | tf_op jit(solution)/shard_map/ppermute | solution.py:40
  (49 other events, 315.7 us)

commit v3 on v2

--- a/solution.py
+++ b/solution.py
@@ -89,11 +89,6 @@
         after = lax.ppermute(leading, axis, down)
         shard = jnp.concatenate([before, shard, after], axis=dim)
     return shard
-
-
-def widen(field):
-    beside_all = padded_2(field, (("lon", 1),), 1, True)
-    return padded_2(beside_all, (("lat", 0),), 1, False)
 
 
 def to_patches(tile):
@@ -395,9 +390,8 @@
     away, keep = split_sum(keep, came, halves[1])
     away, spread = lax.optimization_barrier((away, spread))
     came = step(away, plan[1][0], lats, lons)
-    small = backward(
-        meta, arrived, kernels.transpose(0, 2, 1), gain_col, spread, slopes, d_normed_t
-    )
+    kernels_t = kernels.transpose(0, 2, 1)
+    small = backward(meta, arrived, kernels_t, gain_col, spread, slopes, d_normed_t)
     small_keep = pick(small, core)
     small_came = step(pick(small, 1 - core).astype(jnp.bfloat16), plan[0][0], lats, lons)
 
@@ -416,7 +410,8 @@
         came = step(away, plan[n][0], lats, lons)
     normed = normed_t.reshape(width, tile_rows // PH, tile_cols // PW, PH, PW)
     normed = normed.transpose(1, 3, 2, 4, 0).reshape(tile_rows, tile_cols, width)
-    padded = widen(normed)
+    padded = padded_2(normed, (("lon", 1),), 1, True)
+    padded = padded_2(padded, (("lat", 0),), 1, False)
     result_sum = jnp.zeros((cells, width), jnp.float32)
     for a in range(3):
         for b in range(3):

time: 287 us -> 287 us (level)
  no operation moved by 1% of the time
where the time goes in v3:
time: 287 us; the launch traced here: 283 us
  starting transfers between devices  73.2 us (26%)
  waiting for transfers between devices  66.7 us (23%)
  local copies, waits for them, and re-layouts  44.4 us (15%)
  Pallas kernels  41.1 us (14%)
  matrix products  39.9 us (14%)
  other arithmetic  16 us (6%)
    ppermute x21, waiting for transfers between devices, exchange(): return lax.ppermute(value, AXES, pairs)  66.6 us
    ppermute x21, starting transfers between devices, exchange(): return lax.ppermute(value, AXES, pairs)  52.1 us
    pallas_call x10, Pallas kernels, call(): pl.pallas_call(body, out_shape=outs, grid_spec=pltpu.PrefetchScalarGridSp...  41.1 us
    unnamed x97, local copies, waits for them, and re-layouts  28 us
    dot_general x1, matrix products, nt(): lax.dot_general(left, right, (((1,), (1,)), ((), ())), preferred_element_...  13.4 us
    concatenate x5, other arithmetic, padded_2(): shard = jnp.concatenate([before, shard, after], axis=dim)  10.6 us
    ppermute x4, starting transfers between devices, padded_2(): after = lax.ppermute(leading, axis, down)  10.4 us
    dot_general x9, matrix products, shards(): jnp.dot(window, conv_weight[a, b], preferred_element_type=jnp.float32)  10.2 us
  transfers between devices with their start and end apart: 30, of which 11 were waited for; matrix products, arithmetic and copies ran while one was open for 27% of the time, Pallas kernels for 12%

profile of v3, /device:TPU:0, one launch (start us, length us, event | category | flops | bytes accessed | tf_op | source)
XLA Modules:
  0.0 282.8 jit_solution(10981608408332592033)
XLA Ops:
  4.1 7.3 %all-to-all-start = ((s32[8,1,3]{2,1,0:T(1,128)}), s32[8,1,3]{2,1,0:T(1,128)S(1)}, u32[]{:S(2)}, u32[]{:S(2)}) async-start(s32[8,1,3]{2,1,0:T(1,128)} %copy.81), calls=%async_computation | async-start | bytes 8192 | tf_op jit(solution)/shard_map/all_to_all | solution.py:345
  13.1 4.7 %collective-permute-start.1 = (bf16[24,1,512]{2,1,0:T(2,128)(2,1)}, bf16[24,1,512]{2,1,0:T(2,128)(2,1)}, u32[]{:S(2)}, u32[]{:S(2)}) collective-permute-start(bf16[24,1,512]{2,1,0:T(2,128)(2,1)} %get-tuple-element.107), channel_id=1, source_target_pairs={{1,0},{2,1},{3,2},{4,3},{5,4},{6,5},{7,6},{0,7},{9,8},{10,9},{11,1... | collective-permute-start | bytes 73736 | tf_op jit(solution)/shard_map/ppermute | solution.py:89
  31.2 6.7 %copy.93 = bf16[3,3,512,512]{2,3,1,0:T(8,128)(2,1)} copy(bf16[3,3,512,512]{3,2,1,0:T(8,128)(2,1)} %param.16) | data formatting | bytes 9437184 | tf_op args[7]
  68.8 4.1 %collective-permute-start.7 = (bf16[616,384]{1,0:T(8,128)(2,1)S(1)}, bf16[616,384]{1,0:T(8,128)(2,1)S(1)}, u32[]{:S(2)}, u32[]{:S(2)}) collective-permute-start(bf16[616,384]{1,0:T(8,128)(2,1)S(1)} %copy-done.28), channel_id=1, source_target_pairs={{0,6},{1,7},{2,4},{3,5},{4,2},{5,3},{6,0},{7,1},{8,14},{9,15},{10,... | collective-permute-start | bytes 1419272 | tf_op jit(solution)/shard_map/ppermute | solution.py:40
  72.9 13.4 %convolution_bitcast_fusion.refs_14_ = f32[512,1536]{1,0:T(8,128)} fusion(bf16[1536,4608]{1,0:T(8,128)(2,1)} %constant_dynamic-update-slice_fusion, bf16[512,4608]{0,1:T(8,128)(2,1)} %bitcast.194), kind=kOutput, calls=%fused_computation.11 | convolution fusion | flops 7247757312 | bytes 22020096 | tf_op jit(solution)/shard_map/dot_general | solution.py:126
  86.3 6.6 %shard_map.122 = (f32[12,512,128]{2,1,0:T(8,128)S(1)}, bf16[4,512,384]{2,1,0:T(8,128)(2,1)S(1)}) custom-call(s32[24]{0:T(128)S(1)} %reshape.354.meta_ref, bf16[616,384]{1,0:T(8,128)(2,1)S(1)} %get-tuple-element.43.refs_0_, bf16[616,384]{1,0:T(8,128)(2,1)S(1)} %collective-permute-done.8.refs_1_, bf16[616,384]{1,0:T(8,128)(2,1)S(1)} %collective-permute-done.9.refs_2_, ...), custom_call_target="tpu_custom_call" | custom-call | tf_op jit(solution)/shard_map/pallas_call | solution.py:106
  93.0 8.2 %collective-permute-done.5.refs_0_.refs_4_ = bf16[616,384]{1,0:T(8,128)(2,1)S(1)} collective-permute-done((bf16[616,384]{1,0:T(8,128)(2,1)S(1)}, bf16[616,384]{1,0:T(8,128)(2,1)S(1)}, u32[]{:S(2)}, u32[]{:S(2)}) %collective-permute-start.5) | collective-permute-done | bytes 473120 | tf_op jit(solution)/shard_map/ppermute | solution.py:40
  101.2 9.4 %collective-permute-done.6.refs_1_.refs_5_ = bf16[616,384]{1,0:T(8,128)(2,1)S(1)} collective-permute-done((bf16[616,384]{1,0:T(8,128)(2,1)S(1)}, bf16[616,384]{1,0:T(8,128)(2,1)S(1)}, u32[]{:S(2)}, u32[]{:S(2)}) %collective-permute-start.6) | collective-permute-done | bytes 473120 | tf_op jit(solution)/shard_map/ppermute | solution.py:40
  110.6 4.3 %shard_map.123 = (f32[12,512,128]{2,1,0:T(8,128)S(1)}, bf16[3,512,384]{2,1,0:T(8,128)(2,1)S(1)}) custom-call(s32[24]{0:T(128)S(1)} %reshape.354.meta_ref, bf16[616,384]{1,0:T(8,128)(2,1)S(1)} %collective-permute-done.5.refs_0_.refs_4_, bf16[616,384]{1,0:T(8,128)(2,1)S(1)} %collective-permute-done.6.refs_1_.refs_5_, ...), custom_call_target="tpu_custom_call" | custom-call | tf_op jit(solution)/shard_map/pallas_call | solution.py:106
  122.8 9.2 %convolution_convert_fusion = bf16[256,4608]{1,0:T(8,128)(2,1)S(1)} fusion(bf16[1536,4608]{1,0:T(8,128)(2,1)} %constant_dynamic-update-slice_fusion, bf16[2,256,1536]{2,1,0:T(8,128)(2,1)S(1)} %bitcast.155, s32[]{:T(128)S(6)} %select_n.115), kind=kOutput, calls=%fused_computation.2 | convolution fusion | flops 3625058304 | bytes 17301508 | tf_op jit(solution)/shard_map/dot_general | solution.py:384
  137.8 7.1 %fusion = f32[2,128,4608]{2,1,0:T(8,128)S(1)} fusion(bf16[2,128,1536]{2,1,0:T(8,128)(2,1)S(1)} %bitcast.204, bf16[1536,4608]{1,0:T(8,128)(2,1)} %constant_dynamic-update-slice_fusion), kind=kOutput, calls=%fused_computation | convolution fusion | flops 3623878656 | bytes 19660800 | tf_op jit(solution)/shard_map/dot_general | solution.py:387
  154.2 4.6 %collective-permute-start.12 = (bf16[128,4608]{1,0:T(8,128)(2,1)}, bf16[128,4608]{1,0:T(8,128)(2,1)S(1)}, u32[]{:S(2)}, u32[]{:S(2)}) collective-permute-start(bf16[128,4608]{1,0:T(8,128)(2,1)} %get-tuple-element.52), channel_id=1, source_target_pairs={{0,16},{1,17},{2,18},{3,19},{4,20},{5,21},{6,22},{7,23},{8,9},{9,8... | collective-permute-start | bytes 3538952 | tf_op jit(solution)/shard_map/ppermute | solution.py:40
  165.0 13.5 %shard_map.125 = f32[512,640]{1,0:T(8,128)S(1)} custom-call(s32[24]{0:T(128)S(1)} %reshape.354.meta_ref, bf16[616,384]{1,0:T(8,128)(2,1)S(1)} %copy-done.6, bf16[616,384]{1,0:T(8,128)(2,1)S(1)} %copy-done.8, bf16[616,384]{1,0:T(8,128)(2,1)S(1)} %copy-done.10, bf16[616,384]{1,0:T(8,128)(2,1)} %collective-permute-done.10.refs_3_, ...), custom_call_target="tpu_custom_call" | custom-call | tf_op jit(solution)/shard_map/pallas_call | solution.py:106
  178.6 11.6 %collective-permute-start.13 = (bf16[256,640]{1,0:T(8,128)(2,1)S(1)}, bf16[256,640]{1,0:T(8,128)(2,1)S(1)}, u32[]{:S(2)}, u32[]{:S(2)}) collective-permute-start(bf16[256,640]{1,0:T(8,128)(2,1)S(1)} %fusion.37), channel_id=1, source_target_pairs={{0,8},{1,9},{2,10},{3,11},{4,12},{5,13},{6,14},{7,15},{8,0},{9,1},... | collective-permute-start | bytes 983048 | tf_op jit(solution)/shard_map/ppermute | solution.py:40
  197.2 3.8 %collective-permute-start.16 = (bf16[64,640]{1,0:T(8,128)(2,1)S(1)}, bf16[64,640]{1,0:T(8,128)(2,1)S(1)}, u32[]{:S(2)}, u32[]{:S(2)}) collective-permute-start(bf16[64,640]{1,0:T(8,128)(2,1)S(1)} %get-tuple-element.110), channel_id=1, source_target_pairs={{0,1},{1,0},{2,3},{3,2},{4,5},{5,4},{6,7},{7,6},{8,24},{9,25},{10,... | collective-permute-start | bytes 245768 | tf_op jit(solution)/shard_map/ppermute | solution.py:40
  207.7 7.2 %collective-permute-done.17 = bf16[32,5248]{1,0:T(8,128)(2,1)S(1)} collective-permute-done((bf16[32,5248]{1,0:T(8,128)(2,1)S(1)}, bf16[32,5248]{1,0:T(8,128)(2,1)S(1)}, u32[]{:S(2)}, u32[]{:S(2)}) %collective-permute-start.17) | collective-permute-done | bytes 335904 | tf_op jit(solution)/shard_map/ppermute | solution.py:40
  215.0 3.6 %collective-permute-start.18 = (bf16[16,5248]{1,0:T(8,128)(2,1)S(1)}, bf16[16,5248]{1,0:T(8,128)(2,1)S(1)}, u32[]{:S(2)}, u32[]{:S(2)}) collective-permute-start(bf16[16,5248]{1,0:T(8,128)(2,1)S(1)} %fusion.38), channel_id=1, source_target_pairs={{0,6},{1,7},{2,4},{3,5},{4,2},{5,3},{6,0},{7,1},{8,14},{9,15},{10,... | collective-permute-start | bytes 503816 | tf_op jit(solution)/shard_map/ppermute | solution.py:40
  219.7 3.5 %collective-permute-done.18 = bf16[16,5248]{1,0:T(8,128)(2,1)S(1)} collective-permute-done((bf16[16,5248]{1,0:T(8,128)(2,1)S(1)}, bf16[16,5248]{1,0:T(8,128)(2,1)S(1)}, u32[]{:S(2)}, u32[]{:S(2)}) %collective-permute-start.18) | collective-permute-done | bytes 167968 | tf_op jit(solution)/shard_map/ppermute | solution.py:40
  223.3 3.6 %collective-permute-start.19 = (bf16[16,5248]{1,0:T(8,128)(2,1)S(1)}, bf16[16,5248]{1,0:T(8,128)(2,1)S(1)}, u32[]{:S(2)}, u32[]{:S(2)}) collective-permute-start(bf16[16,5248]{1,0:T(8,128)(2,1)S(1)} %fusion.36), channel_id=1, source_target_pairs={{0,6},{1,7},{2,4},{3,5},{4,2},{5,3},{6,0},{7,1},{8,14},{9,15},{10,... | collective-permute-start | bytes 503816 | tf_op jit(solution)/shard_map/ppermute | solution.py:40
  230.7 4.3 %collective-permute-start.20 = (bf16[32,5248]{1,0:T(8,128)(2,1)S(1)}, bf16[32,5248]{1,0:T(8,128)(2,1)S(1)}, u32[]{:S(2)}, u32[]{:S(2)}) collective-permute-start(bf16[32,5248]{1,0:T(8,128)(2,1)S(1)} %maximum_select_fusion.2), channel_id=1, source_target_pairs={{0,2},{1,3},{2,0},{3,1},{4,6},{5,7},{6,4},{7,5},{8,10},{9,11},{10,... | collective-permute-start | bytes 1007624 | tf_op jit(solution)/shard_map/ppermute | solution.py:40
  236.0 7.1 %collective-permute-done.20 = bf16[32,5248]{1,0:T(8,128)(2,1)S(1)} collective-permute-done((bf16[32,5248]{1,0:T(8,128)(2,1)S(1)}, bf16[32,5248]{1,0:T(8,128)(2,1)S(1)}, u32[]{:S(2)}, u32[]{:S(2)}) %collective-permute-start.20) | collective-permute-done | bytes 335904 | tf_op jit(solution)/shard_map/ppermute | solution.py:40
  247.4 6.6 %collective-permute-done.21 = bf16[64,5248]{1,0:T(8,128)(2,1)S(1)} collective-permute-done((bf16[64,5248]{1,0:T(8,128)(2,1)S(1)}, bf16[64,5248]{1,0:T(8,128)(2,1)S(1)}, u32[]{:S(2)}, u32[]{:S(2)}) %collective-permute-start.21) | collective-permute-done | bytes 671776 | tf_op jit(solution)/shard_map/ppermute | solution.py:40
  254.4 17.9 %collective-permute-done.26.piece.small = bf16[128,5248]{1,0:T(8,128)(2,1)S(1)} collective-permute-done((bf16[128,5248]{1,0:T(8,128)(2,1)S(1)}, bf16[128,5248]{1,0:T(8,128)(2,1)S(1)}, u32[]{:S(2)}, u32[]{:S(2)}) %collective-permute-start.26) | collective-permute-done | bytes 1343520 | tf_op jit(solution)/shard_map/ppermute | solution.py:40
  279.1 3.5 %shard_map.129 = (f32[9,512,512]{2,1,0:T(8,128)}, f32[616,512]{1,0:T(8,128)}, f32[1,512]{1,0:T(1,128)}) custom-call(s32[1]{0:T(128)} %bitcast.85.at, bf16[128,5248]{1,0:T(8,128)(2,1)} %collective-permute-done.27.piece.small, bf16[128,5248]{1,0:T(8,128)(2,1)} %collective-permute-done.27.piece.small, ...), custom_call_target="tpu_custom_call", output_to_operand_aliasing={{0}: (3, {}), {1}: (4, {}), {2}: (5, {})} | custom-call | tf_op jit(solution)/shard_map/pallas_call | solution.py:106
  (212 shorter events, 109.6 us)
Async XLA Ops:
  4.1 35.1 %all-to-all-start = ((s32[8,1,3]{2,1,0:T(1,128)}), s32[8,1,3]{2,1,0:T(1,128)S(1)}, u32[]{:S(2)}, u32[]{:S(2)}) async-start(s32[8,1,3]{2,1,0:T(1,128)} %copy.81), calls=%async_computation | async-start | bytes 8192 | tf_op jit(solution)/shard_map/all_to_all | solution.py:345
  13.1 26.5 %collective-permute-start.1 = (bf16[24,1,512]{2,1,0:T(2,128)(2,1)}, bf16[24,1,512]{2,1,0:T(2,128)(2,1)}, u32[]{:S(2)}, u32[]{:S(2)}) collective-permute-start(bf16[24,1,512]{2,1,0:T(2,128)(2,1)} %get-tuple-element.107), channel_id=1, source_target_pairs={{1,0},{2,1},{3,2},{4,3},{5,4},{6,5},{7,6},{0,7},{9,8},{10,9},{11,1... | collective-permute-start | bytes 73736 | tf_op jit(solution)/shard_map/ppermute | solution.py:89
  17.8 21.8 %collective-permute-start = (bf16[24,1,512]{2,1,0:T(2,128)(2,1)}, bf16[24,1,512]{2,1,0:T(2,128)(2,1)}, u32[]{:S(2)}, u32[]{:S(2)}) collective-permute-start(bf16[24,1,512]{2,1,0:T(2,128)(2,1)} %get-tuple-element.106), channel_id=1, source_target_pairs={{0,1},{1,2},{2,3},{3,4},{4,5},{5,6},{6,7},{7,0},{8,9},{9,10},{10,1... | collective-permute-start | bytes 73736 | tf_op jit(solution)/shard_map/ppermute | solution.py:88
  22.4 46.4 %collective-permute-start.8 = (bf16[616,384]{1,0:T(8,128)(2,1)}, bf16[616,384]{1,0:T(8,128)(2,1)S(1)}, u32[]{:S(2)}, u32[]{:S(2)}) collective-permute-start(bf16[616,384]{1,0:T(8,128)(2,1)} %get-tuple-element.44), channel_id=1, source_target_pairs={{0,1},{1,0},{2,3},{3,2},{4,5},{5,4},{6,7},{7,6},{8,9},{9,8},{10,11... | collective-permute-start | bytes 1419272 | tf_op jit(solution)/shard_map/ppermute | solution.py:40
  22.7 50.2 %collective-permute-start.9 = (bf16[616,384]{1,0:T(8,128)(2,1)}, bf16[616,384]{1,0:T(8,128)(2,1)S(1)}, u32[]{:S(2)}, u32[]{:S(2)}) collective-permute-start(bf16[616,384]{1,0:T(8,128)(2,1)} %get-tuple-element.45), channel_id=1, source_target_pairs={{0,2},{1,3},{2,0},{3,1},{4,6},{5,7},{6,4},{7,5},{8,10},{9,11},{10,... | collective-permute-start | bytes 1419272 | tf_op jit(solution)/shard_map/ppermute | solution.py:40
  24.1 62.2 %collective-permute-start.10 = (bf16[616,384]{1,0:T(8,128)(2,1)}, bf16[616,384]{1,0:T(8,128)(2,1)}, u32[]{:S(2)}, u32[]{:S(2)}) collective-permute-start(bf16[616,384]{1,0:T(8,128)(2,1)} %get-tuple-element.46), channel_id=1, source_target_pairs={{0,3},{1,2},{2,1},{3,0},{4,7},{5,6},{6,5},{7,4},{8,11},{9,10},{10,... | collective-permute-start | bytes 1419272 | tf_op jit(solution)/shard_map/ppermute | solution.py:40
  46.5 54.6 %collective-permute-start.5 = (bf16[616,384]{1,0:T(8,128)(2,1)S(1)}, bf16[616,384]{1,0:T(8,128)(2,1)S(1)}, u32[]{:S(2)}, u32[]{:S(2)}) collective-permute-start(bf16[616,384]{1,0:T(8,128)(2,1)S(1)} %copy-done.32), channel_id=1, source_target_pairs={{0,4},{1,5},{2,6},{3,7},{4,0},{5,1},{6,2},{7,3},{8,12},{9,13},{10,... | collective-permute-start | bytes 1419272 | tf_op jit(solution)/shard_map/ppermute | solution.py:40
  48.9 61.7 %collective-permute-start.6 = (bf16[616,384]{1,0:T(8,128)(2,1)S(1)}, bf16[616,384]{1,0:T(8,128)(2,1)S(1)}, u32[]{:S(2)}, u32[]{:S(2)}) collective-permute-start(bf16[616,384]{1,0:T(8,128)(2,1)S(1)} %copy-done.30), channel_id=1, source_target_pairs={{0,5},{1,4},{2,7},{3,6},{4,1},{5,0},{6,3},{7,2},{8,13},{9,12},{10,... | collective-permute-start | bytes 1419272 | tf_op jit(solution)/shard_map/ppermute | solution.py:40
  68.8 41.8 %collective-permute-start.7 = (bf16[616,384]{1,0:T(8,128)(2,1)S(1)}, bf16[616,384]{1,0:T(8,128)(2,1)S(1)}, u32[]{:S(2)}, u32[]{:S(2)}) collective-permute-start(bf16[616,384]{1,0:T(8,128)(2,1)S(1)} %copy-done.28), channel_id=1, source_target_pairs={{0,6},{1,7},{2,4},{3,5},{4,2},{5,3},{6,0},{7,1},{8,14},{9,15},{10,... | collective-permute-start | bytes 1419272 | tf_op jit(solution)/shard_map/ppermute | solution.py:40
  72.9 43.1 %collective-permute-start.4 = (bf16[616,384]{1,0:T(8,128)(2,1)S(1)}, bf16[616,384]{1,0:T(8,128)(2,1)S(1)}, u32[]{:S(2)}, u32[]{:S(2)}) collective-permute-start(bf16[616,384]{1,0:T(8,128)(2,1)S(1)} %copy-done.26), channel_id=1, source_target_pairs={{0,7},{1,6},{2,5},{3,4},{4,3},{5,2},{6,1},{7,0},{8,15},{9,14},{10,... | collective-permute-start | bytes 1419272 | tf_op jit(solution)/shard_map/ppermute | solution.py:40
  132.0 20.5 %collective-permute-start.11 = (bf16[256,4608]{1,0:T(8,128)(2,1)S(1)}, bf16[256,4608]{1,0:T(8,128)(2,1)S(1)}, u32[]{:S(2)}, u32[]{:S(2)}) collective-permute-start(bf16[256,4608]{1,0:T(8,128)(2,1)S(1)} %convolution_convert_fusion), channel_id=1, source_target_pairs={{0,8},{1,9},{2,10},{3,11},{4,12},{5,13},{6,14},{7,15},{8,0},{9,1},... | collective-permute-start | bytes 7077896 | tf_op jit(solution)/shard_map/ppermute | solution.py:40
  135.3 10.7 %collective-permute-start.23 = (bf16[24,1,512]{2,1,0:T(2,128)(2,1)S(1)}, bf16[24,1,512]{2,1,0:T(2,128)(2,1)S(1)}, u32[]{:S(2)}, u32[]{:S(2)}) collective-permute-start(bf16[24,1,512]{2,1,0:T(2,128)(2,1)S(1)} %get-tuple-element.103), channel_id=1, source_target_pairs={{1,0},{2,1},{3,2},{4,3},{5,4},{6,5},{7,6},{0,7},{9,8},{10,9},{11,1... | collective-permute-start | bytes 73736 | tf_op jit(solution)/shard_map/ppermute | solution.py:89
  137.8 8.2 %collective-permute-start.22 = (bf16[24,1,512]{2,1,0:T(2,128)(2,1)S(1)}, bf16[24,1,512]{2,1,0:T(2,128)(2,1)S(1)}, u32[]{:S(2)}, u32[]{:S(2)}) collective-permute-start(bf16[24,1,512]{2,1,0:T(2,128)(2,1)S(1)} %get-tuple-element.102), channel_id=1, source_target_pairs={{0,1},{1,2},{2,3},{3,4},{4,5},{5,6},{6,7},{7,0},{8,9},{9,10},{10,1... | collective-permute-start | bytes 73736 | tf_op jit(solution)/shard_map/ppermute | solution.py:88
  146.1 12.8 %collective-permute-start.24 = (bf16[1,66,512]{2,1,0:T(8,128)(2,1)S(1)}, bf16[1,66,512]{2,1,0:T(8,128)(2,1)S(1)}, u32[]{:S(2)}, u32[]{:S(2)}) collective-permute-start(bf16[1,66,512]{2,1,0:T(8,128)(2,1)S(1)} %get-tuple-element.94), channel_id=1, source_target_pairs={{0,8},{8,16},{16,24},{1,9},{9,17},{17,25},{2,10},{10,18},{18,26},{... | collective-permute-start | bytes 202760 | tf_op jit(solution)/shard_map/ppermute | solution.py:88
  148.1 10.7 %collective-permute-start.25 = (bf16[1,66,512]{2,1,0:T(8,128)(2,1)S(1)}, bf16[1,66,512]{2,1,0:T(8,128)(2,1)S(1)}, u32[]{:S(2)}, u32[]{:S(2)}) collective-permute-start(bf16[1,66,512]{2,1,0:T(8,128)(2,1)S(1)} %get-tuple-element.95), channel_id=1, source_target_pairs={{8,0},{16,8},{24,16},{9,1},{17,9},{25,17},{10,2},{18,10},{26,18},{... | collective-permute-start | bytes 202760 | tf_op jit(solution)/shard_map/ppermute | solution.py:89
  154.2 38.0 %collective-permute-start.12 = (bf16[128,4608]{1,0:T(8,128)(2,1)}, bf16[128,4608]{1,0:T(8,128)(2,1)S(1)}, u32[]{:S(2)}, u32[]{:S(2)}) collective-permute-start(bf16[128,4608]{1,0:T(8,128)(2,1)} %get-tuple-element.52), channel_id=1, source_target_pairs={{0,16},{1,17},{2,18},{3,19},{4,20},{5,21},{6,22},{7,23},{8,9},{9,8... | collective-permute-start | bytes 3538952 | tf_op jit(solution)/shard_map/ppermute | solution.py:40
  178.6 12.8 %collective-permute-start.13 = (bf16[256,640]{1,0:T(8,128)(2,1)S(1)}, bf16[256,640]{1,0:T(8,128)(2,1)S(1)}, u32[]{:S(2)}, u32[]{:S(2)}) collective-permute-start(bf16[256,640]{1,0:T(8,128)(2,1)S(1)} %fusion.37), channel_id=1, source_target_pairs={{0,8},{1,9},{2,10},{3,11},{4,12},{5,13},{6,14},{7,15},{8,0},{9,1},... | collective-permute-start | bytes 983048 | tf_op jit(solution)/shard_map/ppermute | solution.py:40
  192.3 11.4 %collective-permute-start.15 = (bf16[64,4608]{1,0:T(8,128)(2,1)S(1)}, bf16[64,4608]{1,0:T(8,128)(2,1)S(1)}, u32[]{:S(2)}, u32[]{:S(2)}) collective-permute-start(bf16[64,4608]{1,0:T(8,128)(2,1)S(1)} %get-tuple-element.76), channel_id=1, source_target_pairs={{0,1},{1,0},{2,3},{3,2},{4,5},{5,4},{6,7},{7,6},{8,24},{9,25},{10,... | collective-permute-start | bytes 1769480 | tf_op jit(solution)/shard_map/ppermute | solution.py:40
  204.0 11.0 %collective-permute-start.17 = (bf16[32,5248]{1,0:T(8,128)(2,1)S(1)}, bf16[32,5248]{1,0:T(8,128)(2,1)S(1)}, u32[]{:S(2)}, u32[]{:S(2)}) collective-permute-start(bf16[32,5248]{1,0:T(8,128)(2,1)S(1)} %get-tuple-element.78), channel_id=1, source_target_pairs={{0,2},{1,3},{2,0},{3,1},{4,6},{5,7},{6,4},{7,5},{8,10},{9,11},{10,... | collective-permute-start | bytes 1007624 | tf_op jit(solution)/shard_map/ppermute | solution.py:40
  215.0 8.2 %collective-permute-start.18 = (bf16[16,5248]{1,0:T(8,128)(2,1)S(1)}, bf16[16,5248]{1,0:T(8,128)(2,1)S(1)}, u32[]{:S(2)}, u32[]{:S(2)}) collective-permute-start(bf16[16,5248]{1,0:T(8,128)(2,1)S(1)} %fusion.38), channel_id=1, source_target_pairs={{0,6},{1,7},{2,4},{3,5},{4,2},{5,3},{6,0},{7,1},{8,14},{9,15},{10,... | collective-permute-start | bytes 503816 | tf_op jit(solution)/shard_map/ppermute | solution.py:40
  230.7 12.4 %collective-permute-start.20 = (bf16[32,5248]{1,0:T(8,128)(2,1)S(1)}, bf16[32,5248]{1,0:T(8,128)(2,1)S(1)}, u32[]{:S(2)}, u32[]{:S(2)}) collective-permute-start(bf16[32,5248]{1,0:T(8,128)(2,1)S(1)} %maximum_select_fusion.2), channel_id=1, source_target_pairs={{0,2},{1,3},{2,0},{3,1},{4,6},{5,7},{6,4},{7,5},{8,10},{9,11},{10,... | collective-permute-start | bytes 1007624 | tf_op jit(solution)/shard_map/ppermute | solution.py:40
  243.2 10.8 %collective-permute-start.21 = (bf16[64,5248]{1,0:T(8,128)(2,1)S(1)}, bf16[64,5248]{1,0:T(8,128)(2,1)S(1)}, u32[]{:S(2)}, u32[]{:S(2)}) collective-permute-start(bf16[64,5248]{1,0:T(8,128)(2,1)S(1)} %maximum_select_fusion.1), channel_id=1, source_target_pairs={{0,1},{1,0},{2,3},{3,2},{4,5},{5,4},{6,7},{7,6},{8,24},{9,25},{10,... | collective-permute-start | bytes 2015240 | tf_op jit(solution)/shard_map/ppermute | solution.py:40
  254.2 18.0 %collective-permute-start.26 = (bf16[128,5248]{1,0:T(8,128)(2,1)S(1)}, bf16[128,5248]{1,0:T(8,128)(2,1)S(1)}, u32[]{:S(2)}, u32[]{:S(2)}) collective-permute-start(bf16[128,5248]{1,0:T(8,128)(2,1)S(1)} %maximum_select_fusion.piece.small), channel_id=1, source_target_pairs={{0,16},{1,17},{2,18},{3,19},{4,20},{5,21},{6,22},{7,23},{8,9},{9,8... | collective-permute-start | bytes 4030472 | tf_op jit(solution)/shard_map/ppermute | solution.py:40
  254.3 19.7 %collective-permute-start.28 = (bf16[128,5248]{1,0:T(8,128)(2,1)S(1)}, bf16[128,5248]{1,0:T(8,128)(2,1)}, u32[]{:S(2)}, u32[]{:S(2)}) collective-permute-start(bf16[128,5248]{1,0:T(8,128)(2,1)S(1)} %maximum_select_fusion.piece.small), channel_id=1, source_target_pairs={{0,8},{1,9},{2,10},{3,11},{4,12},{5,13},{6,14},{7,15},{8,0},{9,1},... | collective-permute-start | bytes 4030472 | tf_op jit(solution)/shard_map/ppermute | solution.py:40
  (49 other events, 315.7 us)

commit v4 on v3

--- a/solution.py
+++ b/solution.py
@@ -169,7 +169,7 @@
     def body(meta_ref, *refs):
         xs = refs[:count]
         w, kern, g = refs[count : count + 3]
-        spread, slope, *rest = refs[count + 3 + (before is not None) :]
+        spread, slope, *rest, enc = refs[count + 3 + (before is not None) :]
         if before is None:
             spread[...] = jnp.zeros_like(spread)
         else:
@@ -178,23 +178,32 @@
             pre = jnp.dot(w[...], xs[k][...], preferred_element_type=jnp.float32)
             s = jax.nn.sigmoid(pre)
             slope[k] = (s * (1.0 + pre * (1.0 - s))).astype(jnp.bfloat16)
-            enc = (pre * s).astype(jnp.bfloat16)
-            for j in range(MOST):
+            enc[...] = (pre * s).astype(jnp.bfloat16)
+
+            def add(j, _, k=k):
                 code = meta_ref[(first + k) * MOST + j]
 
                 @pl.when(code >= 0)
                 def _():
                     spread[code // kernel_count] += jnp.dot(
-                        enc[:, j * rows : (j + 1) * rows],
+                        enc[:, lanes(j, rows)],
                         kern[code % kernel_count],
                         preferred_element_type=jnp.float32,
                     )
 
+                return 0
+
+            lax.fori_loop(0, MOST, add, 0)
+
         if last:
-            for q in range(patches):
+
+            def norm(q, _):
                 cell = spread[q]
                 r = lax.rsqrt(jnp.mean(cell * cell, axis=0, keepdims=True) + EPS)
-                rest[0][:, q * cells : (q + 1) * cells] = (cell * r * g[...]).astype(jnp.bfloat16)
+                rest[0][:, lanes(q, cells)] = (cell * r * g[...]).astype(jnp.bfloat16)
+                return 0
+
+            lax.fori_loop(0, patches, norm, 0)
 
     outs = [
         shape_of((patches, width, cells), jnp.float32),
@@ -203,7 +212,8 @@
     if last:
         outs.append(shape_of((width, patches * cells), jnp.bfloat16))
     ins = [*arrived, weight_t, kernels, gain_col] + ([] if before is None else [before])
-    return call(body, meta, ins, outs)
+    scratch = [pltpu.VMEM((width, MOST * rows), jnp.bfloat16)]
+    return call(body, meta, ins, outs, scratch=scratch)
 
 
 def backward(meta, arrived, kernels_t, gain_col, spread, slopes, d_normed_t):
@@ -218,22 +228,26 @@
         xs = refs[:count]
         slos = refs[count : count + groups]
         kern, g, spr, dn, out, dsp, dpre = refs[count + groups :]
-        total = jnp.zeros((width, 1), jnp.float32)
-        for q in range(patches):
+
+        def unnorm(q, total):
             cell = spr[q]
-            d = dn[:, q * cells : (q + 1) * cells]
+            d = dn[:, lanes(q, cells)]
             r = lax.rsqrt(jnp.mean(cell * cell, axis=0, keepdims=True) + EPS)
             unit = cell * r
-            total = total + jnp.sum(d * unit, axis=1, keepdims=True)
             dg = d * g[...]
             inner = jnp.mean(dg * unit, axis=0, keepdims=True)
             dsp[q] = ((dg - unit * inner) * r).astype(jnp.bfloat16)
+            return total + jnp.sum(d * unit, axis=1, keepdims=True)
+
+        total = lax.fori_loop(0, patches, unnorm, jnp.zeros((width, 1), jnp.float32))
         out[...] = jnp.zeros_like(out)
         out[:, channels : channels + 1] = total
         for k in range(count):
-            for j in range(MOST):
+            n, at = place_of[k]
+
+            def back(j, _, k=k, n=n, at=at):
                 code = meta_ref[k * MOST + j]
-                span = slice(j * rows, (j + 1) * rows)
+                span = lanes(j, rows)
 
                 @pl.when(code >= 0)
                 def _():
@@ -243,13 +257,16 @@
                         preferred_element_type=jnp.float32,
                     ).astype(jnp.bfloat16)
                     dpre[:, span] = (
-                        drow.astype(jnp.float32) * slos[place_of[k][0]][place_of[k][1], :, span].astype(jnp.float32)
+                        drow.astype(jnp.float32) * slos[n][at, :, span].astype(jnp.float32)
                     ).astype(jnp.bfloat16)
 
                 @pl.when(code < 0)
                 def _():
                     dpre[:, span] = jnp.zeros((width, rows), jnp.bfloat16)
 
+                return 0
+
+            lax.fori_loop(0, MOST, back, 0)
             out[:, :channels] += nt(dpre[...], xs[k][...])
 
     ins = [*arrived, *slopes, kernels_t, gain_col, spread, d_normed_t]
@@ -388,7 +405,7 @@
     came = step(away, plan[0][0], lats, lons)
 
     away, keep = split_sum(keep, came, halves[1])
-    away, spread = lax.optimization_barrier((away, spread))
+    away, spread, normed_after = lax.optimization_barrier((away, spread, normed_t))
     came = step(away, plan[1][0], lats, lons)
     kernels_t = kernels.transpose(0, 2, 1)
     small = backward(meta, arrived, kernels_t, gain_col, spread, slopes, d_normed_t)
@@ -408,7 +425,7 @@
     for n in range(apart, len(plan)):
         away, keep = split_sum(keep, came, halves[n])
         came = step(away, plan[n][0], lats, lons)
-    normed = normed_t.reshape(width, tile_rows // PH, tile_cols // PW, PH, PW)
+    normed = normed_after.reshape(width, tile_rows // PH, tile_cols // PW, PH, PW)
     normed = normed.transpose(1, 3, 2, 4, 0).reshape(tile_rows, tile_cols, width)
     padded = padded_2(normed, (("lon", 1),), 1, True)
     padded = padded_2(padded, (("lat", 0),), 1, False)
@@ -426,7 +443,6 @@
         part = jnp.where(
             halves[n] == 0, jnp.concatenate([part, other]), jnp.concatenate([other, part])
         )
-    part, conv_out = lax.optimization_barrier((part, conv_out))
     own, beside = halves[1], kept_half(plan[1][1], lat ^ 1, lon)
     other = step(part, plan[1][0], lats, lons)
     beside_part = step(part, plan[0][0], lats, lons)

time: 287 us -> 268 us (0.934)
  starting transfers between devices: 73.2 us -> 51.3 us
  waiting for transfers between devices: 66.7 us -> 72.5 us
  local copies, waits for them, and re-layouts: 44.4 us -> 39.7 us
  other arithmetic: 16 us -> 20.3 us
  matrix products: 39.9 us -> 35.7 us
    ppermute x21, starting transfers between devices: 52.1 us -> 30.6 us  [exchange(): return lax.ppermute(value, AXES, pairs)]
    ppermute x4, waiting for transfers between devices: 0.01 us -> 4.46 us  [padded_2(): before = lax.ppermute(last, axis, up)]
    dot_general x1, matrix products: 9.2 us -> 5.13 us  [shards(): jnp.dot(pick(normed_t, 1 - core), windows, preferred_element_type=jnp.flo...]
    add x0 -> x1, other arithmetic: none -> 3.97 us  [split_sum(): stay = pick(keep, half) + pick(came, half).astype(jnp.float32)]
    concatenate x5, other arithmetic: 10.6 us -> 7.76 us  [padded_2(): shard = jnp.concatenate([before, shard, after], axis=dim)]
    unnamed x97 -> x69, local copies, waits for them, and re-layouts: 28 us -> 26.5 us
  transfers between devices with their start and end apart: 30 -> 30, of which waited for: 11 -> 11; matrix products, arithmetic and copies ran while one was open for 27% -> 25% of each run, Pallas kernels for 12% -> 14%
where the time goes in v4:
time: 268 us; the launch traced here: 263 us
  waiting for transfers between devices  72.5 us (27%)
  starting transfers between devices  51.3 us (19%)
  Pallas kernels  42 us (16%)
  local copies, waits for them, and re-layouts  39.7 us (15%)
  matrix products  35.7 us (13%)
  other arithmetic  20.3 us (8%)
    ppermute x21, waiting for transfers between devices, exchange(): return lax.ppermute(value, AXES, pairs)  68 us
    pallas_call x10, Pallas kernels, call(): pl.pallas_call(body, out_shape=outs, grid_spec=pltpu.PrefetchScalarGridSp...  42 us
    ppermute x21, starting transfers between devices, exchange(): return lax.ppermute(value, AXES, pairs)  30.6 us
    unnamed x69, local copies, waits for them, and re-layouts  26.5 us
    dot_general x1, matrix products, nt(): lax.dot_general(left, right, (((1,), (1,)), ((), ())), preferred_element_...  13.4 us
    ppermute x4, starting transfers between devices, padded_2(): after = lax.ppermute(leading, axis, down)  10.7 us
    dot_general x9, matrix products, shards(): jnp.dot(window, conv_weight[a, b], preferred_element_type=jnp.float32)  10.1 us
    concatenate x5, other arithmetic, padded_2(): shard = jnp.concatenate([before, shard, after], axis=dim)  7.76 us
  transfers between devices with their start and end apart: 30, of which 11 were waited for; matrix products, arithmetic and copies ran while one was open for 25% of the time, Pallas kernels for 14%

profile of v4, /device:TPU:0, one launch (start us, length us, event | category | flops | bytes accessed | tf_op | source)
XLA Modules:
  0.0 263.1 jit_solution(17758529884545912066)
XLA Ops:
  4.1 7.3 %all-to-all-start = ((s32[8,1,3]{2,1,0:T(1,128)}), s32[8,1,3]{2,1,0:T(1,128)S(1)}, u32[]{:S(2)}, u32[]{:S(2)}) async-start(s32[8,1,3]{2,1,0:T(1,128)} %copy.81), calls=%async_computation | async-start | bytes 8192 | tf_op jit(solution)/shard_map/all_to_all | solution.py:362
  12.5 4.8 %collective-permute-start.1 = (bf16[24,1,512]{2,1,0:T(2,128)(2,1)S(1)}, bf16[24,1,512]{2,1,0:T(2,128)(2,1)S(1)}, u32[]{:S(2)}, u32[]{:S(2)}) collective-permute-start(bf16[24,1,512]{2,1,0:T(2,128)(2,1)S(1)} %get-tuple-element.105), channel_id=1, source_target_pairs={{1,0},{2,1},{3,2},{4,3},{5,4},{6,5},{7,6},{0,7},{9,8},{10,9},{11,1... | collective-permute-start | bytes 73736 | tf_op jit(solution)/shard_map/ppermute | solution.py:89
  21.9 4.8 %collective-permute-start.4 = (bf16[616,384]{1,0:T(8,128)(2,1)}, bf16[616,384]{1,0:T(8,128)(2,1)}, u32[]{:S(2)}, u32[]{:S(2)}) collective-permute-start(bf16[616,384]{1,0:T(8,128)(2,1)} %get-tuple-element.38), channel_id=1, source_target_pairs={{0,7},{1,6},{2,5},{3,4},{4,3},{5,2},{6,1},{7,0},{8,15},{9,14},{10,... | collective-permute-start | bytes 1419272 | tf_op jit(solution)/shard_map/ppermute | solution.py:40
  30.2 6.6 %copy.93 = bf16[3,3,512,512]{2,3,1,0:T(8,128)(2,1)} copy(bf16[3,3,512,512]{3,2,1,0:T(8,128)(2,1)} %param.16) | data formatting | bytes 9437184 | tf_op args[7]
  43.9 4.2 %collective-permute-start.8 = (bf16[616,384]{1,0:T(8,128)(2,1)S(1)}, bf16[616,384]{1,0:T(8,128)(2,1)S(1)}, u32[]{:S(2)}, u32[]{:S(2)}) collective-permute-start(bf16[616,384]{1,0:T(8,128)(2,1)S(1)} %get-tuple-element.43), channel_id=1, source_target_pairs={{0,1},{1,0},{2,3},{3,2},{4,5},{5,4},{6,7},{7,6},{8,9},{9,8},{10,11... | collective-permute-start | bytes 1419272 | tf_op jit(solution)/shard_map/ppermute | solution.py:40
  58.5 10.1 %collective-permute-done.9.refs_2_ = bf16[616,384]{1,0:T(8,128)(2,1)S(1)} collective-permute-done((bf16[616,384]{1,0:T(8,128)(2,1)S(1)}, bf16[616,384]{1,0:T(8,128)(2,1)S(1)}, u32[]{:S(2)}, u32[]{:S(2)}) %collective-permute-start.9) | collective-permute-done | bytes 473120 | tf_op jit(solution)/shard_map/ppermute | solution.py:40
  68.6 7.6 %collective-permute-start.10 = (bf16[616,384]{1,0:T(8,128)(2,1)}, bf16[616,384]{1,0:T(8,128)(2,1)S(1)}, u32[]{:S(2)}, u32[]{:S(2)}) collective-permute-start(bf16[616,384]{1,0:T(8,128)(2,1)} %get-tuple-element.45), channel_id=1, source_target_pairs={{0,3},{1,2},{2,1},{3,0},{4,7},{5,6},{6,5},{7,4},{8,11},{9,10},{10,... | collective-permute-start | bytes 1419272 | tf_op jit(solution)/shard_map/ppermute | solution.py:40
  76.2 13.4 %convolution_bitcast_fusion.refs_14_ = f32[512,1536]{1,0:T(8,128)} fusion(bf16[1536,4608]{1,0:T(8,128)(2,1)} %copy-done.24, bf16[512,4608]{0,1:T(8,128)(2,1)} %bitcast.194), kind=kOutput, calls=%fused_computation.11 | convolution fusion | flops 7247757312 | bytes 22020096 | tf_op jit(solution)/shard_map/dot_general | solution.py:126
  89.5 15.7 %collective-permute-done.10.refs_3_ = bf16[616,384]{1,0:T(8,128)(2,1)S(1)} collective-permute-done((bf16[616,384]{1,0:T(8,128)(2,1)}, bf16[616,384]{1,0:T(8,128)(2,1)S(1)}, u32[]{:S(2)}, u32[]{:S(2)}) %collective-permute-start.10) | collective-permute-done | bytes 473120 | tf_op jit(solution)/shard_map/ppermute | solution.py:40
  105.2 5.5 %shard_map.122 = (f32[12,512,128]{2,1,0:T(8,128)S(1)}, bf16[4,512,384]{2,1,0:T(8,128)(2,1)S(1)}) custom-call(s32[24]{0:T(128)S(1)} %reshape.354.meta_ref, bf16[616,384]{1,0:T(8,128)(2,1)S(1)} %get-tuple-element.42.refs_0_, bf16[616,384]{1,0:T(8,128)(2,1)S(1)} %collective-permute-done.8.refs_1_, bf16[616,384]{1,0:T(8,128)(2,1)S(1)} %collective-permute-done.9.refs_2_, ...), custom_call_target="tpu_custom_call" | custom-call | tf_op jit(solution)/shard_map/pallas_call | solution.py:106
  110.8 5.8 %shard_map.123 = (f32[12,512,128]{2,1,0:T(8,128)S(1)}, bf16[3,512,384]{2,1,0:T(8,128)(2,1)S(1)}) custom-call(s32[24]{0:T(128)S(1)} %reshape.354.meta_ref, bf16[616,384]{1,0:T(8,128)(2,1)} %collective-permute-done.5.refs_0_.refs_4_, bf16[616,384]{1,0:T(8,128)(2,1)} %collective-permute-done.6.refs_1_.refs_5_, ...), custom_call_target="tpu_custom_call" | custom-call | tf_op jit(solution)/shard_map/pallas_call | solution.py:106
  116.7 4.6 %shard_map.124 = (f32[12,512,128]{2,1,0:T(8,128)S(1)}, bf16[1,512,384]{2,1,0:T(8,128)(2,1)S(1)}, bf16[512,1536]{1,0:T(8,128)(2,1)S(1)}) custom-call(s32[24]{0:T(128)S(1)} %reshape.354.meta_ref, bf16[616,384]{1,0:T(8,128)(2,1)} %collective-permute-done.4.refs_0_.refs_7_, bf16[512,616]{1,0:T(8,128)(2,1)S(1)} %bitcast.152, bf16[16,128,128]{2,1,0:T(8,128)(2,1)S(1)} %copy-done.1, ...), custom_call_target="tpu_custom_call" | custom-call | tf_op jit(solution)/shard_map/pallas_call | solution.py:106
  123.7 5.1 %convolution_convert_fusion = bf16[256,4608]{1,0:T(8,128)(2,1)} fusion(bf16[1536,4608]{1,0:T(8,128)(2,1)S(1)} %copy-done.25, bf16[2,256,1536]{2,1,0:T(8,128)(2,1)S(1)} %bitcast.155, s32[]{:T(128)S(6)} %select_n.111), kind=kOutput, calls=%fused_computation.2 | convolution fusion | flops 3625058304 | bytes 17301508 | tf_op jit(solution)/shard_map/dot_general | solution.py:401
  129.0 7.0 %fusion = f32[2,128,4608]{2,1,0:T(8,128)S(1)} fusion(bf16[2,128,1536]{2,1,0:T(8,128)(2,1)S(1)} %bitcast.202, bf16[1536,4608]{1,0:T(8,128)(2,1)} %copy-done.24), kind=kOutput, calls=%fused_computation | convolution fusion | flops 3623878656 | bytes 19660800 | tf_op jit(solution)/shard_map/dot_general | solution.py:404
  136.1 4.0 %convert_add_fusion = (f32[1,128,4608]{2,1,0:T(8,128)}, bf16[128,4608]{1,0:T(8,128)(2,1)}) fusion(f32[2,128,4608]{2,1,0:T(8,128)S(1)} %fusion, s32[]{:T(128)S(6)} %select_n.117, bf16[2,128,4608]{2,1,0:T(8,128)(2,1)} %bitcast.40, s32[]{:T(128)S(6)} %select_n.110), kind=kLoop, calls=%fused_computation.13 | loop fusion | flops 2949120 | bytes 10616840 | tf_op jit(solution)/shard_map/add | solution.py:77
  153.4 14.6 %shard_map.125 = f32[512,640]{1,0:T(8,128)S(1)} custom-call(s32[24]{0:T(128)S(1)} %reshape.354.meta_ref, bf16[616,384]{1,0:T(8,128)(2,1)S(1)} %get-tuple-element.42.refs_0_, bf16[616,384]{1,0:T(8,128)(2,1)S(1)} %copy-done.6, bf16[616,384]{1,0:T(8,128)(2,1)S(1)} %copy-done.8, bf16[616,384]{1,0:T(8,128)(2,1)S(1)} %copy-done.10, ...), custom_call_target="tpu_custom_call" | custom-call | tf_op jit(solution)/shard_map/pallas_call | solution.py:106
  176.8 3.4 %collective-permute-done.18 = bf16[128,640]{1,0:T(8,128)(2,1)} collective-permute-done((bf16[128,640]{1,0:T(8,128)(2,1)}, bf16[128,640]{1,0:T(8,128)(2,1)}, u32[]{:S(2)}, u32[]{:S(2)}) %collective-permute-start.18) | collective-permute-done | bytes 163872 | tf_op jit(solution)/shard_map/ppermute | solution.py:40
  182.0 3.1 %collective-permute-start.13 = (bf16[24,1,512]{2,1,0:T(2,128)(2,1)S(1)}, bf16[24,1,512]{2,1,0:T(2,128)(2,1)S(1)}, u32[]{:S(2)}, u32[]{:S(2)}) collective-permute-start(bf16[24,1,512]{2,1,0:T(2,128)(2,1)S(1)} %get-tuple-element.101), channel_id=1, source_target_pairs={{1,0},{2,1},{3,2},{4,3},{5,4},{6,5},{7,6},{0,7},{9,8},{10,9},{11,1... | collective-permute-start | bytes 73736 | tf_op jit(solution)/shard_map/ppermute | solution.py:89
  188.0 4.5 %collective-permute-done.12 = bf16[24,1,512]{2,1,0:T(2,128)(2,1)S(1)} collective-permute-done((bf16[24,1,512]{2,1,0:T(2,128)(2,1)S(1)}, bf16[24,1,512]{2,1,0:T(2,128)(2,1)S(1)}, u32[]{:S(2)}, u32[]{:S(2)}) %collective-permute-start.12) | collective-permute-done | bytes 24608 | tf_op jit(solution)/shard_map/ppermute | solution.py:88
  198.8 4.8 %collective-permute-done.22 = bf16[16,5248]{1,0:T(8,128)(2,1)S(1)} collective-permute-done((bf16[16,5248]{1,0:T(8,128)(2,1)S(1)}, bf16[16,5248]{1,0:T(8,128)(2,1)S(1)}, u32[]{:S(2)}, u32[]{:S(2)}) %collective-permute-start.22) | collective-permute-done | bytes 167968 | tf_op jit(solution)/shard_map/ppermute | solution.py:40
  207.9 4.6 %collective-permute-done.23 = bf16[16,5248]{1,0:T(8,128)(2,1)S(1)} collective-permute-done((bf16[16,5248]{1,0:T(8,128)(2,1)S(1)}, bf16[16,5248]{1,0:T(8,128)(2,1)S(1)}, u32[]{:S(2)}, u32[]{:S(2)}) %collective-permute-start.23) | collective-permute-done | bytes 167968 | tf_op jit(solution)/shard_map/ppermute | solution.py:40
  215.6 6.8 %collective-permute-done.24 = bf16[32,5248]{1,0:T(8,128)(2,1)S(1)} collective-permute-done((bf16[32,5248]{1,0:T(8,128)(2,1)S(1)}, bf16[32,5248]{1,0:T(8,128)(2,1)S(1)}, u32[]{:S(2)}, u32[]{:S(2)}) %collective-permute-start.24) | collective-permute-done | bytes 335904 | tf_op jit(solution)/shard_map/ppermute | solution.py:40
  226.1 7.2 %collective-permute-done.25 = bf16[64,5248]{1,0:T(8,128)(2,1)S(1)} collective-permute-done((bf16[64,5248]{1,0:T(8,128)(2,1)S(1)}, bf16[64,5248]{1,0:T(8,128)(2,1)S(1)}, u32[]{:S(2)}, u32[]{:S(2)}) %collective-permute-start.25) | collective-permute-done | bytes 671776 | tf_op jit(solution)/shard_map/ppermute | solution.py:40
  237.8 13.7 %collective-permute-done.26.piece.small = bf16[128,5248]{1,0:T(8,128)(2,1)S(1)} collective-permute-done((bf16[128,5248]{1,0:T(8,128)(2,1)S(1)}, bf16[128,5248]{1,0:T(8,128)(2,1)S(1)}, u32[]{:S(2)}, u32[]{:S(2)}) %collective-permute-start.26) | collective-permute-done | bytes 1343520 | tf_op jit(solution)/shard_map/ppermute | solution.py:40
  (184 shorter events, 92.3 us)
Async XLA Ops:
  4.1 34.3 %all-to-all-start = ((s32[8,1,3]{2,1,0:T(1,128)}), s32[8,1,3]{2,1,0:T(1,128)S(1)}, u32[]{:S(2)}, u32[]{:S(2)}) async-start(s32[8,1,3]{2,1,0:T(1,128)} %copy.81), calls=%async_computation | async-start | bytes 8192 | tf_op jit(solution)/shard_map/all_to_all | solution.py:362
  12.5 26.3 %collective-permute-start.1 = (bf16[24,1,512]{2,1,0:T(2,128)(2,1)S(1)}, bf16[24,1,512]{2,1,0:T(2,128)(2,1)S(1)}, u32[]{:S(2)}, u32[]{:S(2)}) collective-permute-start(bf16[24,1,512]{2,1,0:T(2,128)(2,1)S(1)} %get-tuple-element.105), channel_id=1, source_target_pairs={{1,0},{2,1},{3,2},{4,3},{5,4},{6,5},{7,6},{0,7},{9,8},{10,9},{11,1... | collective-permute-start | bytes 73736 | tf_op jit(solution)/shard_map/ppermute | solution.py:89
  17.3 21.6 %collective-permute-start = (bf16[24,1,512]{2,1,0:T(2,128)(2,1)S(1)}, bf16[24,1,512]{2,1,0:T(2,128)(2,1)S(1)}, u32[]{:S(2)}, u32[]{:S(2)}) collective-permute-start(bf16[24,1,512]{2,1,0:T(2,128)(2,1)S(1)} %get-tuple-element.104), channel_id=1, source_target_pairs={{0,1},{1,2},{2,3},{3,4},{4,5},{5,6},{6,7},{7,0},{8,9},{9,10},{10,1... | collective-permute-start | bytes 73736 | tf_op jit(solution)/shard_map/ppermute | solution.py:88
  21.9 94.7 %collective-permute-start.4 = (bf16[616,384]{1,0:T(8,128)(2,1)}, bf16[616,384]{1,0:T(8,128)(2,1)}, u32[]{:S(2)}, u32[]{:S(2)}) collective-permute-start(bf16[616,384]{1,0:T(8,128)(2,1)} %get-tuple-element.38), channel_id=1, source_target_pairs={{0,7},{1,6},{2,5},{3,4},{4,3},{5,2},{6,1},{7,0},{8,15},{9,14},{10,... | collective-permute-start | bytes 1419272 | tf_op jit(solution)/shard_map/ppermute | solution.py:40
  26.7 84.0 %collective-permute-start.5 = (bf16[616,384]{1,0:T(8,128)(2,1)}, bf16[616,384]{1,0:T(8,128)(2,1)}, u32[]{:S(2)}, u32[]{:S(2)}) collective-permute-start(bf16[616,384]{1,0:T(8,128)(2,1)} %get-tuple-element.39), channel_id=1, source_target_pairs={{0,4},{1,5},{2,6},{3,7},{4,0},{5,1},{6,2},{7,3},{8,12},{9,13},{10,... | collective-permute-start | bytes 1419272 | tf_op jit(solution)/shard_map/ppermute | solution.py:40
  26.7 84.1 %collective-permute-start.6 = (bf16[616,384]{1,0:T(8,128)(2,1)}, bf16[616,384]{1,0:T(8,128)(2,1)}, u32[]{:S(2)}, u32[]{:S(2)}) collective-permute-start(bf16[616,384]{1,0:T(8,128)(2,1)} %get-tuple-element.40), channel_id=1, source_target_pairs={{0,5},{1,4},{2,7},{3,6},{4,1},{5,0},{6,3},{7,2},{8,13},{9,12},{10,... | collective-permute-start | bytes 1419272 | tf_op jit(solution)/shard_map/ppermute | solution.py:40
  43.9 13.7 %collective-permute-start.8 = (bf16[616,384]{1,0:T(8,128)(2,1)S(1)}, bf16[616,384]{1,0:T(8,128)(2,1)S(1)}, u32[]{:S(2)}, u32[]{:S(2)}) collective-permute-start(bf16[616,384]{1,0:T(8,128)(2,1)S(1)} %get-tuple-element.43), channel_id=1, source_target_pairs={{0,1},{1,0},{2,3},{3,2},{4,5},{5,4},{6,7},{7,6},{8,9},{9,8},{10,11... | collective-permute-start | bytes 1419272 | tf_op jit(solution)/shard_map/ppermute | solution.py:40
  48.1 20.5 %collective-permute-start.9 = (bf16[616,384]{1,0:T(8,128)(2,1)S(1)}, bf16[616,384]{1,0:T(8,128)(2,1)S(1)}, u32[]{:S(2)}, u32[]{:S(2)}) collective-permute-start(bf16[616,384]{1,0:T(8,128)(2,1)S(1)} %get-tuple-element.44), channel_id=1, source_target_pairs={{0,2},{1,3},{2,0},{3,1},{4,6},{5,7},{6,4},{7,5},{8,10},{9,11},{10,... | collective-permute-start | bytes 1419272 | tf_op jit(solution)/shard_map/ppermute | solution.py:40
  57.6 53.2 %collective-permute-start.7 = (bf16[616,384]{1,0:T(8,128)(2,1)}, bf16[616,384]{1,0:T(8,128)(2,1)S(1)}, u32[]{:S(2)}, u32[]{:S(2)}) collective-permute-start(bf16[616,384]{1,0:T(8,128)(2,1)} %get-tuple-element.41), channel_id=1, source_target_pairs={{0,6},{1,7},{2,4},{3,5},{4,2},{5,3},{6,0},{7,1},{8,14},{9,15},{10,... | collective-permute-start | bytes 1419272 | tf_op jit(solution)/shard_map/ppermute | solution.py:40
  68.6 36.6 %collective-permute-start.10 = (bf16[616,384]{1,0:T(8,128)(2,1)}, bf16[616,384]{1,0:T(8,128)(2,1)S(1)}, u32[]{:S(2)}, u32[]{:S(2)}) collective-permute-start(bf16[616,384]{1,0:T(8,128)(2,1)} %get-tuple-element.45), channel_id=1, source_target_pairs={{0,3},{1,2},{2,1},{3,0},{4,7},{5,6},{6,5},{7,4},{8,11},{9,10},{10,... | collective-permute-start | bytes 1419272 | tf_op jit(solution)/shard_map/ppermute | solution.py:40
  140.0 28.3 %collective-permute-start.16 = (bf16[128,4608]{1,0:T(8,128)(2,1)}, bf16[128,4608]{1,0:T(8,128)(2,1)}, u32[]{:S(2)}, u32[]{:S(2)}) collective-permute-start(bf16[128,4608]{1,0:T(8,128)(2,1)} %get-tuple-element.52), channel_id=1, source_target_pairs={{0,16},{1,17},{2,18},{3,19},{4,20},{5,21},{6,22},{7,23},{8,9},{9,8... | collective-permute-start | bytes 3538952 | tf_op jit(solution)/shard_map/ppermute | solution.py:40
  170.6 15.0 %collective-permute-start.19 = (bf16[64,4608]{1,0:T(8,128)(2,1)}, bf16[64,4608]{1,0:T(8,128)(2,1)}, u32[]{:S(2)}, u32[]{:S(2)}) collective-permute-start(bf16[64,4608]{1,0:T(8,128)(2,1)} %get-tuple-element.74), channel_id=1, source_target_pairs={{0,1},{1,0},{2,3},{3,2},{4,5},{5,4},{6,7},{7,6},{8,24},{9,25},{10,... | collective-permute-start | bytes 1769480 | tf_op jit(solution)/shard_map/ppermute | solution.py:40
  172.8 7.4 %collective-permute-start.18 = (bf16[128,640]{1,0:T(8,128)(2,1)}, bf16[128,640]{1,0:T(8,128)(2,1)}, u32[]{:S(2)}, u32[]{:S(2)}) collective-permute-start(bf16[128,640]{1,0:T(8,128)(2,1)} %get-tuple-element.106), channel_id=1, source_target_pairs={{0,16},{1,17},{2,18},{3,19},{4,20},{5,21},{6,22},{7,23},{8,9},{9,8... | collective-permute-start | bytes 491528 | tf_op jit(solution)/shard_map/ppermute | solution.py:40
  185.1 7.3 %collective-permute-start.12 = (bf16[24,1,512]{2,1,0:T(2,128)(2,1)S(1)}, bf16[24,1,512]{2,1,0:T(2,128)(2,1)S(1)}, u32[]{:S(2)}, u32[]{:S(2)}) collective-permute-start(bf16[24,1,512]{2,1,0:T(2,128)(2,1)S(1)} %get-tuple-element.100), channel_id=1, source_target_pairs={{0,1},{1,2},{2,3},{3,4},{4,5},{5,6},{6,7},{7,0},{8,9},{9,10},{10,1... | collective-permute-start | bytes 73736 | tf_op jit(solution)/shard_map/ppermute | solution.py:88
  186.9 8.4 %collective-permute-start.21 = (bf16[32,5248]{1,0:T(8,128)(2,1)S(1)}, bf16[32,5248]{1,0:T(8,128)(2,1)S(1)}, u32[]{:S(2)}, u32[]{:S(2)}) collective-permute-start(bf16[32,5248]{1,0:T(8,128)(2,1)S(1)} %get-tuple-element.76), channel_id=1, source_target_pairs={{0,2},{1,3},{2,0},{3,1},{4,6},{5,7},{6,4},{7,5},{8,10},{9,11},{10,... | collective-permute-start | bytes 1007624 | tf_op jit(solution)/shard_map/ppermute | solution.py:40
  192.5 13.4 %collective-permute-start.14 = (bf16[1,66,512]{2,1,0:T(8,128)(2,1)S(1)}, bf16[1,66,512]{2,1,0:T(8,128)(2,1)S(1)}, u32[]{:S(2)}, u32[]{:S(2)}) collective-permute-start(bf16[1,66,512]{2,1,0:T(8,128)(2,1)S(1)} %get-tuple-element.92), channel_id=1, source_target_pairs={{0,8},{8,16},{16,24},{1,9},{9,17},{17,25},{2,10},{10,18},{18,26},{... | collective-permute-start | bytes 202760 | tf_op jit(solution)/shard_map/ppermute | solution.py:88
  193.8 12.1 %collective-permute-start.15 = (bf16[1,66,512]{2,1,0:T(8,128)(2,1)S(1)}, bf16[1,66,512]{2,1,0:T(8,128)(2,1)S(1)}, u32[]{:S(2)}, u32[]{:S(2)}) collective-permute-start(bf16[1,66,512]{2,1,0:T(8,128)(2,1)S(1)} %get-tuple-element.93), channel_id=1, source_target_pairs={{8,0},{16,8},{24,16},{9,1},{17,9},{25,17},{10,2},{18,10},{26,18},{... | collective-permute-start | bytes 202760 | tf_op jit(solution)/shard_map/ppermute | solution.py:89
  195.4 8.2 %collective-permute-start.22 = (bf16[16,5248]{1,0:T(8,128)(2,1)S(1)}, bf16[16,5248]{1,0:T(8,128)(2,1)S(1)}, u32[]{:S(2)}, u32[]{:S(2)}) collective-permute-start(bf16[16,5248]{1,0:T(8,128)(2,1)S(1)} %fusion.38), channel_id=1, source_target_pairs={{0,6},{1,7},{2,4},{3,5},{4,2},{5,3},{6,0},{7,1},{8,14},{9,15},{10,... | collective-permute-start | bytes 503816 | tf_op jit(solution)/shard_map/ppermute | solution.py:40
  203.6 8.9 %collective-permute-start.23 = (bf16[16,5248]{1,0:T(8,128)(2,1)S(1)}, bf16[16,5248]{1,0:T(8,128)(2,1)S(1)}, u32[]{:S(2)}, u32[]{:S(2)}) collective-permute-start(bf16[16,5248]{1,0:T(8,128)(2,1)S(1)} %fusion.36), channel_id=1, source_target_pairs={{0,6},{1,7},{2,4},{3,5},{4,2},{5,3},{6,0},{7,1},{8,14},{9,15},{10,... | collective-permute-start | bytes 503816 | tf_op jit(solution)/shard_map/ppermute | solution.py:40
  212.6 9.7 %collective-permute-start.24 = (bf16[32,5248]{1,0:T(8,128)(2,1)S(1)}, bf16[32,5248]{1,0:T(8,128)(2,1)S(1)}, u32[]{:S(2)}, u32[]{:S(2)}) collective-permute-start(bf16[32,5248]{1,0:T(8,128)(2,1)S(1)} %maximum_select_fusion.2), channel_id=1, source_target_pairs={{0,2},{1,3},{2,0},{3,1},{4,6},{5,7},{6,4},{7,5},{8,10},{9,11},{10,... | collective-permute-start | bytes 1007624 | tf_op jit(solution)/shard_map/ppermute | solution.py:40
  222.5 10.8 %collective-permute-start.25 = (bf16[64,5248]{1,0:T(8,128)(2,1)S(1)}, bf16[64,5248]{1,0:T(8,128)(2,1)S(1)}, u32[]{:S(2)}, u32[]{:S(2)}) collective-permute-start(bf16[64,5248]{1,0:T(8,128)(2,1)S(1)} %maximum_select_fusion.1), channel_id=1, source_target_pairs={{0,1},{1,0},{2,3},{3,2},{4,5},{5,4},{6,7},{7,6},{8,24},{9,25},{10,... | collective-permute-start | bytes 2015240 | tf_op jit(solution)/shard_map/ppermute | solution.py:40
  233.5 18.0 %collective-permute-start.26 = (bf16[128,5248]{1,0:T(8,128)(2,1)S(1)}, bf16[128,5248]{1,0:T(8,128)(2,1)S(1)}, u32[]{:S(2)}, u32[]{:S(2)}) collective-permute-start(bf16[128,5248]{1,0:T(8,128)(2,1)S(1)} %maximum_select_fusion.piece.small), channel_id=1, source_target_pairs={{0,16},{1,17},{2,18},{3,19},{4,20},{5,21},{6,22},{7,23},{8,9},{9,8... | collective-permute-start | bytes 4030472 | tf_op jit(solution)/shard_map/ppermute | solution.py:40
  237.7 19.8 %collective-permute-start.28 = (bf16[128,5248]{1,0:T(8,128)(2,1)S(1)}, bf16[128,5248]{1,0:T(8,128)(2,1)S(1)}, u32[]{:S(2)}, u32[]{:S(2)}) collective-permute-start(bf16[128,5248]{1,0:T(8,128)(2,1)S(1)} %maximum_select_fusion.piece.small), channel_id=1, source_target_pairs={{0,8},{1,9},{2,10},{3,11},{4,12},{5,13},{6,14},{7,15},{8,0},{9,1},... | collective-permute-start | bytes 4030472 | tf_op jit(solution)/shard_map/ppermute | solution.py:40
  251.5 9.5 %collective-permute-start.27 = (bf16[128,5248]{1,0:T(8,128)(2,1)S(1)}, bf16[128,5248]{1,0:T(8,128)(2,1)S(1)}, u32[]{:S(2)}, u32[]{:S(2)}) collective-permute-start(bf16[128,5248]{1,0:T(8,128)(2,1)S(1)} %collective-permute-done.26.piece.small), channel_id=1, source_target_pairs={{0,8},{1,9},{2,10},{3,11},{4,12},{5,13},{6,14},{7,15},{8,0},{9,1},... | collective-permute-start | bytes 4030472 | tf_op jit(solution)/shard_map/ppermute | solution.py:40
  (35 other events, 288.7 us)

commit v5 on v4

--- a/solution.py
+++ b/solution.py
@@ -227,7 +227,14 @@
     def body(meta_ref, *refs):
         xs = refs[:count]
         slos = refs[count : count + groups]
-        kern, g, spr, dn, out, dsp, dpre = refs[count + groups :]
+        kern, g, spr, dn, out, dsp, dpre, xbuf, sbuf, sems = refs[count + groups :]
+        copies = []
+        for k in range(count):
+            n, at = place_of[k]
+            copies.append(pltpu.make_async_copy(xs[k], xbuf.at[k], sems.at[2 * k]))
+            copies.append(pltpu.make_async_copy(slos[n].at[at], sbuf.at[k], sems.at[2 * k + 1]))
+        for one in copies:
+            one.start()
 
         def unnorm(q, total):
             cell = spr[q]
@@ -243,9 +250,10 @@
         out[...] = jnp.zeros_like(out)
         out[:, channels : channels + 1] = total
         for k in range(count):
-            n, at = place_of[k]
-
-            def back(j, _, k=k, n=n, at=at):
+            copies[2 * k].wait()
+            copies[2 * k + 1].wait()
+
+            def back(j, _, k=k):
                 code = meta_ref[k * MOST + j]
                 span = lanes(j, rows)
 
@@ -257,7 +265,7 @@
                         preferred_element_type=jnp.float32,
                     ).astype(jnp.bfloat16)
                     dpre[:, span] = (
-                        drow.astype(jnp.float32) * slos[n][at, :, span].astype(jnp.float32)
+                        drow.astype(jnp.float32) * sbuf[k, :, span].astype(jnp.float32)
                     ).astype(jnp.bfloat16)
 
                 @pl.when(code < 0)
@@ -267,15 +275,20 @@
                 return 0
 
             lax.fori_loop(0, MOST, back, 0)
-            out[:, :channels] += nt(dpre[...], xs[k][...])
+            out[:, :channels] += nt(dpre[...], xbuf[k])
 
     ins = [*arrived, *slopes, kernels_t, gain_col, spread, d_normed_t]
     outs = [shape_of((width, (channels // LANES + 1) * LANES), jnp.float32)]
     scratch = [
         pltpu.VMEM((patches, width, cells), jnp.bfloat16),
         pltpu.VMEM((width, MOST * rows), jnp.bfloat16),
+        pltpu.VMEM((count, channels, MOST * rows), jnp.bfloat16),
+        pltpu.VMEM((count, width, MOST * rows), jnp.bfloat16),
+        pltpu.SemaphoreType.DMA((2 * count,)),
     ]
-    return call(body, meta, ins, outs, scratch=scratch)[0]
+    far = [pl.BlockSpec(memory_space=pl.ANY)] * (count + groups)
+    in_specs = far + [whole(a.shape) for a in ins[count + groups :]]
+    return call(body, meta, ins, outs, in_specs=in_specs, scratch=scratch)[0]
 
 
 def place(quarter, part, taps, lane, channels, scale, into=None):
@@ -401,28 +414,17 @@
     away = jnp.dot(
         pick(normed_t, 1 - core), windows, preferred_element_type=jnp.float32
     ).astype(jnp.bfloat16)
-    keep = jnp.dot(pick(normed_t, core), windows, preferred_element_type=jnp.float32)
     came = step(away, plan[0][0], lats, lons)
-
-    away, keep = split_sum(keep, came, halves[1])
-    away, spread, normed_after = lax.optimization_barrier((away, spread, normed_t))
-    came = step(away, plan[1][0], lats, lons)
     kernels_t = kernels.transpose(0, 2, 1)
     small = backward(meta, arrived, kernels_t, gain_col, spread, slopes, d_normed_t)
-    small_keep = pick(small, core)
     small_came = step(pick(small, 1 - core).astype(jnp.bfloat16), plan[0][0], lats, lons)
-
-    away, small_keep = split_sum(small_keep, small_came, halves[1])
-    small_came = step(away, plan[1][0], lats, lons)
-    apart = len(plan) - 2
-    for n in range(2, apart):
-        away, keep = split_sum(keep, came, halves[n])
-        came = step(away, plan[n][0], lats, lons)
-        away, small_keep = split_sum(small_keep, small_came, halves[n])
-        small_came = step(away, plan[n][0], lats, lons)
-    keep = jnp.concatenate([keep, small_keep], axis=1)
-    came = jnp.concatenate([came, small_came], axis=1)
-    for n in range(apart, len(plan)):
+    keep = jnp.dot(pick(normed_t, core), windows, preferred_element_type=jnp.float32)
+    big_split = split_sum(keep, came, halves[1])
+    small_split = split_sum(pick(small, core), small_came, halves[1])
+    away, keep = [jnp.concatenate(both, axis=1) for both in zip(big_split, small_split)]
+    away, normed_after = lax.optimization_barrier((away, normed_t))
+    came = step(away, plan[1][0], lats, lons)
+    for n in range(2, len(plan)):
         away, keep = split_sum(keep, came, halves[n])
         came = step(away, plan[n][0], lats, lons)
     normed = normed_after.reshape(width, tile_rows // PH, tile_cols // PW, PH, PW)
@@ -436,7 +438,8 @@
             result_sum = result_sum + jnp.dot(
                 window, conv_weight[a, b], preferred_element_type=jnp.float32
             )
-    conv_out = result_sum.reshape(tile_rows, tile_cols, width).astype(jnp.bfloat16)
+        if a == 2:
+            conv_out = result_sum.reshape(tile_rows, tile_cols, width).astype(jnp.bfloat16)
     part = (keep + came.astype(jnp.float32)).astype(jnp.bfloat16)
     for n in range(len(plan) - 1, 1, -1):
         other = step(part, plan[n][0], lats, lons)

time: 268 us -> 300 us (1.12)
  starting transfers between devices: 51.3 us -> 69.2 us
  waiting for transfers between devices: 72.5 us -> 81.6 us
  local copies, waits for them, and re-layouts: 39.7 us -> 43.8 us
    ppermute x21 -> x19, starting transfers between devices: 30.6 us -> 48.3 us  [exchange(): return lax.ppermute(value, AXES, pairs)]
    ppermute x21 -> x19, waiting for transfers between devices: 68 us -> 81.6 us  [exchange(): return lax.ppermute(value, AXES, pairs)]
    ppermute x4, waiting for transfers between devices: 4.46 us -> 0.01 us  [padded_2(): before = lax.ppermute(last, axis, up)]
    unnamed x69 -> x79, local copies, waits for them, and re-layouts: 26.5 us -> 30 us
  transfers between devices with their start and end apart: 30 -> 28, of which waited for: 11 -> 10; matrix products, arithmetic and copies ran while one was open for 25% -> 21% of each run, Pallas kernels for 14% -> 13%
where the time goes in v5:
time: 300 us; the launch traced here: 295 us
  waiting for transfers between devices  81.6 us (27%)
  starting transfers between devices  69.2 us (23%)
  local copies, waits for them, and re-layouts  43.8 us (15%)
  Pallas kernels  42.6 us (14%)
  matrix products  36.7 us (12%)
  other arithmetic  19.4 us (6%)
    ppermute x19, waiting for transfers between devices, exchange(): return lax.ppermute(value, AXES, pairs)  81.6 us
    ppermute x19, starting transfers between devices, exchange(): return lax.ppermute(value, AXES, pairs)  48.3 us
    pallas_call x10, Pallas kernels, call(): pl.pallas_call(body, out_shape=outs, grid_spec=pltpu.PrefetchScalarGridSp...  42.6 us
    unnamed x79, local copies, waits for them, and re-layouts  30 us
    dot_general x1, matrix products, nt(): lax.dot_general(left, right, (((1,), (1,)), ((), ())), preferred_element_...  13.4 us
    dot_general x9, matrix products, shards(): jnp.dot(window, conv_weight[a, b], preferred_element_type=jnp.float32)  11.2 us
    ppermute x4, starting transfers between devices, padded_2(): after = lax.ppermute(leading, axis, down)  10.8 us
    concatenate x5, other arithmetic, padded_2(): shard = jnp.concatenate([before, shard, after], axis=dim)  7.77 us
  transfers between devices with their start and end apart: 28, of which 10 were waited for; matrix products, arithmetic and copies ran while one was open for 21% of the time, Pallas kernels for 13%

profile of v5, /device:TPU:0, one launch (start us, length us, event | category | flops | bytes accessed | tf_op | source)
XLA Modules:
  0.0 294.8 jit_solution(14493053536485788725)
XLA Ops:
  4.1 7.3 %all-to-all-start = ((s32[8,1,3]{2,1,0:T(1,128)}), s32[8,1,3]{2,1,0:T(1,128)S(1)}, u32[]{:S(2)}, u32[]{:S(2)}) async-start(s32[8,1,3]{2,1,0:T(1,128)} %copy.81), calls=%async_computation | async-start | bytes 8192 | tf_op jit(solution)/shard_map/all_to_all | solution.py:375
  13.1 4.7 %collective-permute-start.1 = (bf16[24,1,512]{2,1,0:T(2,128)(2,1)}, bf16[24,1,512]{2,1,0:T(2,128)(2,1)S(1)}, u32[]{:S(2)}, u32[]{:S(2)}) collective-permute-start(bf16[24,1,512]{2,1,0:T(2,128)(2,1)} %get-tuple-element.103), channel_id=1, source_target_pairs={{1,0},{2,1},{3,2},{4,3},{5,4},{6,5},{7,6},{0,7},{9,8},{10,9},{11,1... | collective-permute-start | bytes 73736 | tf_op jit(solution)/shard_map/ppermute | solution.py:89
  29.5 6.6 %copy.93 = bf16[3,3,512,512]{2,3,1,0:T(8,128)(2,1)} copy(bf16[3,3,512,512]{3,2,1,0:T(8,128)(2,1)} %param.16) | data formatting | bytes 9437184 | tf_op args[7]
  61.9 13.4 %convolution_bitcast_fusion.refs_14_ = f32[512,1536]{1,0:T(8,128)} fusion(bf16[1536,4608]{1,0:T(8,128)(2,1)} %copy-done.29, bf16[512,4608]{0,1:T(8,128)(2,1)} %bitcast.191), kind=kOutput, calls=%fused_computation.13 | convolution fusion | flops 7247757312 | bytes 22020096 | tf_op jit(solution)/shard_map/dot_general | solution.py:126
  75.3 5.5 %shard_map.122 = (f32[12,512,128]{2,1,0:T(8,128)S(1)}, bf16[4,512,384]{2,1,0:T(8,128)(2,1)S(1)}) custom-call(s32[24]{0:T(128)S(1)} %reshape.341.meta_ref, bf16[616,384]{1,0:T(8,128)(2,1)S(1)} %get-tuple-element.41.refs_0_, bf16[616,384]{1,0:T(8,128)(2,1)S(1)} %collective-permute-done.8.refs_1_, bf16[616,384]{1,0:T(8,128)(2,1)S(1)} %collective-permute-done.9.refs_2_, ...), custom_call_target="tpu_custom_call" | custom-call | tf_op jit(solution)/shard_map/pallas_call | solution.py:106
  80.8 17.3 %collective-permute-done.5.refs_0_.refs_4_ = bf16[616,384]{1,0:T(8,128)(2,1)S(1)} collective-permute-done((bf16[616,384]{1,0:T(8,128)(2,1)}, bf16[616,384]{1,0:T(8,128)(2,1)S(1)}, u32[]{:S(2)}, u32[]{:S(2)}) %collective-permute-start.5) | collective-permute-done | bytes 473120 | tf_op jit(solution)/shard_map/ppermute | solution.py:40
  98.1 9.4 %collective-permute-done.6.refs_1_.refs_5_ = bf16[616,384]{1,0:T(8,128)(2,1)S(1)} collective-permute-done((bf16[616,384]{1,0:T(8,128)(2,1)}, bf16[616,384]{1,0:T(8,128)(2,1)S(1)}, u32[]{:S(2)}, u32[]{:S(2)}) %collective-permute-start.6) | collective-permute-done | bytes 473120 | tf_op jit(solution)/shard_map/ppermute | solution.py:40
  107.5 4.5 %shard_map.123 = (f32[12,512,128]{2,1,0:T(8,128)S(1)}, bf16[3,512,384]{2,1,0:T(8,128)(2,1)S(1)}) custom-call(s32[24]{0:T(128)S(1)} %reshape.341.meta_ref, bf16[616,384]{1,0:T(8,128)(2,1)S(1)} %collective-permute-done.5.refs_0_.refs_4_, bf16[616,384]{1,0:T(8,128)(2,1)S(1)} %collective-permute-done.6.refs_1_.refs_5_, ...), custom_call_target="tpu_custom_call" | custom-call | tf_op jit(solution)/shard_map/pallas_call | solution.py:106
  112.1 3.6 %shard_map.124 = (f32[12,512,128]{2,1,0:T(8,128)S(1)}, bf16[1,512,384]{2,1,0:T(8,128)(2,1)S(1)}, bf16[512,1536]{1,0:T(8,128)(2,1)S(1)}) custom-call(s32[24]{0:T(128)S(1)} %reshape.341.meta_ref, bf16[616,384]{1,0:T(8,128)(2,1)S(1)} %collective-permute-done.4.refs_0_.refs_7_, bf16[512,616]{1,0:T(8,128)(2,1)S(1)} %bitcast.148, ...), custom_call_target="tpu_custom_call" | custom-call | tf_op jit(solution)/shard_map/pallas_call | solution.py:106
  117.5 5.1 %convolution_convert_fusion = bf16[256,4608]{1,0:T(8,128)(2,1)} fusion(bf16[1536,4608]{1,0:T(8,128)(2,1)S(1)} %copy-done.30, bf16[2,256,1536]{2,1,0:T(8,128)(2,1)S(1)} %bitcast.151, s32[]{:T(128)S(6)} %select_n.105), kind=kOutput, calls=%fused_computation.2 | convolution fusion | flops 3625058304 | bytes 17301508 | tf_op jit(solution)/shard_map/dot_general | solution.py:414
  140.5 17.3 %shard_map.125 = f32[512,640]{1,0:T(8,128)S(1)} custom-call(s32[24]{0:T(128)S(1)} %reshape.341.meta_ref, bf16[616,384]{1,0:T(8,128)(2,1)S(1)} %get-tuple-element.41.refs_0_, bf16[616,384]{1,0:T(8,128)(2,1)S(1)} %copy-done.6, bf16[616,384]{1,0:T(8,128)(2,1)S(1)} %copy-done.8, bf16[616,384]{1,0:T(8,128)(2,1)S(1)} %copy-done.10, ...), custom_call_target="tpu_custom_call" | custom-call | tf_op jit(solution)/shard_map/pallas_call | solution.py:106
  158.0 7.0 %fusion = f32[2,128,4608]{2,1,0:T(8,128)S(1)} fusion(bf16[2,128,1536]{2,1,0:T(8,128)(2,1)S(1)} %bitcast.197, bf16[1536,4608]{1,0:T(8,128)(2,1)} %copy-done.29), kind=kOutput, calls=%fused_computation | convolution fusion | flops 3623878656 | bytes 19660800 | tf_op jit(solution)/shard_map/dot_general | solution.py:421
  165.2 3.6 %convert_add_fusion = (f32[1,128,4608]{2,1,0:T(8,128)}, bf16[128,4608]{1,0:T(8,128)(2,1)S(1)}) fusion(f32[2,128,4608]{2,1,0:T(8,128)S(1)} %fusion, s32[]{:T(128)S(6)} %select_n.111, bf16[2,128,4608]{2,1,0:T(8,128)(2,1)} %bitcast.40, s32[]{:T(128)S(6)} %select_n.104), kind=kLoop, calls=%fused_computation.17 | loop fusion | flops 2949120 | bytes 10616840 | tf_op jit(solution)/shard_map/add | solution.py:77
  173.2 16.3 %collective-permute-done.17 = bf16[128,5248]{1,0:T(8,128)(2,1)} collective-permute-done((bf16[128,5248]{1,0:T(8,128)(2,1)}, bf16[128,5248]{1,0:T(8,128)(2,1)}, u32[]{:S(2)}, u32[]{:S(2)}) %collective-permute-start.17) | collective-permute-done | bytes 1343520 | tf_op jit(solution)/shard_map/ppermute | solution.py:40
  189.4 3.3 %fusion.13 = (bf16[64,5248]{1,0:T(8,128)(2,1)S(1)}, f32[1,64,5248]{2,1,0:T(8,128)}) fusion(s32[]{:T(128)S(6)} %select_n.114, f32[2,64,640]{2,1,0:T(8,128)S(1)} %bitcast.196, f32[2,64,4608]{2,1,0:T(8,128)} %bitcast.165, bf16[2,64,5248]{2,1,0:T(8,128)(2,1)} %bitcast.74, s32[]{:T(128)S(6)} %select_n.112), kind=kLoop, calls=%fused_computation.37 | loop fusion | flops 2351104 | bytes 6045704 | tf_op jit(solution)/shard_map/convert_element_type | solution.py:78
  196.2 3.5 %collective-permute-start.14 = (bf16[24,1,512]{2,1,0:T(2,128)(2,1)S(1)}, bf16[24,1,512]{2,1,0:T(2,128)(2,1)S(1)}, u32[]{:S(2)}, u32[]{:S(2)}) collective-permute-start(bf16[24,1,512]{2,1,0:T(2,128)(2,1)S(1)} %get-tuple-element.99), channel_id=1, source_target_pairs={{1,0},{2,1},{3,2},{4,3},{5,4},{6,5},{7,6},{0,7},{9,8},{10,9},{11,1... | collective-permute-start | bytes 73736 | tf_op jit(solution)/shard_map/ppermute | solution.py:89
  199.9 4.1 %collective-permute-done.18 = bf16[64,5248]{1,0:T(8,128)(2,1)S(1)} collective-permute-done((bf16[64,5248]{1,0:T(8,128)(2,1)S(1)}, bf16[64,5248]{1,0:T(8,128)(2,1)S(1)}, u32[]{:S(2)}, u32[]{:S(2)}) %collective-permute-start.18) | collective-permute-done | bytes 671776 | tf_op jit(solution)/shard_map/ppermute | solution.py:40
  204.2 15.8 %collective-permute-start.19 = (bf16[32,5248]{1,0:T(8,128)(2,1)S(1)}, bf16[32,5248]{1,0:T(8,128)(2,1)S(1)}, u32[]{:S(2)}, u32[]{:S(2)}) collective-permute-start(bf16[32,5248]{1,0:T(8,128)(2,1)S(1)} %get-tuple-element.74), channel_id=1, source_target_pairs={{0,2},{1,3},{2,0},{3,1},{4,6},{5,7},{6,4},{7,5},{8,10},{9,11},{10,... | collective-permute-start | bytes 1007624 | tf_op jit(solution)/shard_map/ppermute | solution.py:40
  225.1 3.6 %collective-permute-start.20 = (bf16[16,5248]{1,0:T(8,128)(2,1)S(1)}, bf16[16,5248]{1,0:T(8,128)(2,1)S(1)}, u32[]{:S(2)}, u32[]{:S(2)}) collective-permute-start(bf16[16,5248]{1,0:T(8,128)(2,1)S(1)} %fusion.38), channel_id=1, source_target_pairs={{0,6},{1,7},{2,4},{3,5},{4,2},{5,3},{6,0},{7,1},{8,14},{9,15},{10,... | collective-permute-start | bytes 503816 | tf_op jit(solution)/shard_map/ppermute | solution.py:40
  232.5 3.6 %collective-permute-start.21 = (bf16[16,5248]{1,0:T(8,128)(2,1)S(1)}, bf16[16,5248]{1,0:T(8,128)(2,1)S(1)}, u32[]{:S(2)}, u32[]{:S(2)}) collective-permute-start(bf16[16,5248]{1,0:T(8,128)(2,1)S(1)} %fusion.36), channel_id=1, source_target_pairs={{0,6},{1,7},{2,4},{3,5},{4,2},{5,3},{6,0},{7,1},{8,14},{9,15},{10,... | collective-permute-start | bytes 503816 | tf_op jit(solution)/shard_map/ppermute | solution.py:40
  240.9 5.1 %collective-permute-start.22 = (bf16[32,5248]{1,0:T(8,128)(2,1)S(1)}, bf16[32,5248]{1,0:T(8,128)(2,1)S(1)}, u32[]{:S(2)}, u32[]{:S(2)}) collective-permute-start(bf16[32,5248]{1,0:T(8,128)(2,1)S(1)} %maximum_select_fusion.2), channel_id=1, source_target_pairs={{0,2},{1,3},{2,0},{3,1},{4,6},{5,7},{6,4},{7,5},{8,10},{9,11},{10,... | collective-permute-start | bytes 1007624 | tf_op jit(solution)/shard_map/ppermute | solution.py:40
  247.1 7.0 %collective-permute-done.22 = bf16[32,5248]{1,0:T(8,128)(2,1)S(1)} collective-permute-done((bf16[32,5248]{1,0:T(8,128)(2,1)S(1)}, bf16[32,5248]{1,0:T(8,128)(2,1)S(1)}, u32[]{:S(2)}, u32[]{:S(2)}) %collective-permute-start.22) | collective-permute-done | bytes 335904 | tf_op jit(solution)/shard_map/ppermute | solution.py:40
  257.0 8.0 %collective-permute-done.23 = bf16[64,5248]{1,0:T(8,128)(2,1)S(1)} collective-permute-done((bf16[64,5248]{1,0:T(8,128)(2,1)S(1)}, bf16[64,5248]{1,0:T(8,128)(2,1)S(1)}, u32[]{:S(2)}, u32[]{:S(2)}) %collective-permute-start.23) | collective-permute-done | bytes 671776 | tf_op jit(solution)/shard_map/ppermute | solution.py:40
  269.5 13.8 %collective-permute-done.24.piece.small = bf16[128,5248]{1,0:T(8,128)(2,1)S(1)} collective-permute-done((bf16[128,5248]{1,0:T(8,128)(2,1)S(1)}, bf16[128,5248]{1,0:T(8,128)(2,1)S(1)}, u32[]{:S(2)}, u32[]{:S(2)}) %collective-permute-start.24) | collective-permute-done | bytes 1343520 | tf_op jit(solution)/shard_map/ppermute | solution.py:40
  (189 shorter events, 103.6 us)
Async XLA Ops:
  4.1 33.6 %all-to-all-start = ((s32[8,1,3]{2,1,0:T(1,128)}), s32[8,1,3]{2,1,0:T(1,128)S(1)}, u32[]{:S(2)}, u32[]{:S(2)}) async-start(s32[8,1,3]{2,1,0:T(1,128)} %copy.81), calls=%async_computation | async-start | bytes 8192 | tf_op jit(solution)/shard_map/all_to_all | solution.py:375
  13.1 25.0 %collective-permute-start.1 = (bf16[24,1,512]{2,1,0:T(2,128)(2,1)}, bf16[24,1,512]{2,1,0:T(2,128)(2,1)S(1)}, u32[]{:S(2)}, u32[]{:S(2)}) collective-permute-start(bf16[24,1,512]{2,1,0:T(2,128)(2,1)} %get-tuple-element.103), channel_id=1, source_target_pairs={{1,0},{2,1},{3,2},{4,3},{5,4},{6,5},{7,6},{0,7},{9,8},{10,9},{11,1... | collective-permute-start | bytes 73736 | tf_op jit(solution)/shard_map/ppermute | solution.py:89
  17.8 20.3 %collective-permute-start = (bf16[24,1,512]{2,1,0:T(2,128)(2,1)}, bf16[24,1,512]{2,1,0:T(2,128)(2,1)S(1)}, u32[]{:S(2)}, u32[]{:S(2)}) collective-permute-start(bf16[24,1,512]{2,1,0:T(2,128)(2,1)} %get-tuple-element.102), channel_id=1, source_target_pairs={{0,1},{1,2},{2,3},{3,4},{4,5},{5,6},{6,7},{7,0},{8,9},{9,10},{10,1... | collective-permute-start | bytes 73736 | tf_op jit(solution)/shard_map/ppermute | solution.py:88
  22.2 34.6 %collective-permute-start.8 = (bf16[616,384]{1,0:T(8,128)(2,1)}, bf16[616,384]{1,0:T(8,128)(2,1)S(1)}, u32[]{:S(2)}, u32[]{:S(2)}) collective-permute-start(bf16[616,384]{1,0:T(8,128)(2,1)} %get-tuple-element.42), channel_id=1, source_target_pairs={{0,1},{1,0},{2,3},{3,2},{4,5},{5,4},{6,7},{7,6},{8,9},{9,8},{10,11... | collective-permute-start | bytes 1419272 | tf_op jit(solution)/shard_map/ppermute | solution.py:40
  22.5 36.7 %collective-permute-start.9 = (bf16[616,384]{1,0:T(8,128)(2,1)S(1)}, bf16[616,384]{1,0:T(8,128)(2,1)S(1)}, u32[]{:S(2)}, u32[]{:S(2)}) collective-permute-start(bf16[616,384]{1,0:T(8,128)(2,1)S(1)} %get-tuple-element.43), channel_id=1, source_target_pairs={{0,2},{1,3},{2,0},{3,1},{4,6},{5,7},{6,4},{7,5},{8,10},{9,11},{10,... | collective-permute-start | bytes 1419272 | tf_op jit(solution)/shard_map/ppermute | solution.py:40
  24.0 51.2 %collective-permute-start.10 = (bf16[616,384]{1,0:T(8,128)(2,1)}, bf16[616,384]{1,0:T(8,128)(2,1)S(1)}, u32[]{:S(2)}, u32[]{:S(2)}) collective-permute-start(bf16[616,384]{1,0:T(8,128)(2,1)} %get-tuple-element.44), channel_id=1, source_target_pairs={{0,3},{1,2},{2,1},{3,0},{4,7},{5,6},{6,5},{7,4},{8,11},{9,10},{10,... | collective-permute-start | bytes 1419272 | tf_op jit(solution)/shard_map/ppermute | solution.py:40
  43.2 54.9 %collective-permute-start.5 = (bf16[616,384]{1,0:T(8,128)(2,1)}, bf16[616,384]{1,0:T(8,128)(2,1)S(1)}, u32[]{:S(2)}, u32[]{:S(2)}) collective-permute-start(bf16[616,384]{1,0:T(8,128)(2,1)} %get-tuple-element.38), channel_id=1, source_target_pairs={{0,4},{1,5},{2,6},{3,7},{4,0},{5,1},{6,2},{7,3},{8,12},{9,13},{10,... | collective-permute-start | bytes 1419272 | tf_op jit(solution)/shard_map/ppermute | solution.py:40
  45.6 61.9 %collective-permute-start.6 = (bf16[616,384]{1,0:T(8,128)(2,1)}, bf16[616,384]{1,0:T(8,128)(2,1)S(1)}, u32[]{:S(2)}, u32[]{:S(2)}) collective-permute-start(bf16[616,384]{1,0:T(8,128)(2,1)} %get-tuple-element.39), channel_id=1, source_target_pairs={{0,5},{1,4},{2,7},{3,6},{4,1},{5,0},{6,3},{7,2},{8,13},{9,12},{10,... | collective-permute-start | bytes 1419272 | tf_op jit(solution)/shard_map/ppermute | solution.py:40
  56.8 50.7 %collective-permute-start.7 = (bf16[616,384]{1,0:T(8,128)(2,1)}, bf16[616,384]{1,0:T(8,128)(2,1)S(1)}, u32[]{:S(2)}, u32[]{:S(2)}) collective-permute-start(bf16[616,384]{1,0:T(8,128)(2,1)} %get-tuple-element.40), channel_id=1, source_target_pairs={{0,6},{1,7},{2,4},{3,5},{4,2},{5,3},{6,0},{7,1},{8,14},{9,15},{10,... | collective-permute-start | bytes 1419272 | tf_op jit(solution)/shard_map/ppermute | solution.py:40
  59.2 52.9 %collective-permute-start.4 = (bf16[616,384]{1,0:T(8,128)(2,1)}, bf16[616,384]{1,0:T(8,128)(2,1)S(1)}, u32[]{:S(2)}, u32[]{:S(2)}) collective-permute-start(bf16[616,384]{1,0:T(8,128)(2,1)} %get-tuple-element.37), channel_id=1, source_target_pairs={{0,7},{1,6},{2,5},{3,4},{4,3},{5,2},{6,1},{7,0},{8,15},{9,14},{10,... | collective-permute-start | bytes 1419272 | tf_op jit(solution)/shard_map/ppermute | solution.py:40
  122.6 42.6 %collective-permute-start.11 = (bf16[256,4608]{1,0:T(8,128)(2,1)}, bf16[256,4608]{1,0:T(8,128)(2,1)}, u32[]{:S(2)}, u32[]{:S(2)}) collective-permute-start(bf16[256,4608]{1,0:T(8,128)(2,1)} %convolution_convert_fusion), channel_id=1, source_target_pairs={{0,8},{1,9},{2,10},{3,11},{4,12},{5,13},{6,14},{7,15},{8,0},{9,1},... | collective-permute-start | bytes 7077896 | tf_op jit(solution)/shard_map/ppermute | solution.py:40
  169.9 19.5 %collective-permute-start.17 = (bf16[128,5248]{1,0:T(8,128)(2,1)}, bf16[128,5248]{1,0:T(8,128)(2,1)}, u32[]{:S(2)}, u32[]{:S(2)}) collective-permute-start(bf16[128,5248]{1,0:T(8,128)(2,1)} %pad_maximum_fusion.6), channel_id=1, source_target_pairs={{0,16},{1,17},{2,18},{3,19},{4,20},{5,21},{6,22},{7,23},{8,9},{9,8... | collective-permute-start | bytes 4030472 | tf_op jit(solution)/shard_map/ppermute | solution.py:40
  192.7 11.3 %collective-permute-start.18 = (bf16[64,5248]{1,0:T(8,128)(2,1)S(1)}, bf16[64,5248]{1,0:T(8,128)(2,1)S(1)}, u32[]{:S(2)}, u32[]{:S(2)}) collective-permute-start(bf16[64,5248]{1,0:T(8,128)(2,1)S(1)} %get-tuple-element.72), channel_id=1, source_target_pairs={{0,1},{1,0},{2,3},{3,2},{4,5},{5,4},{6,7},{7,6},{8,24},{9,25},{10,... | collective-permute-start | bytes 2015240 | tf_op jit(solution)/shard_map/ppermute | solution.py:40
  196.2 25.8 %collective-permute-start.14 = (bf16[24,1,512]{2,1,0:T(2,128)(2,1)S(1)}, bf16[24,1,512]{2,1,0:T(2,128)(2,1)S(1)}, u32[]{:S(2)}, u32[]{:S(2)}) collective-permute-start(bf16[24,1,512]{2,1,0:T(2,128)(2,1)S(1)} %get-tuple-element.99), channel_id=1, source_target_pairs={{1,0},{2,1},{3,2},{4,3},{5,4},{6,5},{7,6},{0,7},{9,8},{10,9},{11,1... | collective-permute-start | bytes 73736 | tf_op jit(solution)/shard_map/ppermute | solution.py:89
  199.7 22.3 %collective-permute-start.13 = (bf16[24,1,512]{2,1,0:T(2,128)(2,1)S(1)}, bf16[24,1,512]{2,1,0:T(2,128)(2,1)S(1)}, u32[]{:S(2)}, u32[]{:S(2)}) collective-permute-start(bf16[24,1,512]{2,1,0:T(2,128)(2,1)S(1)} %get-tuple-element.98), channel_id=1, source_target_pairs={{0,1},{1,2},{2,3},{3,4},{4,5},{5,6},{6,7},{7,0},{8,9},{9,10},{10,1... | collective-permute-start | bytes 73736 | tf_op jit(solution)/shard_map/ppermute | solution.py:88
  204.2 20.9 %collective-permute-start.19 = (bf16[32,5248]{1,0:T(8,128)(2,1)S(1)}, bf16[32,5248]{1,0:T(8,128)(2,1)S(1)}, u32[]{:S(2)}, u32[]{:S(2)}) collective-permute-start(bf16[32,5248]{1,0:T(8,128)(2,1)S(1)} %get-tuple-element.74), channel_id=1, source_target_pairs={{0,2},{1,3},{2,0},{3,1},{4,6},{5,7},{6,4},{7,5},{8,10},{9,11},{10,... | collective-permute-start | bytes 1007624 | tf_op jit(solution)/shard_map/ppermute | solution.py:40
  222.0 14.1 %collective-permute-start.15 = (bf16[1,66,512]{2,1,0:T(8,128)(2,1)S(1)}, bf16[1,66,512]{2,1,0:T(8,128)(2,1)S(1)}, u32[]{:S(2)}, u32[]{:S(2)}) collective-permute-start(bf16[1,66,512]{2,1,0:T(8,128)(2,1)S(1)} %get-tuple-element.90), channel_id=1, source_target_pairs={{0,8},{8,16},{16,24},{1,9},{9,17},{17,25},{2,10},{10,18},{18,26},{... | collective-permute-start | bytes 202760 | tf_op jit(solution)/shard_map/ppermute | solution.py:88
  223.3 12.8 %collective-permute-start.16 = (bf16[1,66,512]{2,1,0:T(8,128)(2,1)S(1)}, bf16[1,66,512]{2,1,0:T(8,128)(2,1)S(1)}, u32[]{:S(2)}, u32[]{:S(2)}) collective-permute-start(bf16[1,66,512]{2,1,0:T(8,128)(2,1)S(1)} %get-tuple-element.91), channel_id=1, source_target_pairs={{8,0},{16,8},{24,16},{9,1},{17,9},{25,17},{10,2},{18,10},{26,18},{... | collective-permute-start | bytes 202760 | tf_op jit(solution)/shard_map/ppermute | solution.py:89
  232.5 8.3 %collective-permute-start.21 = (bf16[16,5248]{1,0:T(8,128)(2,1)S(1)}, bf16[16,5248]{1,0:T(8,128)(2,1)S(1)}, u32[]{:S(2)}, u32[]{:S(2)}) collective-permute-start(bf16[16,5248]{1,0:T(8,128)(2,1)S(1)} %fusion.36), channel_id=1, source_target_pairs={{0,6},{1,7},{2,4},{3,5},{4,2},{5,3},{6,0},{7,1},{8,14},{9,15},{10,... | collective-permute-start | bytes 503816 | tf_op jit(solution)/shard_map/ppermute | solution.py:40
  240.9 13.2 %collective-permute-start.22 = (bf16[32,5248]{1,0:T(8,128)(2,1)S(1)}, bf16[32,5248]{1,0:T(8,128)(2,1)S(1)}, u32[]{:S(2)}, u32[]{:S(2)}) collective-permute-start(bf16[32,5248]{1,0:T(8,128)(2,1)S(1)} %maximum_select_fusion.2), channel_id=1, source_target_pairs={{0,2},{1,3},{2,0},{3,1},{4,6},{5,7},{6,4},{7,5},{8,10},{9,11},{10,... | collective-permute-start | bytes 1007624 | tf_op jit(solution)/shard_map/ppermute | solution.py:40
  254.2 10.8 %collective-permute-start.23 = (bf16[64,5248]{1,0:T(8,128)(2,1)S(1)}, bf16[64,5248]{1,0:T(8,128)(2,1)S(1)}, u32[]{:S(2)}, u32[]{:S(2)}) collective-permute-start(bf16[64,5248]{1,0:T(8,128)(2,1)S(1)} %maximum_select_fusion.1), channel_id=1, source_target_pairs={{0,1},{1,0},{2,3},{3,2},{4,5},{5,4},{6,7},{7,6},{8,24},{9,25},{10,... | collective-permute-start | bytes 2015240 | tf_op jit(solution)/shard_map/ppermute | solution.py:40
  265.3 18.0 %collective-permute-start.24 = (bf16[128,5248]{1,0:T(8,128)(2,1)S(1)}, bf16[128,5248]{1,0:T(8,128)(2,1)S(1)}, u32[]{:S(2)}, u32[]{:S(2)}) collective-permute-start(bf16[128,5248]{1,0:T(8,128)(2,1)S(1)} %maximum_select_fusion.piece.small), channel_id=1, source_target_pairs={{0,16},{1,17},{2,18},{3,19},{4,20},{5,21},{6,22},{7,23},{8,9},{9,8... | collective-permute-start | bytes 4030472 | tf_op jit(solution)/shard_map/ppermute | solution.py:40
  269.4 19.8 %collective-permute-start.26 = (bf16[128,5248]{1,0:T(8,128)(2,1)S(1)}, bf16[128,5248]{1,0:T(8,128)(2,1)S(1)}, u32[]{:S(2)}, u32[]{:S(2)}) collective-permute-start(bf16[128,5248]{1,0:T(8,128)(2,1)S(1)} %maximum_select_fusion.piece.small), channel_id=1, source_target_pairs={{0,8},{1,9},{2,10},{3,11},{4,12},{5,13},{6,14},{7,15},{8,0},{9,1},... | collective-permute-start | bytes 4030472 | tf_op jit(solution)/shard_map/ppermute | solution.py:40
  283.3 9.5 %collective-permute-start.25 = (bf16[128,5248]{1,0:T(8,128)(2,1)S(1)}, bf16[128,5248]{1,0:T(8,128)(2,1)S(1)}, u32[]{:S(2)}, u32[]{:S(2)}) collective-permute-start(bf16[128,5248]{1,0:T(8,128)(2,1)S(1)} %collective-permute-done.24.piece.small), channel_id=1, source_target_pairs={{0,8},{1,9},{2,10},{3,11},{4,12},{5,13},{6,14},{7,15},{8,0},{9,1},... | collective-permute-start | bytes 4030472 | tf_op jit(solution)/shard_map/ppermute | solution.py:40
  (38 other events, 295.7 us)

commit v6 on v4

--- a/solution.py
+++ b/solution.py
@@ -175,10 +175,16 @@
         else:
             spread[...] = refs[count + 3][...]
         for k in range(count):
-            pre = jnp.dot(w[...], xs[k][...], preferred_element_type=jnp.float32)
-            s = jax.nn.sigmoid(pre)
-            slope[k] = (s * (1.0 + pre * (1.0 - s))).astype(jnp.bfloat16)
-            enc[...] = (pre * s).astype(jnp.bfloat16)
+
+            def encode(c, _, k=k):
+                span = lanes(c, width // 2)
+                pre = jnp.dot(w[span], xs[k][...], preferred_element_type=jnp.float32)
+                s = jax.nn.sigmoid(pre)
+                slope[k, span] = (s * (1.0 + pre * (1.0 - s))).astype(jnp.bfloat16)
+                enc[span] = (pre * s).astype(jnp.bfloat16)
+                return 0
+
+            lax.fori_loop(0, 2, encode, 0)
 
             def add(j, _, k=k):
                 code = meta_ref[(first + k) * MOST + j]
@@ -209,6 +215,7 @@
         shape_of((patches, width, cells), jnp.float32),
         shape_of((count, width, MOST * rows), jnp.bfloat16),
     ]
+    outs = [pltpu.HBM(o.shape, o.dtype) if last or n == 1 else o for n, o in enumerate(outs)]
     if last:
         outs.append(shape_of((width, patches * cells), jnp.bfloat16))
     ins = [*arrived, weight_t, kernels, gain_col] + ([] if before is None else [before])
@@ -227,11 +234,32 @@
     def body(meta_ref, *refs):
         xs = refs[:count]
         slos = refs[count : count + groups]
-        kern, g, spr, dn, out, dsp, dpre = refs[count + groups :]
+        spr, dn, kern, g, out, dsp, dpre, xbuf, sbuf, spr_buf, dn_buf, sems, patch_sems = refs[
+            count + groups :
+        ]
+
+        def field(q):
+            return (
+                pltpu.make_async_copy(spr.at[q], spr_buf.at[q], patch_sems.at[2 * q]),
+                pltpu.make_async_copy(dn.at[:, lanes(q, cells)], dn_buf.at[q], patch_sems.at[2 * q + 1]),
+            )
+
+        for q in range(patches):
+            for one in field(q):
+                one.start()
+        copies = []
+        for k in range(count):
+            n, at = place_of[k]
+            copies.append(pltpu.make_async_copy(xs[k], xbuf.at[k], sems.at[2 * k]))
+            copies.append(pltpu.make_async_copy(slos[n].at[at], sbuf.at[k], sems.at[2 * k + 1]))
+        for one in copies:
+            one.start()
 
         def unnorm(q, total):
-            cell = spr[q]
-            d = dn[:, lanes(q, cells)]
+            for one in field(q):
+                one.wait()
+            cell = spr_buf[q]
+            d = dn_buf[q]
             r = lax.rsqrt(jnp.mean(cell * cell, axis=0, keepdims=True) + EPS)
             unit = cell * r
             dg = d * g[...]
@@ -242,10 +270,12 @@
         total = lax.fori_loop(0, patches, unnorm, jnp.zeros((width, 1), jnp.float32))
         out[...] = jnp.zeros_like(out)
         out[:, channels : channels + 1] = total
-        for k in range(count):
-            n, at = place_of[k]
-
-            def back(j, _, k=k, n=n, at=at):
+
+        def arrival(k, _):
+            pltpu.make_async_copy(xbuf.at[k], xbuf.at[k], sems.at[2 * k]).wait()
+            pltpu.make_async_copy(sbuf.at[k], sbuf.at[k], sems.at[2 * k + 1]).wait()
+
+            def back(j, _):
                 code = meta_ref[k * MOST + j]
                 span = lanes(j, rows)
 
@@ -257,7 +287,7 @@
                         preferred_element_type=jnp.float32,
                     ).astype(jnp.bfloat16)
                     dpre[:, span] = (
-                        drow.astype(jnp.float32) * slos[n][at, :, span].astype(jnp.float32)
+                        drow.astype(jnp.float32) * sbuf[k, :, span].astype(jnp.float32)
                     ).astype(jnp.bfloat16)
 
                 @pl.when(code < 0)
@@ -267,15 +297,27 @@
                 return 0
 
             lax.fori_loop(0, MOST, back, 0)
-            out[:, :channels] += nt(dpre[...], xs[k][...])
-
-    ins = [*arrived, *slopes, kernels_t, gain_col, spread, d_normed_t]
+            out[:, :channels] += nt(dpre[...], xbuf[k])
+            return 0
+
+        lax.fori_loop(0, count, arrival, 0)
+
+    held = [pltpu.with_memory_space_constraint(x, pltpu.HBM) for x in (*slopes, spread, d_normed_t)]
+    ins = [*arrived, *held, kernels_t, gain_col]
     outs = [shape_of((width, (channels // LANES + 1) * LANES), jnp.float32)]
     scratch = [
         pltpu.VMEM((patches, width, cells), jnp.bfloat16),
         pltpu.VMEM((width, MOST * rows), jnp.bfloat16),
+        pltpu.VMEM((count, channels, MOST * rows), jnp.bfloat16),
+        pltpu.VMEM((count, width, MOST * rows), jnp.bfloat16),
+        pltpu.VMEM((patches, width, cells), jnp.float32),
+        pltpu.VMEM((patches, width, cells), jnp.float32),
+        pltpu.SemaphoreType.DMA((2 * count,)),
+        pltpu.SemaphoreType.DMA((2 * patches,)),
     ]
-    return call(body, meta, ins, outs, scratch=scratch)[0]
+    far = [pl.BlockSpec(memory_space=pltpu.HBM)] * (count + groups + 2)
+    in_specs = far + [whole(a.shape) for a in ins[count + groups + 2 :]]
+    return call(body, meta, ins, outs, in_specs=in_specs, scratch=scratch)[0]
 
 
 def place(quarter, part, taps, lane, channels, scale, into=None):
@@ -381,6 +423,8 @@
     d_normed_t = nt(weight_all, windows)
 
     meta, d_normed_t, windows = lax.optimization_barrier((meta, d_normed_t, windows))
+    arrived = [pltpu.with_memory_space_constraint(x, pltpu.HBM) for x in arrived]
+    d_normed_t = pltpu.with_memory_space_constraint(d_normed_t, pltpu.HBM)
     patches = tile_rows // PH * (tile_cols // PW)
     gain_col = gain.reshape(width, 1)
     weight_t = encoder_weight.T
@@ -436,7 +480,8 @@
             result_sum = result_sum + jnp.dot(
                 window, conv_weight[a, b], preferred_element_type=jnp.float32
             )
-    conv_out = result_sum.reshape(tile_rows, tile_cols, width).astype(jnp.bfloat16)
+        if a == 2:
+            conv_out = result_sum.reshape(tile_rows, tile_cols, width).astype(jnp.bfloat16)
     part = (keep + came.astype(jnp.float32)).astype(jnp.bfloat16)
     for n in range(len(plan) - 1, 1, -1):
         other = step(part, plan[n][0], lats, lons)

time: 268 us -> 261 us (0.974)
  waiting for transfers between devices: 72.5 us -> 59.9 us
  Pallas kernels: 42 us -> 48.4 us
    ppermute x21, waiting for transfers between devices: 68 us -> 55.4 us  [exchange(): return lax.ppermute(value, AXES, pairs)]
    pallas_call x10, Pallas kernels: 42 us -> 48.4 us  [call(): pl.pallas_call(body, out_shape=outs, grid_spec=pltpu.PrefetchScalarGridSp...]
    unnamed x69 -> x53, local copies, waits for them, and re-layouts: 26.5 us -> 24.3 us
  transfers between devices with their start and end apart: 30 -> 30, of which waited for: 11 -> 9; matrix products, arithmetic and copies ran while one was open for 25% -> 27% of each run, Pallas kernels for 14% -> 16%
where the time goes in v6:
time: 261 us; the launch traced here: 257 us
  waiting for transfers between devices  59.9 us (23%)
  starting transfers between devices  53.1 us (20%)
  Pallas kernels  48.4 us (19%)
  local copies, waits for them, and re-layouts  38.6 us (15%)
  matrix products  34.6 us (13%)
  other arithmetic  20.5 us (8%)
    ppermute x21, waiting for transfers between devices, exchange(): return lax.ppermute(value, AXES, pairs)  55.4 us
    pallas_call x10, Pallas kernels, call(): pl.pallas_call(body, out_shape=outs, grid_spec=pltpu.PrefetchScalarGridSp...  48.4 us
    ppermute x21, starting transfers between devices, exchange(): return lax.ppermute(value, AXES, pairs)  32.8 us
    unnamed x53, local copies, waits for them, and re-layouts  24.3 us
    dot_general x1, matrix products, nt(): lax.dot_general(left, right, (((1,), (1,)), ((), ())), preferred_element_...  12.3 us
    ppermute x4, starting transfers between devices, padded_2(): after = lax.ppermute(leading, axis, down)  10.4 us
    dot_general x9, matrix products, shards(): jnp.dot(window, conv_weight[a, b], preferred_element_type=jnp.float32)  10.1 us
    concatenate x5, other arithmetic, padded_2(): shard = jnp.concatenate([before, shard, after], axis=dim)  7.95 us
  transfers between devices with their start and end apart: 30, of which 9 were waited for; matrix products, arithmetic and copies ran while one was open for 27% of the time, Pallas kernels for 16%

profile of v6, /device:TPU:0, one launch (start us, length us, event | category | flops | bytes accessed | tf_op | source)
XLA Modules:
  0.0 256.5 jit_solution(17056201962442241378)
XLA Ops:
  4.1 7.3 %all-to-all-start = ((s32[8,1,3]{2,1,0:T(1,128)}), s32[8,1,3]{2,1,0:T(1,128)S(1)}, u32[]{:S(2)}, u32[]{:S(2)}) async-start(s32[8,1,3]{2,1,0:T(1,128)} %copy.81), calls=%async_computation | async-start | bytes 8192 | tf_op jit(solution)/shard_map/all_to_all | solution.py:404
  12.5 4.8 %collective-permute-start.1 = (bf16[24,1,512]{2,1,0:T(2,128)(2,1)S(1)}, bf16[24,1,512]{2,1,0:T(2,128)(2,1)S(1)}, u32[]{:S(2)}, u32[]{:S(2)}) collective-permute-start(bf16[24,1,512]{2,1,0:T(2,128)(2,1)S(1)} %get-tuple-element.105), channel_id=1, source_target_pairs={{1,0},{2,1},{3,2},{4,3},{5,4},{6,5},{7,6},{0,7},{9,8},{10,9},{11,1... | collective-permute-start | bytes 73736 | tf_op jit(solution)/shard_map/ppermute | solution.py:89
  20.7 4.8 %collective-permute-start.4 = (bf16[616,384]{1,0:T(8,128)(2,1)S(1)}, bf16[616,384]{1,0:T(8,128)(2,1)}, u32[]{:S(2)}, u32[]{:S(2)}) collective-permute-start(bf16[616,384]{1,0:T(8,128)(2,1)S(1)} %get-tuple-element.38), channel_id=1, source_target_pairs={{0,7},{1,6},{2,5},{3,4},{4,3},{5,2},{6,1},{7,0},{8,15},{9,14},{10,... | collective-permute-start | bytes 1419272 | tf_op jit(solution)/shard_map/ppermute | solution.py:40
  29.8 6.6 %copy.93 = bf16[3,3,512,512]{2,3,1,0:T(8,128)(2,1)} copy(bf16[3,3,512,512]{3,2,1,0:T(8,128)(2,1)} %param.16) | data formatting | bytes 9437184 | tf_op args[7]
  44.2 4.2 %collective-permute-start.8 = (bf16[616,384]{1,0:T(8,128)(2,1)S(1)}, bf16[616,384]{1,0:T(8,128)(2,1)S(1)}, u32[]{:S(2)}, u32[]{:S(2)}) collective-permute-start(bf16[616,384]{1,0:T(8,128)(2,1)S(1)} %copy-done.4), channel_id=1, source_target_pairs={{0,1},{1,0},{2,3},{3,2},{4,5},{5,4},{6,7},{7,6},{8,9},{9,8},{10,11... | collective-permute-start | bytes 1419272 | tf_op jit(solution)/shard_map/ppermute | solution.py:40
  54.8 5.1 %copy-done.14 = bf16[1536,4608]{1,0:T(8,128)(2,1)} copy-done((bf16[1536,4608]{1,0:T(8,128)(2,1)}, bf16[1536,4608]{1,0:T(8,128)(2,1)S(1)}, u32[]{:S(2)}) %copy-start.14) | copy-done | bytes 14155800
  67.8 8.4 %collective-permute-start.10 = (bf16[616,384]{1,0:T(8,128)(2,1)}, bf16[616,384]{1,0:T(8,128)(2,1)S(1)}, u32[]{:S(2)}, u32[]{:S(2)}) collective-permute-start(bf16[616,384]{1,0:T(8,128)(2,1)} %get-tuple-element.45), channel_id=1, source_target_pairs={{0,3},{1,2},{2,1},{3,0},{4,7},{5,6},{6,5},{7,4},{8,11},{9,10},{10,... | collective-permute-start | bytes 1419272 | tf_op jit(solution)/shard_map/ppermute | solution.py:40
  76.2 12.3 %convolution_bitcast_fusion.refs_12_ = f32[512,1536]{1,0:T(8,128)} fusion(bf16[1536,4608]{1,0:T(8,128)(2,1)} %constant_dynamic-update-slice_fusion, bf16[512,4608]{0,1:T(8,128)(2,1)S(1)} %bitcast.196), kind=kOutput, calls=%fused_computation.11 | convolution fusion | flops 7247757312 | bytes 22020096 | tf_op jit(solution)/shard_map/dot_general | solution.py:126
  88.5 15.5 %collective-permute-done.10.refs_3_ = bf16[616,384]{1,0:T(8,128)(2,1)S(1)} collective-permute-done((bf16[616,384]{1,0:T(8,128)(2,1)}, bf16[616,384]{1,0:T(8,128)(2,1)S(1)}, u32[]{:S(2)}, u32[]{:S(2)}) %collective-permute-start.10) | collective-permute-done | bytes 473120 | tf_op jit(solution)/shard_map/ppermute | solution.py:40
  104.8 9.0 %shard_map.122 = (f32[12,512,128]{2,1,0:T(8,128)S(1)}, bf16[4,512,384]{2,1,0:T(8,128)(2,1)}) custom-call(s32[24]{0:T(128)S(1)} %reshape.354.meta_ref, bf16[616,384]{1,0:T(8,128)(2,1)} %copy-done.2, bf16[616,384]{1,0:T(8,128)(2,1)} %copy-done.9, bf16[616,384]{1,0:T(8,128)(2,1)} %copy-done.10, bf16[616,384]{1,0:T(8,128)(2,1)} %copy-done.11, ...), custom_call_target="tpu_custom_call" | custom-call | tf_op jit(solution)/shard_map/pallas_call | solution.py:106
  114.6 7.2 %shard_map.123 = (f32[12,512,128]{2,1,0:T(8,128)S(1)}, bf16[3,512,384]{2,1,0:T(8,128)(2,1)}) custom-call(s32[24]{0:T(128)S(1)} %reshape.354.meta_ref, bf16[616,384]{1,0:T(8,128)(2,1)} %collective-permute-done.5.refs_0_.refs_4_, bf16[616,384]{1,0:T(8,128)(2,1)} %collective-permute-done.6.refs_1_.refs_5_, bf16[616,384]{1,0:T(8,128)(2,1)} %copy-done.12, ...), custom_call_target="tpu_custom_call" | custom-call | tf_op jit(solution)/shard_map/pallas_call | solution.py:106
  121.8 6.7 %shard_map.124 = (f32[12,512,128]{2,1,0:T(8,128)}, bf16[1,512,384]{2,1,0:T(8,128)(2,1)}, bf16[512,1536]{1,0:T(8,128)(2,1)S(1)}) custom-call(s32[24]{0:T(128)S(1)} %reshape.354.meta_ref, bf16[616,384]{1,0:T(8,128)(2,1)} %collective-permute-done.4.refs_0_.refs_7_, bf16[512,616]{1,0:T(8,128)(2,1)S(1)} %bitcast.152, bf16[16,128,128]{2,1,0:T(8,128)(2,1)S(1)} %copy-done.1, ...), custom_call_target="tpu_custom_call" | custom-call | tf_op jit(solution)/shard_map/pallas_call | solution.py:106
  128.5 5.1 %convolution_convert_fusion = bf16[256,4608]{1,0:T(8,128)(2,1)} fusion(bf16[1536,4608]{1,0:T(8,128)(2,1)S(1)} %copy-done.15, bf16[2,256,1536]{2,1,0:T(8,128)(2,1)S(1)} %bitcast.155, s32[]{:T(128)S(6)} %select_n.111), kind=kOutput, calls=%fused_computation.2 | convolution fusion | flops 3625058304 | bytes 17301508 | tf_op jit(solution)/shard_map/dot_general | solution.py:445
  133.7 7.0 %fusion = f32[2,128,4608]{2,1,0:T(8,128)S(1)} fusion(bf16[2,128,1536]{2,1,0:T(8,128)(2,1)S(1)} %bitcast.204, bf16[1536,4608]{1,0:T(8,128)(2,1)} %constant_dynamic-update-slice_fusion), kind=kOutput, calls=%fused_computation | convolution fusion | flops 3623878656 | bytes 19660800 | tf_op jit(solution)/shard_map/dot_general | solution.py:448
  140.8 4.0 %convert_add_fusion = (f32[1,128,4608]{2,1,0:T(8,128)}, bf16[128,4608]{1,0:T(8,128)(2,1)}) fusion(f32[2,128,4608]{2,1,0:T(8,128)S(1)} %fusion, s32[]{:T(128)S(6)} %select_n.117, bf16[2,128,4608]{2,1,0:T(8,128)(2,1)} %bitcast.40, s32[]{:T(128)S(6)} %select_n.110), kind=kLoop, calls=%fused_computation.13 | loop fusion | flops 2949120 | bytes 10616840 | tf_op jit(solution)/shard_map/add | solution.py:77
  146.5 15.3 %shard_map.125 = f32[512,640]{1,0:T(8,128)S(1)} custom-call(s32[24]{0:T(128)S(1)} %reshape.354.meta_ref, bf16[616,384]{1,0:T(8,128)(2,1)} %copy-done.2, bf16[616,384]{1,0:T(8,128)(2,1)} %copy-done.9, bf16[616,384]{1,0:T(8,128)(2,1)} %copy-done.10, bf16[616,384]{1,0:T(8,128)(2,1)} %copy-done.11, bf16[616,384]{1,0:T(8,128)(2,1)} %collective-permute-done.5.refs_0_.refs_4_, ...), custom_call_target="tpu_custom_call" | custom-call | tf_op jit(solution)/shard_map/pallas_call | solution.py:106
  170.6 3.1 %collective-permute-done.18 = bf16[128,640]{1,0:T(8,128)(2,1)} collective-permute-done((bf16[128,640]{1,0:T(8,128)(2,1)}, bf16[128,640]{1,0:T(8,128)(2,1)}, u32[]{:S(2)}, u32[]{:S(2)}) %collective-permute-start.18) | collective-permute-done | bytes 163872 | tf_op jit(solution)/shard_map/ppermute | solution.py:40
  175.7 3.1 %collective-permute-start.13 = (bf16[24,1,512]{2,1,0:T(2,128)(2,1)S(1)}, bf16[24,1,512]{2,1,0:T(2,128)(2,1)S(1)}, u32[]{:S(2)}, u32[]{:S(2)}) collective-permute-start(bf16[24,1,512]{2,1,0:T(2,128)(2,1)S(1)} %get-tuple-element.101), channel_id=1, source_target_pairs={{1,0},{2,1},{3,2},{4,3},{5,4},{6,5},{7,6},{0,7},{9,8},{10,9},{11,1... | collective-permute-start | bytes 73736 | tf_op jit(solution)/shard_map/ppermute | solution.py:89
  181.6 4.5 %collective-permute-done.12 = bf16[24,1,512]{2,1,0:T(2,128)(2,1)S(1)} collective-permute-done((bf16[24,1,512]{2,1,0:T(2,128)(2,1)S(1)}, bf16[24,1,512]{2,1,0:T(2,128)(2,1)S(1)}, u32[]{:S(2)}, u32[]{:S(2)}) %collective-permute-start.12) | collective-permute-done | bytes 24608 | tf_op jit(solution)/shard_map/ppermute | solution.py:88
  192.4 4.5 %collective-permute-done.22 = bf16[16,5248]{1,0:T(8,128)(2,1)S(1)} collective-permute-done((bf16[16,5248]{1,0:T(8,128)(2,1)S(1)}, bf16[16,5248]{1,0:T(8,128)(2,1)S(1)}, u32[]{:S(2)}, u32[]{:S(2)}) %collective-permute-start.22) | collective-permute-done | bytes 167968 | tf_op jit(solution)/shard_map/ppermute | solution.py:40
  201.7 4.3 %collective-permute-done.23 = bf16[16,5248]{1,0:T(8,128)(2,1)S(1)} collective-permute-done((bf16[16,5248]{1,0:T(8,128)(2,1)S(1)}, bf16[16,5248]{1,0:T(8,128)(2,1)S(1)}, u32[]{:S(2)}, u32[]{:S(2)}) %collective-permute-start.23) | collective-permute-done | bytes 167968 | tf_op jit(solution)/shard_map/ppermute | solution.py:40
  209.1 6.7 %collective-permute-done.24 = bf16[32,5248]{1,0:T(8,128)(2,1)S(1)} collective-permute-done((bf16[32,5248]{1,0:T(8,128)(2,1)S(1)}, bf16[32,5248]{1,0:T(8,128)(2,1)S(1)}, u32[]{:S(2)}, u32[]{:S(2)}) %collective-permute-start.24) | collective-permute-done | bytes 335904 | tf_op jit(solution)/shard_map/ppermute | solution.py:40
  219.7 7.0 %collective-permute-done.25 = bf16[64,5248]{1,0:T(8,128)(2,1)S(1)} collective-permute-done((bf16[64,5248]{1,0:T(8,128)(2,1)S(1)}, bf16[64,5248]{1,0:T(8,128)(2,1)S(1)}, u32[]{:S(2)}, u32[]{:S(2)}) %collective-permute-start.25) | collective-permute-done | bytes 671776 | tf_op jit(solution)/shard_map/ppermute | solution.py:40
  231.3 13.7 %collective-permute-done.26.piece.small = bf16[128,5248]{1,0:T(8,128)(2,1)S(1)} collective-permute-done((bf16[128,5248]{1,0:T(8,128)(2,1)S(1)}, bf16[128,5248]{1,0:T(8,128)(2,1)S(1)}, u32[]{:S(2)}, u32[]{:S(2)}) %collective-permute-start.26) | collective-permute-done | bytes 1343520 | tf_op jit(solution)/shard_map/ppermute | solution.py:40
  (169 shorter events, 85.0 us)
Async XLA Ops:
  4.1 33.9 %all-to-all-start = ((s32[8,1,3]{2,1,0:T(1,128)}), s32[8,1,3]{2,1,0:T(1,128)S(1)}, u32[]{:S(2)}, u32[]{:S(2)}) async-start(s32[8,1,3]{2,1,0:T(1,128)} %copy.81), calls=%async_computation | async-start | bytes 8192 | tf_op jit(solution)/shard_map/all_to_all | solution.py:404
  12.5 25.9 %collective-permute-start.1 = (bf16[24,1,512]{2,1,0:T(2,128)(2,1)S(1)}, bf16[24,1,512]{2,1,0:T(2,128)(2,1)S(1)}, u32[]{:S(2)}, u32[]{:S(2)}) collective-permute-start(bf16[24,1,512]{2,1,0:T(2,128)(2,1)S(1)} %get-tuple-element.105), channel_id=1, source_target_pairs={{1,0},{2,1},{3,2},{4,3},{5,4},{6,5},{7,6},{0,7},{9,8},{10,9},{11,1... | collective-permute-start | bytes 73736 | tf_op jit(solution)/shard_map/ppermute | solution.py:89
  17.2 21.1 %collective-permute-start = (bf16[24,1,512]{2,1,0:T(2,128)(2,1)S(1)}, bf16[24,1,512]{2,1,0:T(2,128)(2,1)S(1)}, u32[]{:S(2)}, u32[]{:S(2)}) collective-permute-start(bf16[24,1,512]{2,1,0:T(2,128)(2,1)S(1)} %get-tuple-element.104), channel_id=1, source_target_pairs={{0,1},{1,2},{2,3},{3,4},{4,5},{5,6},{6,7},{7,0},{8,9},{9,10},{10,1... | collective-permute-start | bytes 73736 | tf_op jit(solution)/shard_map/ppermute | solution.py:88
  20.7 101.1 %collective-permute-start.4 = (bf16[616,384]{1,0:T(8,128)(2,1)S(1)}, bf16[616,384]{1,0:T(8,128)(2,1)}, u32[]{:S(2)}, u32[]{:S(2)}) collective-permute-start(bf16[616,384]{1,0:T(8,128)(2,1)S(1)} %get-tuple-element.38), channel_id=1, source_target_pairs={{0,7},{1,6},{2,5},{3,4},{4,3},{5,2},{6,1},{7,0},{8,15},{9,14},{10,... | collective-permute-start | bytes 1419272 | tf_op jit(solution)/shard_map/ppermute | solution.py:40
  25.5 88.4 %collective-permute-start.5 = (bf16[616,384]{1,0:T(8,128)(2,1)S(1)}, bf16[616,384]{1,0:T(8,128)(2,1)}, u32[]{:S(2)}, u32[]{:S(2)}) collective-permute-start(bf16[616,384]{1,0:T(8,128)(2,1)S(1)} %get-tuple-element.39), channel_id=1, source_target_pairs={{0,4},{1,5},{2,6},{3,7},{4,0},{5,1},{6,2},{7,3},{8,12},{9,13},{10,... | collective-permute-start | bytes 1419272 | tf_op jit(solution)/shard_map/ppermute | solution.py:40
  25.5 88.4 %collective-permute-start.6 = (bf16[616,384]{1,0:T(8,128)(2,1)S(1)}, bf16[616,384]{1,0:T(8,128)(2,1)}, u32[]{:S(2)}, u32[]{:S(2)}) collective-permute-start(bf16[616,384]{1,0:T(8,128)(2,1)S(1)} %get-tuple-element.40), channel_id=1, source_target_pairs={{0,5},{1,4},{2,7},{3,6},{4,1},{5,0},{6,3},{7,2},{8,13},{9,12},{10,... | collective-permute-start | bytes 1419272 | tf_op jit(solution)/shard_map/ppermute | solution.py:40
  40.7 7.7 %collective-permute-start.2 = (bf16[1,66,512]{2,1,0:T(8,128)(2,1)S(1)}, bf16[1,66,512]{2,1,0:T(8,128)(2,1)S(1)}, u32[]{:S(2)}, u32[]{:S(2)}) collective-permute-start(bf16[1,66,512]{2,1,0:T(8,128)(2,1)S(1)} %get-tuple-element.97), channel_id=1, source_target_pairs={{8,0},{16,8},{24,16},{9,1},{17,9},{25,17},{10,2},{18,10},{26,18},{... | collective-permute-start | bytes 202760 | tf_op jit(solution)/shard_map/ppermute | solution.py:89
  44.2 22.0 %collective-permute-start.8 = (bf16[616,384]{1,0:T(8,128)(2,1)S(1)}, bf16[616,384]{1,0:T(8,128)(2,1)S(1)}, u32[]{:S(2)}, u32[]{:S(2)}) collective-permute-start(bf16[616,384]{1,0:T(8,128)(2,1)S(1)} %copy-done.4), channel_id=1, source_target_pairs={{0,1},{1,0},{2,3},{3,2},{4,5},{5,4},{6,7},{7,6},{8,9},{9,8},{10,11... | collective-permute-start | bytes 1419272 | tf_op jit(solution)/shard_map/ppermute | solution.py:40
  48.4 19.3 %collective-permute-start.9 = (bf16[616,384]{1,0:T(8,128)(2,1)S(1)}, bf16[616,384]{1,0:T(8,128)(2,1)S(1)}, u32[]{:S(2)}, u32[]{:S(2)}) collective-permute-start(bf16[616,384]{1,0:T(8,128)(2,1)S(1)} %get-tuple-element.44), channel_id=1, source_target_pairs={{0,2},{1,3},{2,0},{3,1},{4,6},{5,7},{6,4},{7,5},{8,10},{9,11},{10,... | collective-permute-start | bytes 1419272 | tf_op jit(solution)/shard_map/ppermute | solution.py:40
  66.3 47.5 %collective-permute-start.7 = (bf16[616,384]{1,0:T(8,128)(2,1)S(1)}, bf16[616,384]{1,0:T(8,128)(2,1)S(1)}, u32[]{:S(2)}, u32[]{:S(2)}) collective-permute-start(bf16[616,384]{1,0:T(8,128)(2,1)S(1)} %get-tuple-element.41), channel_id=1, source_target_pairs={{0,6},{1,7},{2,4},{3,5},{4,2},{5,3},{6,0},{7,1},{8,14},{9,15},{10,... | collective-permute-start | bytes 1419272 | tf_op jit(solution)/shard_map/ppermute | solution.py:40
  67.8 36.3 %collective-permute-start.10 = (bf16[616,384]{1,0:T(8,128)(2,1)}, bf16[616,384]{1,0:T(8,128)(2,1)S(1)}, u32[]{:S(2)}, u32[]{:S(2)}) collective-permute-start(bf16[616,384]{1,0:T(8,128)(2,1)} %get-tuple-element.45), channel_id=1, source_target_pairs={{0,3},{1,2},{2,1},{3,0},{4,7},{5,6},{6,5},{7,4},{8,11},{9,10},{10,... | collective-permute-start | bytes 1419272 | tf_op jit(solution)/shard_map/ppermute | solution.py:40
  144.7 17.3 %collective-permute-start.16 = (bf16[128,4608]{1,0:T(8,128)(2,1)}, bf16[128,4608]{1,0:T(8,128)(2,1)}, u32[]{:S(2)}, u32[]{:S(2)}) collective-permute-start(bf16[128,4608]{1,0:T(8,128)(2,1)} %get-tuple-element.52), channel_id=1, source_target_pairs={{0,16},{1,17},{2,18},{3,19},{4,20},{5,21},{6,22},{7,23},{8,9},{9,8... | collective-permute-start | bytes 3538952 | tf_op jit(solution)/shard_map/ppermute | solution.py:40
  164.3 14.9 %collective-permute-start.19 = (bf16[64,4608]{1,0:T(8,128)(2,1)}, bf16[64,4608]{1,0:T(8,128)(2,1)}, u32[]{:S(2)}, u32[]{:S(2)}) collective-permute-start(bf16[64,4608]{1,0:T(8,128)(2,1)} %get-tuple-element.74), channel_id=1, source_target_pairs={{0,1},{1,0},{2,3},{3,2},{4,5},{5,4},{6,7},{7,6},{8,24},{9,25},{10,... | collective-permute-start | bytes 1769480 | tf_op jit(solution)/shard_map/ppermute | solution.py:40
  166.4 7.4 %collective-permute-start.18 = (bf16[128,640]{1,0:T(8,128)(2,1)}, bf16[128,640]{1,0:T(8,128)(2,1)}, u32[]{:S(2)}, u32[]{:S(2)}) collective-permute-start(bf16[128,640]{1,0:T(8,128)(2,1)} %get-tuple-element.106), channel_id=1, source_target_pairs={{0,16},{1,17},{2,18},{3,19},{4,20},{5,21},{6,22},{7,23},{8,9},{9,8... | collective-permute-start | bytes 491528 | tf_op jit(solution)/shard_map/ppermute | solution.py:40
  180.5 8.2 %collective-permute-start.21 = (bf16[32,5248]{1,0:T(8,128)(2,1)S(1)}, bf16[32,5248]{1,0:T(8,128)(2,1)S(1)}, u32[]{:S(2)}, u32[]{:S(2)}) collective-permute-start(bf16[32,5248]{1,0:T(8,128)(2,1)S(1)} %get-tuple-element.76), channel_id=1, source_target_pairs={{0,2},{1,3},{2,0},{3,1},{4,6},{5,7},{6,4},{7,5},{8,10},{9,11},{10,... | collective-permute-start | bytes 1007624 | tf_op jit(solution)/shard_map/ppermute | solution.py:40
  186.1 13.3 %collective-permute-start.14 = (bf16[1,66,512]{2,1,0:T(8,128)(2,1)S(1)}, bf16[1,66,512]{2,1,0:T(8,128)(2,1)S(1)}, u32[]{:S(2)}, u32[]{:S(2)}) collective-permute-start(bf16[1,66,512]{2,1,0:T(8,128)(2,1)S(1)} %get-tuple-element.92), channel_id=1, source_target_pairs={{0,8},{8,16},{16,24},{1,9},{9,17},{17,25},{2,10},{10,18},{18,26},{... | collective-permute-start | bytes 202760 | tf_op jit(solution)/shard_map/ppermute | solution.py:88
  187.4 12.0 %collective-permute-start.15 = (bf16[1,66,512]{2,1,0:T(8,128)(2,1)S(1)}, bf16[1,66,512]{2,1,0:T(8,128)(2,1)S(1)}, u32[]{:S(2)}, u32[]{:S(2)}) collective-permute-start(bf16[1,66,512]{2,1,0:T(8,128)(2,1)S(1)} %get-tuple-element.93), channel_id=1, source_target_pairs={{8,0},{16,8},{24,16},{9,1},{17,9},{25,17},{10,2},{18,10},{26,18},{... | collective-permute-start | bytes 202760 | tf_op jit(solution)/shard_map/ppermute | solution.py:89
  188.8 8.1 %collective-permute-start.22 = (bf16[16,5248]{1,0:T(8,128)(2,1)S(1)}, bf16[16,5248]{1,0:T(8,128)(2,1)S(1)}, u32[]{:S(2)}, u32[]{:S(2)}) collective-permute-start(bf16[16,5248]{1,0:T(8,128)(2,1)S(1)} %fusion.38), channel_id=1, source_target_pairs={{0,6},{1,7},{2,4},{3,5},{4,2},{5,3},{6,0},{7,1},{8,14},{9,15},{10,... | collective-permute-start | bytes 503816 | tf_op jit(solution)/shard_map/ppermute | solution.py:40
  196.9 9.0 %collective-permute-start.23 = (bf16[16,5248]{1,0:T(8,128)(2,1)S(1)}, bf16[16,5248]{1,0:T(8,128)(2,1)S(1)}, u32[]{:S(2)}, u32[]{:S(2)}) collective-permute-start(bf16[16,5248]{1,0:T(8,128)(2,1)S(1)} %fusion.36), channel_id=1, source_target_pairs={{0,6},{1,7},{2,4},{3,5},{4,2},{5,3},{6,0},{7,1},{8,14},{9,15},{10,... | collective-permute-start | bytes 503816 | tf_op jit(solution)/shard_map/ppermute | solution.py:40
  206.0 9.8 %collective-permute-start.24 = (bf16[32,5248]{1,0:T(8,128)(2,1)S(1)}, bf16[32,5248]{1,0:T(8,128)(2,1)S(1)}, u32[]{:S(2)}, u32[]{:S(2)}) collective-permute-start(bf16[32,5248]{1,0:T(8,128)(2,1)S(1)} %maximum_select_fusion.2), channel_id=1, source_target_pairs={{0,2},{1,3},{2,0},{3,1},{4,6},{5,7},{6,4},{7,5},{8,10},{9,11},{10,... | collective-permute-start | bytes 1007624 | tf_op jit(solution)/shard_map/ppermute | solution.py:40
  215.9 10.8 %collective-permute-start.25 = (bf16[64,5248]{1,0:T(8,128)(2,1)S(1)}, bf16[64,5248]{1,0:T(8,128)(2,1)S(1)}, u32[]{:S(2)}, u32[]{:S(2)}) collective-permute-start(bf16[64,5248]{1,0:T(8,128)(2,1)S(1)} %maximum_select_fusion.1), channel_id=1, source_target_pairs={{0,1},{1,0},{2,3},{3,2},{4,5},{5,4},{6,7},{7,6},{8,24},{9,25},{10,... | collective-permute-start | bytes 2015240 | tf_op jit(solution)/shard_map/ppermute | solution.py:40
  227.0 18.0 %collective-permute-start.26 = (bf16[128,5248]{1,0:T(8,128)(2,1)S(1)}, bf16[128,5248]{1,0:T(8,128)(2,1)S(1)}, u32[]{:S(2)}, u32[]{:S(2)}) collective-permute-start(bf16[128,5248]{1,0:T(8,128)(2,1)S(1)} %maximum_select_fusion.piece.small), channel_id=1, source_target_pairs={{0,16},{1,17},{2,18},{3,19},{4,20},{5,21},{6,22},{7,23},{8,9},{9,8... | collective-permute-start | bytes 4030472 | tf_op jit(solution)/shard_map/ppermute | solution.py:40
  231.2 19.8 %collective-permute-start.28 = (bf16[128,5248]{1,0:T(8,128)(2,1)S(1)}, bf16[128,5248]{1,0:T(8,128)(2,1)S(1)}, u32[]{:S(2)}, u32[]{:S(2)}) collective-permute-start(bf16[128,5248]{1,0:T(8,128)(2,1)S(1)} %maximum_select_fusion.piece.small), channel_id=1, source_target_pairs={{0,8},{1,9},{2,10},{3,11},{4,12},{5,13},{6,14},{7,15},{8,0},{9,1},... | collective-permute-start | bytes 4030472 | tf_op jit(solution)/shard_map/ppermute | solution.py:40
  245.0 9.5 %collective-permute-start.27 = (bf16[128,5248]{1,0:T(8,128)(2,1)S(1)}, bf16[128,5248]{1,0:T(8,128)(2,1)S(1)}, u32[]{:S(2)}, u32[]{:S(2)}) collective-permute-start(bf16[128,5248]{1,0:T(8,128)(2,1)S(1)} %collective-permute-done.26.piece.small), channel_id=1, source_target_pairs={{0,8},{1,9},{2,10},{3,11},{4,12},{5,13},{6,14},{7,15},{8,0},{9,1},... | collective-permute-start | bytes 4030472 | tf_op jit(solution)/shard_map/ppermute | solution.py:40
  (27 other events, 234.8 us)

commit v7 on v6

--- a/solution.py
+++ b/solution.py
@@ -175,16 +175,10 @@
         else:
             spread[...] = refs[count + 3][...]
         for k in range(count):
-
-            def encode(c, _, k=k):
-                span = lanes(c, width // 2)
-                pre = jnp.dot(w[span], xs[k][...], preferred_element_type=jnp.float32)
-                s = jax.nn.sigmoid(pre)
-                slope[k, span] = (s * (1.0 + pre * (1.0 - s))).astype(jnp.bfloat16)
-                enc[span] = (pre * s).astype(jnp.bfloat16)
-                return 0
-
-            lax.fori_loop(0, 2, encode, 0)
+            pre = jnp.dot(w[...], xs[k][...], preferred_element_type=jnp.float32)
+            s = jax.nn.sigmoid(pre)
+            slope[k] = (s * (1.0 + pre * (1.0 - s))).astype(jnp.bfloat16)
+            enc[...] = (pre * s).astype(jnp.bfloat16)
 
             def add(j, _, k=k):
                 code = meta_ref[(first + k) * MOST + j]
@@ -270,12 +264,11 @@
         total = lax.fori_loop(0, patches, unnorm, jnp.zeros((width, 1), jnp.float32))
         out[...] = jnp.zeros_like(out)
         out[:, channels : channels + 1] = total
-
-        def arrival(k, _):
-            pltpu.make_async_copy(xbuf.at[k], xbuf.at[k], sems.at[2 * k]).wait()
-            pltpu.make_async_copy(sbuf.at[k], sbuf.at[k], sems.at[2 * k + 1]).wait()
-
-            def back(j, _):
+        for k in range(count):
+            copies[2 * k].wait()
+            copies[2 * k + 1].wait()
+
+            def back(j, _, k=k):
                 code = meta_ref[k * MOST + j]
                 span = lanes(j, rows)
 
@@ -298,9 +291,6 @@
 
             lax.fori_loop(0, MOST, back, 0)
             out[:, :channels] += nt(dpre[...], xbuf[k])
-            return 0
-
-        lax.fori_loop(0, count, arrival, 0)
 
     held = [pltpu.with_memory_space_constraint(x, pltpu.HBM) for x in (*slopes, spread, d_normed_t)]
     ins = [*arrived, *held, kernels_t, gain_col]
@@ -392,7 +382,7 @@
     source = jnp.sum(chosen * number[:, None, None], axis=0).reshape(-1)
     code = block_patch * kernel_count + block_kernel + 1
     codes = jnp.sum(chosen * code[:, None, None], axis=0) - 1
-    spectra_t = spectra.T
+    spectra_t = pltpu.with_memory_space_constraint(spectra.T, pltpu.HBM)
     far, near = range(lons // 2, lons), range(lons // 2)
     packed = dict(zip(far, pack(spectra_t, source, far, block_rows)))
     packed |= zip(near, pack(spectra_t, source, near, block_rows))

time: 261 us -> 260 us (level)
    ppermute x21, waiting for transfers between devices: 55.4 us -> 61.6 us  [exchange(): return lax.ppermute(value, AXES, pairs)]
    ppermute x4, waiting for transfers between devices: 4.47 us -> 0.01 us  [padded_2(): before = lax.ppermute(last, axis, up)]
    ppermute x4, starting transfers between devices: 10.4 us -> 7.68 us  [padded_2(): after = lax.ppermute(leading, axis, down)]
    unnamed x53 -> x51, local copies, waits for them, and re-layouts: 24.3 us -> 22.4 us
  transfers between devices with their start and end apart: 30 -> 30, of which waited for: 9 -> 9; matrix products, arithmetic and copies ran while one was open for 27% -> 28% of each run, Pallas kernels for 16% -> 16%
where the time goes in v7:
time: 260 us; the launch traced here: 256 us
  waiting for transfers between devices  61.6 us (24%)
  starting transfers between devices  52.3 us (20%)
  Pallas kernels  49.1 us (19%)
  local copies, waits for them, and re-layouts  36.9 us (14%)
  matrix products  34.6 us (13%)
  other arithmetic  20.3 us (8%)
    ppermute x21, waiting for transfers between devices, exchange(): return lax.ppermute(value, AXES, pairs)  61.6 us
    pallas_call x10, Pallas kernels, call(): pl.pallas_call(body, out_shape=outs, grid_spec=pltpu.PrefetchScalarGridSp...  49.1 us
    ppermute x21, starting transfers between devices, exchange(): return lax.ppermute(value, AXES, pairs)  32.9 us
    unnamed x51, local copies, waits for them, and re-layouts  22.4 us
    dot_general x1, matrix products, nt(): lax.dot_general(left, right, (((1,), (1,)), ((), ())), preferred_element_...  12.3 us
    dot_general x9, matrix products, shards(): jnp.dot(window, conv_weight[a, b], preferred_element_type=jnp.float32)  10.1 us
    concatenate x5, other arithmetic, padded_2(): shard = jnp.concatenate([before, shard, after], axis=dim)  7.74 us
    ppermute x4, starting transfers between devices, padded_2(): after = lax.ppermute(leading, axis, down)  7.68 us
  transfers between devices with their start and end apart: 30, of which 9 were waited for; matrix products, arithmetic and copies ran while one was open for 28% of the time, Pallas kernels for 16%

profile of v7, /device:TPU:0, one launch (start us, length us, event | category | flops | bytes accessed | tf_op | source)
XLA Modules:
  0.0 256.2 jit_solution(14378842843011687175)
XLA Ops:
  4.1 7.3 %all-to-all-start = ((s32[8,1,3]{2,1,0:T(1,128)}), s32[8,1,3]{2,1,0:T(1,128)S(1)}, u32[]{:S(2)}, u32[]{:S(2)}) async-start(s32[8,1,3]{2,1,0:T(1,128)} %copy.81), calls=%async_computation | async-start | bytes 8192 | tf_op jit(solution)/shard_map/all_to_all | solution.py:394
  12.5 4.8 %collective-permute-start.1 = (bf16[24,1,512]{2,1,0:T(2,128)(2,1)S(1)}, bf16[24,1,512]{2,1,0:T(2,128)(2,1)S(1)}, u32[]{:S(2)}, u32[]{:S(2)}) collective-permute-start(bf16[24,1,512]{2,1,0:T(2,128)(2,1)S(1)} %get-tuple-element.105), channel_id=1, source_target_pairs={{1,0},{2,1},{3,2},{4,3},{5,4},{6,5},{7,6},{0,7},{9,8},{10,9},{11,1... | collective-permute-start | bytes 73736 | tf_op jit(solution)/shard_map/ppermute | solution.py:89
  19.7 4.8 %collective-permute-start.4 = (bf16[616,384]{1,0:T(8,128)(2,1)S(1)}, bf16[616,384]{1,0:T(8,128)(2,1)}, u32[]{:S(2)}, u32[]{:S(2)}) collective-permute-start(bf16[616,384]{1,0:T(8,128)(2,1)S(1)} %get-tuple-element.38), channel_id=1, source_target_pairs={{0,7},{1,6},{2,5},{3,4},{4,3},{5,2},{6,1},{7,0},{8,15},{9,14},{10,... | collective-permute-start | bytes 1419272 | tf_op jit(solution)/shard_map/ppermute | solution.py:40
  24.7 3.0 %shard_map.121 = (bf16[616,384]{1,0:T(8,128)(2,1)S(1)}, bf16[616,384]{1,0:T(8,128)(2,1)S(1)}, bf16[616,384]{1,0:T(8,128)(2,1)S(1)}, bf16[616,384]{1,0:T(8,128)(2,1)}) custom-call(s32[24]{0:T(128)S(1)} %reshape.375.src, bf16[616,3072]{1,0:T(8,128)(2,1)} %bitcast.166), custom_call_target="tpu_custom_call" | custom-call | tf_op jit(solution)/shard_map/pallas_call | solution.py:106
  29.9 6.6 %copy.93 = bf16[3,3,512,512]{2,3,1,0:T(8,128)(2,1)} copy(bf16[3,3,512,512]{3,2,1,0:T(8,128)(2,1)} %param.16) | data formatting | bytes 9437184 | tf_op args[7]
  44.3 4.2 %collective-permute-start.8 = (bf16[616,384]{1,0:T(8,128)(2,1)S(1)}, bf16[616,384]{1,0:T(8,128)(2,1)S(1)}, u32[]{:S(2)}, u32[]{:S(2)}) collective-permute-start(bf16[616,384]{1,0:T(8,128)(2,1)S(1)} %copy-done.3), channel_id=1, source_target_pairs={{0,1},{1,0},{2,3},{3,2},{4,5},{5,4},{6,7},{7,6},{8,9},{9,8},{10,11... | collective-permute-start | bytes 1419272 | tf_op jit(solution)/shard_map/ppermute | solution.py:40
  54.9 5.1 %copy-done.13 = bf16[1536,4608]{1,0:T(8,128)(2,1)} copy-done((bf16[1536,4608]{1,0:T(8,128)(2,1)}, bf16[1536,4608]{1,0:T(8,128)(2,1)S(1)}, u32[]{:S(2)}) %copy-start.13) | copy-done | bytes 14155800
  68.0 7.2 %collective-permute-start.10 = (bf16[616,384]{1,0:T(8,128)(2,1)}, bf16[616,384]{1,0:T(8,128)(2,1)S(1)}, u32[]{:S(2)}, u32[]{:S(2)}) collective-permute-start(bf16[616,384]{1,0:T(8,128)(2,1)} %get-tuple-element.45), channel_id=1, source_target_pairs={{0,3},{1,2},{2,1},{3,0},{4,7},{5,6},{6,5},{7,4},{8,11},{9,10},{10,... | collective-permute-start | bytes 1419272 | tf_op jit(solution)/shard_map/ppermute | solution.py:40
  75.2 12.3 %convolution_bitcast_fusion.refs_12_ = f32[512,1536]{1,0:T(8,128)} fusion(bf16[1536,4608]{1,0:T(8,128)(2,1)} %constant_dynamic-update-slice_fusion, bf16[512,4608]{0,1:T(8,128)(2,1)S(1)} %bitcast.196), kind=kOutput, calls=%fused_computation.11 | convolution fusion | flops 7247757312 | bytes 22020096 | tf_op jit(solution)/shard_map/dot_general | solution.py:126
  87.5 16.1 %collective-permute-done.10.refs_3_ = bf16[616,384]{1,0:T(8,128)(2,1)S(1)} collective-permute-done((bf16[616,384]{1,0:T(8,128)(2,1)}, bf16[616,384]{1,0:T(8,128)(2,1)S(1)}, u32[]{:S(2)}, u32[]{:S(2)}) %collective-permute-start.10) | collective-permute-done | bytes 473120 | tf_op jit(solution)/shard_map/ppermute | solution.py:40
  104.4 8.3 %shard_map.122 = (f32[12,512,128]{2,1,0:T(8,128)S(1)}, bf16[4,512,384]{2,1,0:T(8,128)(2,1)}) custom-call(s32[24]{0:T(128)S(1)} %reshape.354.meta_ref, bf16[616,384]{1,0:T(8,128)(2,1)} %copy-done.1, bf16[616,384]{1,0:T(8,128)(2,1)} %copy-done.8, bf16[616,384]{1,0:T(8,128)(2,1)} %copy-done.9, bf16[616,384]{1,0:T(8,128)(2,1)} %copy-done.10, ...), custom_call_target="tpu_custom_call" | custom-call | tf_op jit(solution)/shard_map/pallas_call | solution.py:106
  113.5 6.8 %shard_map.123 = (f32[12,512,128]{2,1,0:T(8,128)S(1)}, bf16[3,512,384]{2,1,0:T(8,128)(2,1)}) custom-call(s32[24]{0:T(128)S(1)} %reshape.354.meta_ref, bf16[616,384]{1,0:T(8,128)(2,1)} %collective-permute-done.5.refs_0_.refs_4_, bf16[616,384]{1,0:T(8,128)(2,1)} %collective-permute-done.6.refs_1_.refs_5_, bf16[616,384]{1,0:T(8,128)(2,1)} %copy-done.11, ...), custom_call_target="tpu_custom_call" | custom-call | tf_op jit(solution)/shard_map/pallas_call | solution.py:106
  120.3 6.4 %shard_map.124 = (f32[12,512,128]{2,1,0:T(8,128)}, bf16[1,512,384]{2,1,0:T(8,128)(2,1)}, bf16[512,1536]{1,0:T(8,128)(2,1)S(1)}) custom-call(s32[24]{0:T(128)S(1)} %reshape.354.meta_ref, bf16[616,384]{1,0:T(8,128)(2,1)} %collective-permute-done.4.refs_0_.refs_7_, bf16[512,616]{1,0:T(8,128)(2,1)S(1)} %bitcast.150, bf16[16,128,128]{2,1,0:T(8,128)(2,1)S(1)} %copy-done, ...), custom_call_target="tpu_custom_call" | custom-call | tf_op jit(solution)/shard_map/pallas_call | solution.py:106
  126.7 5.1 %convolution_convert_fusion = bf16[256,4608]{1,0:T(8,128)(2,1)} fusion(bf16[1536,4608]{1,0:T(8,128)(2,1)S(1)} %copy-done.14, bf16[2,256,1536]{2,1,0:T(8,128)(2,1)S(1)} %bitcast.153, s32[]{:T(128)S(6)} %select_n.111), kind=kOutput, calls=%fused_computation.2 | convolution fusion | flops 3625058304 | bytes 17301508 | tf_op jit(solution)/shard_map/dot_general | solution.py:435
  131.9 7.0 %fusion = f32[2,128,4608]{2,1,0:T(8,128)S(1)} fusion(bf16[2,128,1536]{2,1,0:T(8,128)(2,1)S(1)} %bitcast.204, bf16[1536,4608]{1,0:T(8,128)(2,1)} %constant_dynamic-update-slice_fusion), kind=kOutput, calls=%fused_computation | convolution fusion | flops 3623878656 | bytes 19660800 | tf_op jit(solution)/shard_map/dot_general | solution.py:438
  139.0 3.9 %convert_add_fusion = (f32[1,128,4608]{2,1,0:T(8,128)}, bf16[128,4608]{1,0:T(8,128)(2,1)}) fusion(f32[2,128,4608]{2,1,0:T(8,128)S(1)} %fusion, s32[]{:T(128)S(6)} %select_n.117, bf16[2,128,4608]{2,1,0:T(8,128)(2,1)} %bitcast.40, s32[]{:T(128)S(6)} %select_n.110), kind=kLoop, calls=%fused_computation.13 | loop fusion | flops 2949120 | bytes 10616840 | tf_op jit(solution)/shard_map/add | solution.py:77
  142.9 3.7 %collective-permute-start.16 = (bf16[128,4608]{1,0:T(8,128)(2,1)}, bf16[128,4608]{1,0:T(8,128)(2,1)}, u32[]{:S(2)}, u32[]{:S(2)}) collective-permute-start(bf16[128,4608]{1,0:T(8,128)(2,1)} %get-tuple-element.52), channel_id=1, source_target_pairs={{0,16},{1,17},{2,18},{3,19},{4,20},{5,21},{6,22},{7,23},{8,9},{9,8... | collective-permute-start | bytes 3538952 | tf_op jit(solution)/shard_map/ppermute | solution.py:40
  147.0 15.2 %shard_map.125 = f32[512,640]{1,0:T(8,128)S(1)} custom-call(s32[24]{0:T(128)S(1)} %reshape.354.meta_ref, bf16[616,384]{1,0:T(8,128)(2,1)} %copy-done.1, bf16[616,384]{1,0:T(8,128)(2,1)} %copy-done.8, bf16[616,384]{1,0:T(8,128)(2,1)} %copy-done.9, bf16[616,384]{1,0:T(8,128)(2,1)} %copy-done.10, bf16[616,384]{1,0:T(8,128)(2,1)} %collective-permute-done.5.refs_0_.refs_4_, ...), custom_call_target="tpu_custom_call" | custom-call | tf_op jit(solution)/shard_map/pallas_call | solution.py:106
  191.2 6.4 %collective-permute-done.22 = bf16[16,5248]{1,0:T(8,128)(2,1)S(1)} collective-permute-done((bf16[16,5248]{1,0:T(8,128)(2,1)S(1)}, bf16[16,5248]{1,0:T(8,128)(2,1)S(1)}, u32[]{:S(2)}, u32[]{:S(2)}) %collective-permute-start.22) | collective-permute-done | bytes 167968 | tf_op jit(solution)/shard_map/ppermute | solution.py:40
  200.0 5.2 %collective-permute-done.23 = bf16[16,5248]{1,0:T(8,128)(2,1)S(1)} collective-permute-done((bf16[16,5248]{1,0:T(8,128)(2,1)S(1)}, bf16[16,5248]{1,0:T(8,128)(2,1)S(1)}, u32[]{:S(2)}, u32[]{:S(2)}) %collective-permute-start.23) | collective-permute-done | bytes 167968 | tf_op jit(solution)/shard_map/ppermute | solution.py:40
  205.2 3.2 %collective-permute-start.24 = (bf16[32,5248]{1,0:T(8,128)(2,1)S(1)}, bf16[32,5248]{1,0:T(8,128)(2,1)S(1)}, u32[]{:S(2)}, u32[]{:S(2)}) collective-permute-start(bf16[32,5248]{1,0:T(8,128)(2,1)S(1)} %maximum_select_fusion.2), channel_id=1, source_target_pairs={{0,2},{1,3},{2,0},{3,1},{4,6},{5,7},{6,4},{7,5},{8,10},{9,11},{10,... | collective-permute-start | bytes 1007624 | tf_op jit(solution)/shard_map/ppermute | solution.py:40
  209.5 6.1 %collective-permute-done.24 = bf16[32,5248]{1,0:T(8,128)(2,1)S(1)} collective-permute-done((bf16[32,5248]{1,0:T(8,128)(2,1)S(1)}, bf16[32,5248]{1,0:T(8,128)(2,1)S(1)}, u32[]{:S(2)}, u32[]{:S(2)}) %collective-permute-start.24) | collective-permute-done | bytes 335904 | tf_op jit(solution)/shard_map/ppermute | solution.py:40
  217.7 8.8 %collective-permute-done.25 = bf16[64,5248]{1,0:T(8,128)(2,1)S(1)} collective-permute-done((bf16[64,5248]{1,0:T(8,128)(2,1)S(1)}, bf16[64,5248]{1,0:T(8,128)(2,1)S(1)}, u32[]{:S(2)}, u32[]{:S(2)}) %collective-permute-start.25) | collective-permute-done | bytes 671776 | tf_op jit(solution)/shard_map/ppermute | solution.py:40
  231.0 13.8 %collective-permute-done.26.piece.small = bf16[128,5248]{1,0:T(8,128)(2,1)S(1)} collective-permute-done((bf16[128,5248]{1,0:T(8,128)(2,1)S(1)}, bf16[128,5248]{1,0:T(8,128)(2,1)S(1)}, u32[]{:S(2)}, u32[]{:S(2)}) %collective-permute-start.26) | collective-permute-done | bytes 1343520 | tf_op jit(solution)/shard_map/ppermute | solution.py:40
  (167 shorter events, 83.6 us)
Async XLA Ops:
  4.1 34.0 %all-to-all-start = ((s32[8,1,3]{2,1,0:T(1,128)}), s32[8,1,3]{2,1,0:T(1,128)S(1)}, u32[]{:S(2)}, u32[]{:S(2)}) async-start(s32[8,1,3]{2,1,0:T(1,128)} %copy.81), calls=%async_computation | async-start | bytes 8192 | tf_op jit(solution)/shard_map/all_to_all | solution.py:394
  12.5 26.0 %collective-permute-start.1 = (bf16[24,1,512]{2,1,0:T(2,128)(2,1)S(1)}, bf16[24,1,512]{2,1,0:T(2,128)(2,1)S(1)}, u32[]{:S(2)}, u32[]{:S(2)}) collective-permute-start(bf16[24,1,512]{2,1,0:T(2,128)(2,1)S(1)} %get-tuple-element.105), channel_id=1, source_target_pairs={{1,0},{2,1},{3,2},{4,3},{5,4},{6,5},{7,6},{0,7},{9,8},{10,9},{11,1... | collective-permute-start | bytes 73736 | tf_op jit(solution)/shard_map/ppermute | solution.py:89
  17.3 21.2 %collective-permute-start = (bf16[24,1,512]{2,1,0:T(2,128)(2,1)S(1)}, bf16[24,1,512]{2,1,0:T(2,128)(2,1)S(1)}, u32[]{:S(2)}, u32[]{:S(2)}) collective-permute-start(bf16[24,1,512]{2,1,0:T(2,128)(2,1)S(1)} %get-tuple-element.104), channel_id=1, source_target_pairs={{0,1},{1,2},{2,3},{3,4},{4,5},{5,6},{6,7},{7,0},{8,9},{9,10},{10,1... | collective-permute-start | bytes 73736 | tf_op jit(solution)/shard_map/ppermute | solution.py:88
  19.7 100.6 %collective-permute-start.4 = (bf16[616,384]{1,0:T(8,128)(2,1)S(1)}, bf16[616,384]{1,0:T(8,128)(2,1)}, u32[]{:S(2)}, u32[]{:S(2)}) collective-permute-start(bf16[616,384]{1,0:T(8,128)(2,1)S(1)} %get-tuple-element.38), channel_id=1, source_target_pairs={{0,7},{1,6},{2,5},{3,4},{4,3},{5,2},{6,1},{7,0},{8,15},{9,14},{10,... | collective-permute-start | bytes 1419272 | tf_op jit(solution)/shard_map/ppermute | solution.py:40
  24.5 88.2 %collective-permute-start.5 = (bf16[616,384]{1,0:T(8,128)(2,1)S(1)}, bf16[616,384]{1,0:T(8,128)(2,1)}, u32[]{:S(2)}, u32[]{:S(2)}) collective-permute-start(bf16[616,384]{1,0:T(8,128)(2,1)S(1)} %get-tuple-element.39), channel_id=1, source_target_pairs={{0,4},{1,5},{2,6},{3,7},{4,0},{5,1},{6,2},{7,3},{8,12},{9,13},{10,... | collective-permute-start | bytes 1419272 | tf_op jit(solution)/shard_map/ppermute | solution.py:40
  24.5 88.2 %collective-permute-start.6 = (bf16[616,384]{1,0:T(8,128)(2,1)S(1)}, bf16[616,384]{1,0:T(8,128)(2,1)}, u32[]{:S(2)}, u32[]{:S(2)}) collective-permute-start(bf16[616,384]{1,0:T(8,128)(2,1)S(1)} %get-tuple-element.40), channel_id=1, source_target_pairs={{0,5},{1,4},{2,7},{3,6},{4,1},{5,0},{6,3},{7,2},{8,13},{9,12},{10,... | collective-permute-start | bytes 1419272 | tf_op jit(solution)/shard_map/ppermute | solution.py:40
  40.8 7.7 %collective-permute-start.2 = (bf16[1,66,512]{2,1,0:T(8,128)(2,1)S(1)}, bf16[1,66,512]{2,1,0:T(8,128)(2,1)S(1)}, u32[]{:S(2)}, u32[]{:S(2)}) collective-permute-start(bf16[1,66,512]{2,1,0:T(8,128)(2,1)S(1)} %get-tuple-element.97), channel_id=1, source_target_pairs={{8,0},{16,8},{24,16},{9,1},{17,9},{25,17},{10,2},{18,10},{26,18},{... | collective-permute-start | bytes 202760 | tf_op jit(solution)/shard_map/ppermute | solution.py:89
  44.3 22.2 %collective-permute-start.8 = (bf16[616,384]{1,0:T(8,128)(2,1)S(1)}, bf16[616,384]{1,0:T(8,128)(2,1)S(1)}, u32[]{:S(2)}, u32[]{:S(2)}) collective-permute-start(bf16[616,384]{1,0:T(8,128)(2,1)S(1)} %copy-done.3), channel_id=1, source_target_pairs={{0,1},{1,0},{2,3},{3,2},{4,5},{5,4},{6,7},{7,6},{8,9},{9,8},{10,11... | collective-permute-start | bytes 1419272 | tf_op jit(solution)/shard_map/ppermute | solution.py:40
  48.5 19.5 %collective-permute-start.9 = (bf16[616,384]{1,0:T(8,128)(2,1)S(1)}, bf16[616,384]{1,0:T(8,128)(2,1)S(1)}, u32[]{:S(2)}, u32[]{:S(2)}) collective-permute-start(bf16[616,384]{1,0:T(8,128)(2,1)S(1)} %get-tuple-element.44), channel_id=1, source_target_pairs={{0,2},{1,3},{2,0},{3,1},{4,6},{5,7},{6,4},{7,5},{8,10},{9,11},{10,... | collective-permute-start | bytes 1419272 | tf_op jit(solution)/shard_map/ppermute | solution.py:40
  66.5 46.2 %collective-permute-start.7 = (bf16[616,384]{1,0:T(8,128)(2,1)S(1)}, bf16[616,384]{1,0:T(8,128)(2,1)S(1)}, u32[]{:S(2)}, u32[]{:S(2)}) collective-permute-start(bf16[616,384]{1,0:T(8,128)(2,1)S(1)} %get-tuple-element.41), channel_id=1, source_target_pairs={{0,6},{1,7},{2,4},{3,5},{4,2},{5,3},{6,0},{7,1},{8,14},{9,15},{10,... | collective-permute-start | bytes 1419272 | tf_op jit(solution)/shard_map/ppermute | solution.py:40
  68.0 35.6 %collective-permute-start.10 = (bf16[616,384]{1,0:T(8,128)(2,1)}, bf16[616,384]{1,0:T(8,128)(2,1)S(1)}, u32[]{:S(2)}, u32[]{:S(2)}) collective-permute-start(bf16[616,384]{1,0:T(8,128)(2,1)} %get-tuple-element.45), channel_id=1, source_target_pairs={{0,3},{1,2},{2,1},{3,0},{4,7},{5,6},{6,5},{7,4},{8,11},{9,10},{10,... | collective-permute-start | bytes 1419272 | tf_op jit(solution)/shard_map/ppermute | solution.py:40
  142.9 19.4 %collective-permute-start.16 = (bf16[128,4608]{1,0:T(8,128)(2,1)}, bf16[128,4608]{1,0:T(8,128)(2,1)}, u32[]{:S(2)}, u32[]{:S(2)}) collective-permute-start(bf16[128,4608]{1,0:T(8,128)(2,1)} %get-tuple-element.52), channel_id=1, source_target_pairs={{0,16},{1,17},{2,18},{3,19},{4,20},{5,21},{6,22},{7,23},{8,9},{9,8... | collective-permute-start | bytes 3538952 | tf_op jit(solution)/shard_map/ppermute | solution.py:40
  164.6 14.5 %collective-permute-start.19 = (bf16[64,4608]{1,0:T(8,128)(2,1)}, bf16[64,4608]{1,0:T(8,128)(2,1)}, u32[]{:S(2)}, u32[]{:S(2)}) collective-permute-start(bf16[64,4608]{1,0:T(8,128)(2,1)} %get-tuple-element.74), channel_id=1, source_target_pairs={{0,1},{1,0},{2,3},{3,2},{4,5},{5,4},{6,7},{7,6},{8,24},{9,25},{10,... | collective-permute-start | bytes 1769480 | tf_op jit(solution)/shard_map/ppermute | solution.py:40
  176.0 8.0 %collective-permute-start.13 = (bf16[24,1,512]{2,1,0:T(2,128)(2,1)S(1)}, bf16[24,1,512]{2,1,0:T(2,128)(2,1)S(1)}, u32[]{:S(2)}, u32[]{:S(2)}) collective-permute-start(bf16[24,1,512]{2,1,0:T(2,128)(2,1)S(1)} %get-tuple-element.101), channel_id=1, source_target_pairs={{1,0},{2,1},{3,2},{4,3},{5,4},{6,5},{7,6},{0,7},{9,8},{10,9},{11,1... | collective-permute-start | bytes 73736 | tf_op jit(solution)/shard_map/ppermute | solution.py:89
  176.3 7.7 %collective-permute-start.12 = (bf16[24,1,512]{2,1,0:T(2,128)(2,1)S(1)}, bf16[24,1,512]{2,1,0:T(2,128)(2,1)S(1)}, u32[]{:S(2)}, u32[]{:S(2)}) collective-permute-start(bf16[24,1,512]{2,1,0:T(2,128)(2,1)S(1)} %get-tuple-element.100), channel_id=1, source_target_pairs={{0,1},{1,2},{2,3},{3,4},{4,5},{5,6},{6,7},{7,0},{8,9},{9,10},{10,1... | collective-permute-start | bytes 73736 | tf_op jit(solution)/shard_map/ppermute | solution.py:88
  180.4 8.6 %collective-permute-start.21 = (bf16[32,5248]{1,0:T(8,128)(2,1)S(1)}, bf16[32,5248]{1,0:T(8,128)(2,1)S(1)}, u32[]{:S(2)}, u32[]{:S(2)}) collective-permute-start(bf16[32,5248]{1,0:T(8,128)(2,1)S(1)} %get-tuple-element.76), channel_id=1, source_target_pairs={{0,2},{1,3},{2,0},{3,1},{4,6},{5,7},{6,4},{7,5},{8,10},{9,11},{10,... | collective-permute-start | bytes 1007624 | tf_op jit(solution)/shard_map/ppermute | solution.py:40
  184.1 13.9 %collective-permute-start.14 = (bf16[1,66,512]{2,1,0:T(8,128)(2,1)S(1)}, bf16[1,66,512]{2,1,0:T(8,128)(2,1)S(1)}, u32[]{:S(2)}, u32[]{:S(2)}) collective-permute-start(bf16[1,66,512]{2,1,0:T(8,128)(2,1)S(1)} %get-tuple-element.92), channel_id=1, source_target_pairs={{0,8},{8,16},{16,24},{1,9},{9,17},{17,25},{2,10},{10,18},{18,26},{... | collective-permute-start | bytes 202760 | tf_op jit(solution)/shard_map/ppermute | solution.py:88
  185.4 12.6 %collective-permute-start.15 = (bf16[1,66,512]{2,1,0:T(8,128)(2,1)S(1)}, bf16[1,66,512]{2,1,0:T(8,128)(2,1)S(1)}, u32[]{:S(2)}, u32[]{:S(2)}) collective-permute-start(bf16[1,66,512]{2,1,0:T(8,128)(2,1)S(1)} %get-tuple-element.93), channel_id=1, source_target_pairs={{8,0},{16,8},{24,16},{9,1},{17,9},{25,17},{10,2},{18,10},{26,18},{... | collective-permute-start | bytes 202760 | tf_op jit(solution)/shard_map/ppermute | solution.py:89
  189.1 8.5 %collective-permute-start.22 = (bf16[16,5248]{1,0:T(8,128)(2,1)S(1)}, bf16[16,5248]{1,0:T(8,128)(2,1)S(1)}, u32[]{:S(2)}, u32[]{:S(2)}) collective-permute-start(bf16[16,5248]{1,0:T(8,128)(2,1)S(1)} %fusion.38), channel_id=1, source_target_pairs={{0,6},{1,7},{2,4},{3,5},{4,2},{5,3},{6,0},{7,1},{8,14},{9,15},{10,... | collective-permute-start | bytes 503816 | tf_op jit(solution)/shard_map/ppermute | solution.py:40
  205.2 10.3 %collective-permute-start.24 = (bf16[32,5248]{1,0:T(8,128)(2,1)S(1)}, bf16[32,5248]{1,0:T(8,128)(2,1)S(1)}, u32[]{:S(2)}, u32[]{:S(2)}) collective-permute-start(bf16[32,5248]{1,0:T(8,128)(2,1)S(1)} %maximum_select_fusion.2), channel_id=1, source_target_pairs={{0,2},{1,3},{2,0},{3,1},{4,6},{5,7},{6,4},{7,5},{8,10},{9,11},{10,... | collective-permute-start | bytes 1007624 | tf_op jit(solution)/shard_map/ppermute | solution.py:40
  215.6 10.8 %collective-permute-start.25 = (bf16[64,5248]{1,0:T(8,128)(2,1)S(1)}, bf16[64,5248]{1,0:T(8,128)(2,1)S(1)}, u32[]{:S(2)}, u32[]{:S(2)}) collective-permute-start(bf16[64,5248]{1,0:T(8,128)(2,1)S(1)} %maximum_select_fusion.1), channel_id=1, source_target_pairs={{0,1},{1,0},{2,3},{3,2},{4,5},{5,4},{6,7},{7,6},{8,24},{9,25},{10,... | collective-permute-start | bytes 2015240 | tf_op jit(solution)/shard_map/ppermute | solution.py:40
  226.7 18.0 %collective-permute-start.26 = (bf16[128,5248]{1,0:T(8,128)(2,1)S(1)}, bf16[128,5248]{1,0:T(8,128)(2,1)S(1)}, u32[]{:S(2)}, u32[]{:S(2)}) collective-permute-start(bf16[128,5248]{1,0:T(8,128)(2,1)S(1)} %maximum_select_fusion.piece.small), channel_id=1, source_target_pairs={{0,16},{1,17},{2,18},{3,19},{4,20},{5,21},{6,22},{7,23},{8,9},{9,8... | collective-permute-start | bytes 4030472 | tf_op jit(solution)/shard_map/ppermute | solution.py:40
  230.9 19.8 %collective-permute-start.28 = (bf16[128,5248]{1,0:T(8,128)(2,1)S(1)}, bf16[128,5248]{1,0:T(8,128)(2,1)S(1)}, u32[]{:S(2)}, u32[]{:S(2)}) collective-permute-start(bf16[128,5248]{1,0:T(8,128)(2,1)S(1)} %maximum_select_fusion.piece.small), channel_id=1, source_target_pairs={{0,8},{1,9},{2,10},{3,11},{4,12},{5,13},{6,14},{7,15},{8,0},{9,1},... | collective-permute-start | bytes 4030472 | tf_op jit(solution)/shard_map/ppermute | solution.py:40
  244.7 9.5 %collective-permute-start.27 = (bf16[128,5248]{1,0:T(8,128)(2,1)S(1)}, bf16[128,5248]{1,0:T(8,128)(2,1)S(1)}, u32[]{:S(2)}, u32[]{:S(2)}) collective-permute-start(bf16[128,5248]{1,0:T(8,128)(2,1)S(1)} %collective-permute-done.26.piece.small), channel_id=1, source_target_pairs={{0,8},{1,9},{2,10},{3,11},{4,12},{5,13},{6,14},{7,15},{8,0},{9,1},... | collective-permute-start | bytes 4030472 | tf_op jit(solution)/shard_map/ppermute | solution.py:40
  (26 other events, 232.4 us)
